TPU v7x, 128 devices: a whole 4x4x4 slice. The times are simulated.
128 devices in a mesh: box: 8 (over y, core), samp: 16 (over x, z).
Axes of the slice: x: 4, y: 4, z: 4, core: 2. Of those that a mesh axis runs over, the one named last changes fastest.
Arguments:
- children: bfloat16 [2048, 2, 64, 128], P('box', None, 'samp'), may hold values from -6 to 6
- interp_theta: bfloat16 [64, 128], replicated, may hold values from -0.75 to 0.75
- interp_phi: bfloat16 [128, 256], replicated, may hold values from -0.5 to 0.5
- translator: bfloat16 [316, 2, 128, 256], P(None, None, 'samp'), may hold values from -0.1796875 to 0.1796875
- send_index: int32 [8, 8, 16], P('box'), may hold values from 0 to 31, as said below
- list_slots: int32 [256, 64], P('box'), may hold values from 0 to 127, as said below
- list_kinds: int32 [256, 64], P('box'), may hold values from 0 to 315
Outputs:
- parent_pattern: bfloat16 [256, 2, 128, 256], P('box', None, 'samp')
- local_field: float32 [256, 2, 128, 256], P('box', None, 'samp')
Inputs may be any that keep to these rules, and one draw needn't show every extreme that they name: The 16 entries of send_index[s, d] are distinct, and 31 is among them. `list_slots`: each sender sends a receiver a number of live slots between 4 and 16, the first ones; codes name only live slots, senders are spread over all devices of box, and some receiver has a sender with all 16 slots live.
All inputs are finite; a program needn't handle non-finite values.
Results may differ from a plain program's by a relative error of at most 0.0049.
Values may be sent and summed in bfloat16 or wider, within the bound.
No kernel may reach another device: no remote copies, remote signals or barrier semaphores. Data moves between devices by JAX's collectives and lax.ppermute only.
A program may use at most 192 MiB of HBM per device.

v0:
```python
import functools
import math

import jax
import jax.numpy as jnp
from jax import lax
from jax.experimental import pallas as pl
from jax.experimental.pallas import tpu as pltpu
from jax.sharding import Mesh, PartitionSpec as P


KAPPA_H = 12.0
SAMP = ("x", "z")
BOX = ("y", "c")
WIDTH = 128
ROWS = (0, 2, 4, 6, 7)
CUTS = (0, 14, 28, 46, 54, 64)
CHUNK = 16
VMEM = pl.BlockSpec(memory_space=pltpu.VMEM)
SMEM = pl.BlockSpec(memory_space=pltpu.SMEM)
HBM = pl.BlockSpec(memory_space=pltpu.HBM)


def phase_tables(polar_total, azimuth_total):
    polar = (jnp.arange(polar_total, dtype=jnp.int32).astype(jnp.float32) + 0.5) * (
        math.pi / polar_total
    )
    azimuth = jnp.arange(azimuth_total, dtype=jnp.int32).astype(jnp.float32) * (
        2.0 * math.pi / azimuth_total
    )
    octant = jnp.arange(4, dtype=jnp.int32)
    sign_x = ((octant & 1) * 2 - 1).astype(jnp.float32)[:, None, None]
    sign_y = ((octant >> 1 & 1) * 2 - 1).astype(jnp.float32)[:, None, None]
    along_x = jnp.sin(polar)[:, None] * jnp.cos(azimuth)[None, :]
    along_y = jnp.sin(polar)[:, None] * jnp.sin(azimuth)[None, :]
    along_z = jnp.cos(polar)[:, None] + jnp.zeros((1, azimuth_total), jnp.float32)
    phase = KAPPA_H * (sign_x * along_x + sign_y * along_y - along_z)
    return jnp.cos(phase), jnp.sin(phase)


def aggregate_kernel(x_ref, theta_ref, phi_ref, cos_ref, sin_ref, out_ref, mid_ref):
    theta = jnp.transpose(theta_ref[...].astype(jnp.float32)).astype(jnp.bfloat16)
    phi = phi_ref[...]
    chunks = theta.shape[0] // CHUNK
    for p in range(out_ref.shape[1]):
        for o in range(8):
            for r in range(2):
                x = x_ref[:, p * 8 + o, r].reshape(theta.shape[1], phi.shape[0])
                mid = jnp.dot(theta, x, preferred_element_type=jnp.float32).astype(jnp.bfloat16)
                for h in range(chunks):
                    at = (h * 16 + o * 2 + r) * CHUNK
                    mid_ref[at : at + CHUNK, :] = mid[h * CHUNK : (h + 1) * CHUNK]
        for h in range(chunks):
            mid = mid_ref[h * 16 * CHUNK : (h + 1) * 16 * CHUNK, :]
            raised = jnp.dot(mid, phi, preferred_element_type=jnp.float32)
            for s in range(CHUNK // 8):
                row = h * CHUNK + s * 8
                real = imag = None
                for o in range(4):
                    c = cos_ref[o, row : row + 8, :]
                    d = sin_ref[o, row : row + 8, :]
                    ar, ai, br, bi = (
                        raised[k * CHUNK + s * 8 : k * CHUNK + s * 8 + 8]
                        for k in (2 * o, 2 * o + 1, 14 - 2 * o, 15 - 2 * o)
                    )
                    tr = c * (ar + br) - d * (ai - bi)
                    ti = d * (ar - br) + c * (ai + bi)
                    real = tr if real is None else real + tr
                    imag = ti if imag is None else imag + ti
                out_ref[row // 8, p, 0] = real.astype(jnp.bfloat16)
                out_ref[row // 8, p, 1] = imag.astype(jnp.bfloat16)


def stage_kernel(x_ref, out_ref, sem):
    copy = pltpu.make_async_copy(x_ref, out_ref, sem)
    copy.start()
    copy.wait()


def widen_kernel(x_ref, out_ref):
    def widen(k, carry):
        out_ref[k] = x_ref[k].astype(jnp.float32)
        return carry

    lax.fori_loop(0, x_ref.shape[0], widen, 0, unroll=4)


def class_kernel(k, list_ref, trans_ref, *refs):
    first, last = k == 0, k == len(CUTS) - 2
    if first:
        *blocks, out_ref, pool_ref, parents_ref, sem = refs
        store = pltpu.make_async_copy(blocks[0], parents_ref, sem)
        store.start()
    elif last:
        sum_ref, *blocks, _, final_ref, pool_ref, out_ref, sems = refs
    else:
        sum_ref, *blocks, _, out_ref, pool_ref = refs
    boxes = out_ref.shape[0]
    for i, block in enumerate(blocks):

        def widen(n, carry, block=block, start=(ROWS[k] + i) * boxes):
            pool_ref[start + n] = block[n].astype(jnp.float32)
            return carry

        lax.fori_loop(0, boxes, widen, 0, unroll=4)
    if first:
        pool_ref[pool_ref.shape[0] - 1] = jnp.zeros(pool_ref.shape[1:], jnp.float32)

    def add(b, j, acc):
        value = list_ref[b, j]
        at, kind = lax.shift_right_logical(value, 9), value & 511
        sr, si = pool_ref[at, 0], pool_ref[at, 1]
        tr, ti = trans_ref[kind, 0], trans_ref[kind, 1]
        return acc[0] + (tr * sr - ti * si), acc[1] + (tr * si + ti * sr)

    def box(b, carry):
        if first:
            zero = jnp.zeros(out_ref.shape[2:], jnp.float32)
            acc = (zero, zero)
        else:
            acc = (sum_ref[b, 0], sum_ref[b, 1])
            begin = list_ref[boxes + b, k - 1]
            end = CUTS[k] if last else jnp.minimum(list_ref[boxes + b, k], CUTS[k])
            acc = lax.fori_loop(begin, end, lambda j, acc: add(b, j, acc), acc)
        for j in range(CUTS[k], CUTS[k + 1]):
            acc = add(b, CUTS[-1] + j, acc)
        out_ref[b, 0], out_ref[b, 1] = acc
        return carry

    if not last:
        lax.fori_loop(0, boxes, box, 0)
    else:
        parts = sems.shape[0]
        size = boxes // parts
        copies = []
        for i in range(parts):
            lax.fori_loop(i * size, (i + 1) * size, box, 0)
            rows = pl.ds(i * size, size)
            out = pltpu.make_async_copy(out_ref.at[rows], final_ref.at[rows], sems.at[i])
            out.start()
            copies.append(out)
        for out in copies:
            out.wait()
    if first:
        store.wait()


def shift(x, axis, step):
    size = lax.axis_size(axis)
    return lax.ppermute(x, axis, [(i, (i + step) % size) for i in range(size)])


def plan_kernel(me_ref, own_ref, after_ref, before_ref, far_ref, slots_ref, kinds_ref, *rest):
    out_ref, list_ref, sem = rest
    cores, receivers, cap = own_ref.shape
    boxes, entries = slots_ref.shape
    me = me_ref[:, :entries]
    slots = slots_ref[...]
    sender = lax.shift_right_logical(slots, 4)
    dy = (lax.shift_right_logical(sender, 1) - lax.shift_right_logical(me, 1)) & 3
    dc = (sender & 1) ^ (me & 1)
    code = (dy * cores + dc) * cap + (slots & (cap - 1))
    is_me = lax.broadcasted_iota(jnp.int32, (receivers, cap), 0) == me[:receivers, :cap]
    pieces = []
    for table, block, step in (
        (own_ref, 0, 1),
        (after_ref, 2, 2),
        (far_ref, 6, 1),
        (before_ref, 3, 2),
    ):
        for core in range(cores):
            mine = jnp.sum(jnp.where(is_me, table[core], 0), axis=0, keepdims=True)
            pieces.append(mine + (block + step * core) * boxes)
    table = jnp.broadcast_to(jnp.concatenate(pieces, axis=1), (boxes, WIDTH))
    row = jnp.take_along_axis(table, jnp.concatenate([code, code], axis=1), axis=1)
    row = row[:, :entries]
    far = dy == 2
    klass = jnp.where(dy == 0, 0, jnp.where(far, 3, 1) + dc)
    first = lax.broadcasted_iota(jnp.int32, (entries, entries), 0)
    second = lax.broadcasted_iota(jnp.int32, (entries, entries), 1)
    ahead = (first < second).astype(jnp.float32)
    lane = lax.broadcasted_iota(jnp.int32, (boxes, WIDTH), 1)
    slot = lane - entries
    spot = jnp.zeros_like(slots)
    begin = jnp.zeros((boxes, 1), jnp.int32)
    keep = slot < 0
    ends = jnp.zeros((boxes, WIDTH), jnp.int32)
    for k in range(len(CUTS) - 1):
        mine = klass == k
        inside = jnp.dot(mine.astype(jnp.float32), ahead, preferred_element_type=jnp.float32)
        spot = jnp.where(mine, begin + inside.astype(jnp.int32), spot)
        begin = begin + jnp.sum(mine.astype(jnp.int32), axis=1, keepdims=True)
        keep = keep | ((slot >= CUTS[k]) & (slot < CUTS[k + 1]) & (slot < begin))
        ends = jnp.where(lane == k, begin, ends)
    value = jnp.transpose((row * 512 + kinds_ref[...]).astype(jnp.float32)).astype(jnp.int32)
    spot = jnp.transpose(spot.astype(jnp.float32)).astype(jnp.int32)
    target = lax.broadcasted_iota(jnp.int32, (entries, WIDTH), 1) & (entries - 1)
    for b in range(boxes):
        got = jnp.where(spot[:, b : b + 1] == target, value[:, b : b + 1], 0)
        list_ref[b : b + 1, :] = jnp.sum(got, axis=0, keepdims=True)
    list_ref[:boxes, :] = jnp.where(keep, list_ref[:boxes, :], 8 * boxes * 512)
    list_ref[boxes:, :] = ends
    copy = pltpu.make_async_copy(list_ref, out_ref, sem)
    copy.start()
    copy.wait()


def slot_tables(send_index):
    own = jnp.concatenate([send_index, shift(send_index, "c", 1)], axis=0)
    return own, shift(own, "y", -1), shift(own, "y", 1)


def plan_lists(tables, list_slots, list_kinds):
    boxes = list_slots.shape[0]
    me = lax.axis_index("y") * lax.axis_size("c") + lax.axis_index("c")
    me = jnp.broadcast_to(me.astype(jnp.int32), (boxes, WIDTH))
    return pl.pallas_call(
        plan_kernel,
        out_shape=pltpu.SMEM((2 * boxes, WIDTH), jnp.int32),
        in_specs=[VMEM] * 7,
        out_specs=SMEM,
        scratch_shapes=[pltpu.VMEM((2 * boxes, WIDTH), jnp.int32), pltpu.SemaphoreType.DMA],
        compiler_params=pltpu.CompilerParams(vmem_limit_bytes=4 << 20),
        cost_estimate=pl.CostEstimate(flops=1 << 20, bytes_accessed=1 << 20, transcendentals=0),
        name="plan",
    )(me, *tables, list_slots, list_kinds)


def local(children, interp_theta, interp_phi, translator, send_index, list_slots, list_kinds):
    samp_count = lax.axis_size(SAMP)
    polar_total = interp_theta.shape[1]
    azimuth_total = interp_phi.shape[1]
    child_boxes, _, rows, child_azimuth = children.shape
    own_children = child_boxes // samp_count
    parent_boxes = child_boxes // 8
    out_rows = polar_total // samp_count
    pattern = (2, out_rows, azimuth_total)

    x = children.reshape(samp_count, own_children, 2, rows, child_azimuth)
    x = lax.all_to_all(x, SAMP, split_axis=0, concat_axis=0, tiled=True)

    cosine, sine = phase_tables(polar_total, azimuth_total)
    nothing = lax.optimization_barrier(jnp.zeros((), jnp.bfloat16))
    theta, phi = interp_theta + nothing, interp_phi + nothing
    near_tables = slot_tables(send_index)
    x, theta, phi, *near_tables = lax.optimization_barrier((x, theta, phi, *near_tables))
    mine = pl.pallas_call(
        aggregate_kernel,
        out_shape=jax.ShapeDtypeStruct((samp_count, own_children // 8) + pattern, jnp.bfloat16),
        in_specs=[VMEM] * 5,
        out_specs=VMEM,
        scratch_shapes=[
            pltpu.VMEM((16 * polar_total, child_azimuth), jnp.bfloat16),
        ],
        compiler_params=pltpu.CompilerParams(vmem_limit_bytes=12 << 20),
        cost_estimate=pl.CostEstimate(flops=335 << 20, bytes_accessed=4 << 20, transcendentals=0),
        name="aggregate",
    )(x, theta, phi, cosine, sine)
    source, mine = lax.optimization_barrier((translator, mine))
    mine = lax.all_to_all(mine, SAMP, split_axis=0, concat_axis=0, tiled=True)
    staged = pl.pallas_call(
        stage_kernel,
        out_shape=pltpu.VMEM(translator.shape, translator.dtype),
        in_specs=[HBM],
        out_specs=VMEM,
        scratch_shapes=[pltpu.SemaphoreType.DMA],
        compiler_params=pltpu.CompilerParams(vmem_limit_bytes=56 << 20),
        cost_estimate=pl.CostEstimate(flops=1, bytes_accessed=5 << 20, transcendentals=0),
        name="stage",
    )(source)
    far_table = shift(near_tables[0], "y", 2)
    mine, far_table, staged = lax.optimization_barrier((mine, far_table, staged))
    own = mine.reshape((parent_boxes,) + pattern)
    after = shift(own, "y", -1)
    before = shift(own, "y", 1)
    other = shift(own, "c", 1)
    staged, own = lax.optimization_barrier((staged, own))
    params = pltpu.CompilerParams(vmem_limit_bytes=4 << 20)
    cost = pl.CostEstimate(flops=16 << 20, bytes_accessed=8 << 20, transcendentals=0)
    wide = pl.pallas_call(
        widen_kernel,
        out_shape=pltpu.VMEM(translator.shape, jnp.float32),
        in_specs=[VMEM],
        out_specs=VMEM,
        compiler_params=params,
        cost_estimate=cost,
        name="widen",
    )(staged)
    own, wide, far_table = lax.optimization_barrier((own, wide, far_table))
    lists = plan_lists((*near_tables, far_table), list_slots, list_kinds)
    own, lists = lax.optimization_barrier((own, lists))
    far = shift(own, "y", 2)

    shape = (parent_boxes,) + pattern

    def translate(k, blocks, so_far):
        first, last = k == 0, k == len(CUTS) - 2
        field = (jax.ShapeDtypeStruct if last else pltpu.VMEM)(shape, jnp.float32)
        out = [field, pltpu.VMEM((8 * parent_boxes + 1,) + pattern, jnp.float32)]
        out_specs, scratch, aliases = [HBM if last else VMEM, VMEM], [], {}
        if first:
            out.append(jax.ShapeDtypeStruct(shape, jnp.bfloat16))
            out_specs.append(HBM)
            scratch = [pltpu.SemaphoreType.DMA]
            operands = blocks
        else:
            operands = [so_far[0], *blocks, so_far[1]]
            aliases = {1 + len(operands): 1}
        if last:
            scratch = [pltpu.VMEM(shape, jnp.float32), pltpu.SemaphoreType.DMA((4,))]
        return pl.pallas_call(
            functools.partial(class_kernel, k),
            out_shape=out,
            in_specs=[SMEM] + [VMEM] * (1 + len(operands)),
            out_specs=out_specs,
            scratch_shapes=scratch,
            input_output_aliases=aliases,
            compiler_params=params,
            cost_estimate=cost,
        )(lists, wide, *operands)

    *state, parents = translate(0, [own, other], None)
    after, before, *state = lax.optimization_barrier((after, before, *state))
    across = [shift(after, "c", 1), shift(before, "c", 1)]
    state = translate(1, [after, before], state)
    state = translate(2, across, state)
    far, *state = lax.optimization_barrier((far, *state))
    across = shift(far, "c", 1)
    state = translate(3, [far], state)
    field, _ = translate(4, [across], state)
    return parents, field


def solution(mesh):
    y_count, x_count = 4, 4
    fine = Mesh(
        mesh.devices.reshape(y_count, mesh.shape["box"] // y_count, x_count, -1),
        BOX + SAMP,
    )
    return jax.shard_map(
        local,
        mesh=fine,
        in_specs=(
            P(BOX, None, SAMP, None),
            P(),
            P(),
            P(None, None, SAMP, None),
            P(BOX, None, None),
            P(BOX, None),
            P(BOX, None),
        ),
        out_specs=(P(BOX, None, SAMP, None), P(BOX, None, SAMP, None)),
        check_vma=False,
    )
```

profile of v0, /device:TPU:1, one launch (start us, length us, event | category | flops | bytes accessed | tf_op | source)
XLA Modules:
  0.0 60.7 jit_solution(660572706436151572)
XLA Ops:
  0.6 8.4 %all-to-all-start = ((bf16[16,16,2,4,128]{4,3,2,1,0:T(4,128)(2,1)}), bf16[16,16,2,4,128]{4,3,2,1,0:T(4,128)(2,1)S(1)}, u32[]{:S(2)}, u32[]{:S(2)}) async-start(bf16[16,16,2,4,128]{4,3,2,1,0:T(4,128)(2,1)} %bitcast.7), calls=%async_computation | async-start | bytes 1048576 | tf_op jit(solution)/shard_map/all_to_all | solution.py:240
  9.1 1.0 %collective-permute-start = (s32[1,8,16]{2,1,0:T(8,128)}, s32[1,8,16]{2,1,0:T(8,128)S(1)}, u32[]{:S(2)}, u32[]{:S(2)}) collective-permute-start(s32[1,8,16]{2,1,0:T(8,128)} %param.11), channel_id=1, source_target_pairs={{0,16},{16,0},{1,17},{17,1},{2,18},{18,2},{3,19},{19,3},{4,20},{20... | collective-permute-start | bytes 1544 | tf_op jit(solution)/shard_map/ppermute | solution.py:150
  10.2 0.1 broadcast_multiply_fusion.1
  10.3 2.0 %fusion = (f32[4,128,256]{2,1,0:T(8,128)S(1)}, f32[4,128,256]{2,1,0:T(8,128)S(1)}) fusion(f32[128]{0:T(128)S(1)} %fusion.4, f32[128,256]{1,0:T(8,128)S(1)} %get-tuple-element.75, f32[4]{0:T(128)S(1)} %get-tuple-element.78, f32[128,256]{1,0:T(8,128)S(1)} %get-tuple-element.74, f32[4]{0:T(128)S(1)} %get-tuple-element.79), kind=kLoop, calls=%fused_computation.1 | loop fusion | flops 655360 | bytes 1311264 | tf_op jit(solution)/shard_map/sin | solution.py:38
  12.3 0.8 %broadcast_add_fusion.phi_ref = bf16[128,256]{1,0:T(8,128)(2,1)S(1)} fusion(bf16[128,256]{1,0:T(8,128)(2,1)} %param.9, bf16[]{:T(256)} %constant.11.clone.1), kind=kLoop, calls=%fused_computation.5 | loop fusion | flops 32768 | bytes 131074 | tf_op jit(solution)/shard_map/add | solution.py:244
  13.2 0.7 %constant_dynamic-update-slice_fusion.1 = s32[2,8,16]{2,1,0:T(8,128)S(1)} fusion(s32[1,8,16]{2,1,0:T(8,128)} %param.11), kind=kLoop, calls=%fused_computation.8 | loop fusion | bytes 4608
  13.8 0.0 collective-permute-done
  13.9 1.3 %collective-permute-start.2 = (s32[2,8,16]{2,1,0:T(8,128)S(1)}, s32[2,8,16]{2,1,0:T(8,128)S(1)}, u32[]{:S(2)}, u32[]{:S(2)}) collective-permute-start(s32[2,8,16]{2,1,0:T(8,128)S(1)} %constant_dynamic-update-slice_fusion.own_ref), channel_id=1, source_target_pairs={{0,32},{32,64},{64,96},{96,0},{1,33},{33,65},{65,97},{97,1},{2,34}... | collective-permute-start | bytes 3080 | tf_op jit(solution)/shard_map/ppermute | solution.py:150
  15.1 1.5 %collective-permute-start.1 = (s32[2,8,16]{2,1,0:T(8,128)S(1)}, s32[2,8,16]{2,1,0:T(8,128)S(1)}, u32[]{:S(2)}, u32[]{:S(2)}) collective-permute-start(s32[2,8,16]{2,1,0:T(8,128)S(1)} %constant_dynamic-update-slice_fusion.own_ref), channel_id=1, source_target_pairs={{0,96},{32,0},{64,32},{96,64},{1,97},{33,1},{65,33},{97,65},{2,98}... | collective-permute-start | bytes 3080 | tf_op jit(solution)/shard_map/ppermute | solution.py:150
  16.7 0.7 %broadcast_add_fusion.1.theta_ref = bf16[64,128]{1,0:T(8,128)(2,1)S(1)} fusion(bf16[64,128]{1,0:T(8,128)(2,1)} %param.8, bf16[]{:T(256)} %constant.11.clone.1), kind=kLoop, calls=%fused_computation.6 | loop fusion | flops 8192 | bytes 32770 | tf_op jit(solution)/shard_map/add | solution.py:244
  17.4 0.5 collective-permute-done.2.before_ref
  17.9 0.0 collective-permute-done.1.after_ref
  17.9 1.5 %all-to-all-done.x_ref = bf16[16,16,2,4,128]{4,3,2,1,0:T(4,128)(2,1)S(1)} async-done(((bf16[16,16,2,4,128]{4,3,2,1,0:T(4,128)(2,1)}), bf16[16,16,2,4,128]{4,3,2,1,0:T(4,128)(2,1)S(1)}, u32[]{:S(2)}, u32[]{:S(2)}) %all-to-all-start) | async-done | bytes 524320 | tf_op jit(solution)/shard_map/all_to_all | solution.py:240
  19.4 2.0 %aggregate.1 = bf16[16,2,2,8,256]{4,3,2,1,0:T(8,128)(2,1)} custom-call(bf16[16,16,2,4,128]{4,3,2,1,0:T(4,128)(2,1)S(1)} %all-to-all-done.x_ref, bf16[64,128]{1,0:T(8,128)(2,1)S(1)} %broadcast_add_fusion.1.theta_ref, bf16[128,256]{1,0:T(8,128)(2,1)S(1)} %broadcast_add_fusion.phi_ref, f32[4,128,256]{2,1,0:T(8,128)S(1)} %get-tuple-element.73.cos_ref, ...), custom_call_target="tpu_custom_call" | custom-call | flops 351272960 | bytes 4194304 | tf_op jit(solution)/shard_map/aggregate/pallas_call | solution.py:247
  21.5 5.4 %all-to-all-start.1 = ((bf16[16,2,2,8,256]{4,3,2,1,0:T(8,128)(2,1)}), bf16[16,2,2,8,256]{4,3,2,1,0:T(8,128)(2,1)S(1)}, u32[]{:S(2)}, u32[]{:S(2)}) async-start(bf16[16,2,2,8,256]{4,3,2,1,0:T(8,128)(2,1)} %aggregate.1), calls=%async_computation.1 | async-start | bytes 524288 | tf_op jit(solution)/shard_map/all_to_all | solution.py:260
  26.9 2.5 %collective-permute-start.3 = (s32[2,8,16]{2,1,0:T(8,128)S(1)}, s32[2,8,16]{2,1,0:T(8,128)S(1)}, u32[]{:S(2)}, u32[]{:S(2)}) collective-permute-start(s32[2,8,16]{2,1,0:T(8,128)S(1)} %constant_dynamic-update-slice_fusion.own_ref), channel_id=1, source_target_pairs={{0,64},{32,96},{64,0},{96,32},{1,65},{33,97},{65,1},{97,33},{2,66}... | collective-permute-start | bytes 3080 | tf_op jit(solution)/shard_map/ppermute | solution.py:150
  29.4 1.7 %stage.1.x_ref = bf16[316,2,8,256]{3,2,1,0:T(8,128)(2,1)S(1)} custom-call(bf16[316,2,8,256]{3,2,1,0:T(8,128)(2,1)} %x_ref), custom_call_target="tpu_custom_call" | custom-call | flops 1 | bytes 5242880 | tf_op jit(solution)/shard_map/stage/pallas_call | solution.py:261
  31.1 0.0 copy-start
  31.1 0.0 copy-start.1
  31.1 0.0 collective-permute-done.3.far_ref
  31.1 3.0 %all-to-all-done.1 = bf16[16,2,2,8,256]{4,3,2,1,0:T(8,128)(2,1)S(1)} async-done(((bf16[16,2,2,8,256]{4,3,2,1,0:T(8,128)(2,1)}), bf16[16,2,2,8,256]{4,3,2,1,0:T(8,128)(2,1)S(1)}, u32[]{:S(2)}, u32[]{:S(2)}) %all-to-all-start.1) | async-done | bytes 262176 | tf_op jit(solution)/shard_map/all_to_all | solution.py:260
  34.2 2.6 %collective-permute-start.4 = (bf16[32,2,8,256]{3,2,1,0:T(8,128)(2,1)S(1)}, bf16[32,2,8,256]{3,2,1,0:T(8,128)(2,1)}, u32[]{:S(2)}, u32[]{:S(2)}) collective-permute-start(bf16[32,2,8,256]{3,2,1,0:T(8,128)(2,1)S(1)} %bitcast.2), channel_id=1, source_target_pairs={{0,16},{16,0},{1,17},{17,1},{2,18},{18,2},{3,19},{19,3},{4,20},{20... | collective-permute-start | bytes 786440 | tf_op jit(solution)/shard_map/ppermute | solution.py:150
  36.8 1.3 %collective-permute-start.7 = (bf16[32,2,8,256]{3,2,1,0:T(8,128)(2,1)S(1)}, bf16[32,2,8,256]{3,2,1,0:T(8,128)(2,1)S(1)}, u32[]{:S(2)}, u32[]{:S(2)}) collective-permute-start(bf16[32,2,8,256]{3,2,1,0:T(8,128)(2,1)S(1)} %bitcast.3), channel_id=1, source_target_pairs={{0,32},{32,64},{64,96},{96,0},{1,33},{33,65},{65,97},{97,1},{2,34}... | collective-permute-start | bytes 786440 | tf_op jit(solution)/shard_map/ppermute | solution.py:150
  38.0 1.4 %collective-permute-start.6 = (bf16[32,2,8,256]{3,2,1,0:T(8,128)(2,1)S(1)}, bf16[32,2,8,256]{3,2,1,0:T(8,128)(2,1)S(1)}, u32[]{:S(2)}, u32[]{:S(2)}) collective-permute-start(bf16[32,2,8,256]{3,2,1,0:T(8,128)(2,1)S(1)} %bitcast.4), channel_id=1, source_target_pairs={{0,96},{32,0},{64,32},{96,64},{1,97},{33,1},{65,33},{97,65},{2,98}... | collective-permute-start | bytes 786440 | tf_op jit(solution)/shard_map/ppermute | solution.py:150
  39.5 0.5 widen.1.trans_ref
  40.0 0.0 copy-done
  40.0 0.0 copy-done.1
  40.0 2.0 %plan.1.list_ref = s32[64,128]{1,0:T(8,128)S(4)} custom-call(s32[32,128]{1,0:T(8,128)S(1)} %broadcast_in_dim.2.me_ref, s32[2,8,16]{2,1,0:T(8,128)S(1)} %constant_dynamic-update-slice_fusion.own_ref, s32[2,8,16]{2,1,0:T(8,128)S(1)} %collective-permute-done.1.after_ref, s32[2,8,16]{2,1,0:T(8,128)S(1)} %collective-permute-done.2.before_ref, ...), custom_call_target="tpu_custom_call" | custom-call | flops 1048576 | bytes 1048576 | tf_op jit(solution)/shard_map/plan/pallas_call | solution.py:217
  42.1 0.0 collective-permute-done.4.refs_1_
  42.1 2.4 %shard_map.86 = (f32[32,2,8,256]{3,2,1,0:T(8,128)S(1)}, f32[257,2,8,256]{3,2,1,0:T(8,128)S(1)}, bf16[32,2,8,256]{3,2,1,0:T(8,128)(2,1)}) custom-call(s32[64,128]{1,0:T(8,128)S(4)} %plan.1.list_ref, f32[316,2,8,256]{3,2,1,0:T(8,128)S(1)} %widen.1.trans_ref, bf16[32,2,8,256]{3,2,1,0:T(8,128)(2,1)S(1)} %bitcast.5, ...), custom_call_target="tpu_custom_call" | custom-call | flops 16777216 | bytes 8388608 | tf_op jit(solution)/shard_map/pallas_call | solution.py:311
  44.5 1.3 %collective-permute-done.7.refs_2_ = bf16[32,2,8,256]{3,2,1,0:T(8,128)(2,1)S(1)} collective-permute-done((bf16[32,2,8,256]{3,2,1,0:T(8,128)(2,1)S(1)}, bf16[32,2,8,256]{3,2,1,0:T(8,128)(2,1)S(1)}, u32[]{:S(2)}, u32[]{:S(2)}) %collective-permute-start.7) | collective-permute-done | bytes 262176 | tf_op jit(solution)/shard_map/ppermute | solution.py:150
  45.9 0.0 collective-permute-done.6.refs_1_
  45.9 0.9 %collective-permute-start.8 = (bf16[32,2,8,256]{3,2,1,0:T(8,128)(2,1)S(1)}, bf16[32,2,8,256]{3,2,1,0:T(8,128)(2,1)S(1)}, u32[]{:S(2)}, u32[]{:S(2)}) collective-permute-start(bf16[32,2,8,256]{3,2,1,0:T(8,128)(2,1)S(1)} %collective-permute-done.6.refs_1_), channel_id=1, source_target_pairs={{0,16},{16,0},{1,17},{17,1},{2,18},{18,2},{3,19},{19,3},{4,20},{20... | collective-permute-start | bytes 786440 | tf_op jit(solution)/shard_map/ppermute | solution.py:150
  46.8 0.0 collective-permute-start.9
  46.8 2.5 %collective-permute-start.5 = (bf16[32,2,8,256]{3,2,1,0:T(8,128)(2,1)S(1)}, bf16[32,2,8,256]{3,2,1,0:T(8,128)(2,1)S(1)}, u32[]{:S(2)}, u32[]{:S(2)}) collective-permute-start(bf16[32,2,8,256]{3,2,1,0:T(8,128)(2,1)S(1)} %bitcast.6), channel_id=1, source_target_pairs={{0,64},{32,96},{64,0},{96,32},{1,65},{33,97},{65,1},{97,33},{2,66}... | collective-permute-start | bytes 786440 | tf_op jit(solution)/shard_map/ppermute | solution.py:150
  49.3 2.0 %shard_map.87 = (f32[32,2,8,256]{3,2,1,0:T(8,128)S(1)}, f32[257,2,8,256]{3,2,1,0:T(8,128)S(1)}) custom-call(s32[64,128]{1,0:T(8,128)S(4)} %plan.1.list_ref, f32[316,2,8,256]{3,2,1,0:T(8,128)S(1)} %widen.1.trans_ref, f32[32,2,8,256]{3,2,1,0:T(8,128)S(1)} %get-tuple-element.58.refs_0_, ...), custom_call_target="tpu_custom_call", output_to_operand_aliasing={{1}: (5, {})} | custom-call | flops 16777216 | bytes 8388608 | tf_op jit(solution)/shard_map/pallas_call | solution.py:311
  51.3 0.0 collective-permute-done.8.refs_1_
  51.3 0.0 collective-permute-done.9.refs_2_
  51.4 2.4 %shard_map.88 = (f32[32,2,8,256]{3,2,1,0:T(8,128)S(1)}, f32[257,2,8,256]{3,2,1,0:T(8,128)S(1)}) custom-call(s32[64,128]{1,0:T(8,128)S(4)} %plan.1.list_ref, f32[316,2,8,256]{3,2,1,0:T(8,128)S(1)} %widen.1.trans_ref, f32[32,2,8,256]{3,2,1,0:T(8,128)S(1)} %get-tuple-element.62.refs_0_, ...), custom_call_target="tpu_custom_call", output_to_operand_aliasing={{1}: (5, {})} | custom-call | flops 16777216 | bytes 8388608 | tf_op jit(solution)/shard_map/pallas_call | solution.py:311
  53.8 1.8 %collective-permute-done.5.refs_1_ = bf16[32,2,8,256]{3,2,1,0:T(8,128)(2,1)S(1)} collective-permute-done((bf16[32,2,8,256]{3,2,1,0:T(8,128)(2,1)S(1)}, bf16[32,2,8,256]{3,2,1,0:T(8,128)(2,1)S(1)}, u32[]{:S(2)}, u32[]{:S(2)}) %collective-permute-start.5) | collective-permute-done | bytes 262176 | tf_op jit(solution)/shard_map/ppermute | solution.py:150
  55.6 1.4 %collective-permute-start.10 = (bf16[32,2,8,256]{3,2,1,0:T(8,128)(2,1)S(1)}, bf16[32,2,8,256]{3,2,1,0:T(8,128)(2,1)S(1)}, u32[]{:S(2)}, u32[]{:S(2)}) collective-permute-start(bf16[32,2,8,256]{3,2,1,0:T(8,128)(2,1)S(1)} %collective-permute-done.5.refs_1_), channel_id=1, source_target_pairs={{0,16},{16,0},{1,17},{17,1},{2,18},{18,2},{3,19},{19,3},{4,20},{20... | collective-permute-start | bytes 786440 | tf_op jit(solution)/shard_map/ppermute | solution.py:150
  57.0 1.5 %shard_map.89 = (f32[32,2,8,256]{3,2,1,0:T(8,128)S(1)}, f32[257,2,8,256]{3,2,1,0:T(8,128)S(1)}) custom-call(s32[64,128]{1,0:T(8,128)S(4)} %plan.1.list_ref, f32[316,2,8,256]{3,2,1,0:T(8,128)S(1)} %widen.1.trans_ref, f32[32,2,8,256]{3,2,1,0:T(8,128)S(1)} %get-tuple-element.66.refs_0_, ...), custom_call_target="tpu_custom_call", output_to_operand_aliasing={{1}: (4, {})} | custom-call | flops 16777216 | bytes 8388608 | tf_op jit(solution)/shard_map/pallas_call | solution.py:311
  58.5 0.0 collective-permute-done.10.refs_1_
  58.6 2.1 %shard_map.90 = (f32[32,2,8,256]{3,2,1,0:T(8,128)}, f32[257,2,8,256]{3,2,1,0:T(8,128)S(1)}) custom-call(s32[64,128]{1,0:T(8,128)S(4)} %plan.1.list_ref, f32[316,2,8,256]{3,2,1,0:T(8,128)S(1)} %widen.1.trans_ref, f32[32,2,8,256]{3,2,1,0:T(8,128)S(1)} %get-tuple-element.69.refs_0_, ...), custom_call_target="tpu_custom_call", output_to_operand_aliasing={{1}: (4, {})} | custom-call | flops 16777216 | bytes 8388608 | tf_op jit(solution)/shard_map/pallas_call | solution.py:311
  (6 shorter events, 0.1 us)
Async XLA Ops:
  0.6 18.8 %all-to-all-start = ((bf16[16,16,2,4,128]{4,3,2,1,0:T(4,128)(2,1)}), bf16[16,16,2,4,128]{4,3,2,1,0:T(4,128)(2,1)S(1)}, u32[]{:S(2)}, u32[]{:S(2)}) async-start(bf16[16,16,2,4,128]{4,3,2,1,0:T(4,128)(2,1)} %bitcast.7), calls=%async_computation | async-start | bytes 1048576 | tf_op jit(solution)/shard_map/all_to_all | solution.py:240
  9.1 4.8 %collective-permute-start = (s32[1,8,16]{2,1,0:T(8,128)}, s32[1,8,16]{2,1,0:T(8,128)S(1)}, u32[]{:S(2)}, u32[]{:S(2)}) collective-permute-start(s32[1,8,16]{2,1,0:T(8,128)} %param.11), channel_id=1, source_target_pairs={{0,16},{16,0},{1,17},{17,1},{2,18},{18,2},{3,19},{19,3},{4,20},{20... | collective-permute-start | bytes 1544 | tf_op jit(solution)/shard_map/ppermute | solution.py:150
  13.9 4.1 %collective-permute-start.2 = (s32[2,8,16]{2,1,0:T(8,128)S(1)}, s32[2,8,16]{2,1,0:T(8,128)S(1)}, u32[]{:S(2)}, u32[]{:S(2)}) collective-permute-start(s32[2,8,16]{2,1,0:T(8,128)S(1)} %constant_dynamic-update-slice_fusion.own_ref), channel_id=1, source_target_pairs={{0,32},{32,64},{64,96},{96,0},{1,33},{33,65},{65,97},{97,1},{2,34}... | collective-permute-start | bytes 3080 | tf_op jit(solution)/shard_map/ppermute | solution.py:150
  15.1 2.8 %collective-permute-start.1 = (s32[2,8,16]{2,1,0:T(8,128)S(1)}, s32[2,8,16]{2,1,0:T(8,128)S(1)}, u32[]{:S(2)}, u32[]{:S(2)}) collective-permute-start(s32[2,8,16]{2,1,0:T(8,128)S(1)} %constant_dynamic-update-slice_fusion.own_ref), channel_id=1, source_target_pairs={{0,96},{32,0},{64,32},{96,64},{1,97},{33,1},{65,33},{97,65},{2,98}... | collective-permute-start | bytes 3080 | tf_op jit(solution)/shard_map/ppermute | solution.py:150
  21.5 12.7 %all-to-all-start.1 = ((bf16[16,2,2,8,256]{4,3,2,1,0:T(8,128)(2,1)}), bf16[16,2,2,8,256]{4,3,2,1,0:T(8,128)(2,1)S(1)}, u32[]{:S(2)}, u32[]{:S(2)}) async-start(bf16[16,2,2,8,256]{4,3,2,1,0:T(8,128)(2,1)} %aggregate.1), calls=%async_computation.1 | async-start | bytes 524288 | tf_op jit(solution)/shard_map/all_to_all | solution.py:260
  26.9 4.3 %collective-permute-start.3 = (s32[2,8,16]{2,1,0:T(8,128)S(1)}, s32[2,8,16]{2,1,0:T(8,128)S(1)}, u32[]{:S(2)}, u32[]{:S(2)}) collective-permute-start(s32[2,8,16]{2,1,0:T(8,128)S(1)} %constant_dynamic-update-slice_fusion.own_ref), channel_id=1, source_target_pairs={{0,64},{32,96},{64,0},{96,32},{1,65},{33,97},{65,1},{97,33},{2,66}... | collective-permute-start | bytes 3080 | tf_op jit(solution)/shard_map/ppermute | solution.py:150
  31.1 8.9 %copy-start = (s32[32,64]{1,0:T(8,128)S(1)}, s32[32,64]{1,0:T(8,128)}, u32[]{:S(2)}) copy-start(s32[32,64]{1,0:T(8,128)} %slots_ref.1) | copy-start | bytes 24580
  31.1 8.9 %copy-start.1 = (s32[32,64]{1,0:T(8,128)S(1)}, s32[32,64]{1,0:T(8,128)}, u32[]{:S(2)}) copy-start(s32[32,64]{1,0:T(8,128)} %kinds_ref.1) | copy-start | bytes 24580
  34.2 7.9 %collective-permute-start.4 = (bf16[32,2,8,256]{3,2,1,0:T(8,128)(2,1)S(1)}, bf16[32,2,8,256]{3,2,1,0:T(8,128)(2,1)}, u32[]{:S(2)}, u32[]{:S(2)}) collective-permute-start(bf16[32,2,8,256]{3,2,1,0:T(8,128)(2,1)S(1)} %bitcast.2), channel_id=1, source_target_pairs={{0,16},{16,0},{1,17},{17,1},{2,18},{18,2},{3,19},{19,3},{4,20},{20... | collective-permute-start | bytes 786440 | tf_op jit(solution)/shard_map/ppermute | solution.py:150
  36.8 9.1 %collective-permute-start.7 = (bf16[32,2,8,256]{3,2,1,0:T(8,128)(2,1)S(1)}, bf16[32,2,8,256]{3,2,1,0:T(8,128)(2,1)S(1)}, u32[]{:S(2)}, u32[]{:S(2)}) collective-permute-start(bf16[32,2,8,256]{3,2,1,0:T(8,128)(2,1)S(1)} %bitcast.3), channel_id=1, source_target_pairs={{0,32},{32,64},{64,96},{96,0},{1,33},{33,65},{65,97},{97,1},{2,34}... | collective-permute-start | bytes 786440 | tf_op jit(solution)/shard_map/ppermute | solution.py:150
  38.0 7.8 %collective-permute-start.6 = (bf16[32,2,8,256]{3,2,1,0:T(8,128)(2,1)S(1)}, bf16[32,2,8,256]{3,2,1,0:T(8,128)(2,1)S(1)}, u32[]{:S(2)}, u32[]{:S(2)}) collective-permute-start(bf16[32,2,8,256]{3,2,1,0:T(8,128)(2,1)S(1)} %bitcast.4), channel_id=1, source_target_pairs={{0,96},{32,0},{64,32},{96,64},{1,97},{33,1},{65,33},{97,65},{2,98}... | collective-permute-start | bytes 786440 | tf_op jit(solution)/shard_map/ppermute | solution.py:150
  45.9 5.5 %collective-permute-start.8 = (bf16[32,2,8,256]{3,2,1,0:T(8,128)(2,1)S(1)}, bf16[32,2,8,256]{3,2,1,0:T(8,128)(2,1)S(1)}, u32[]{:S(2)}, u32[]{:S(2)}) collective-permute-start(bf16[32,2,8,256]{3,2,1,0:T(8,128)(2,1)S(1)} %collective-permute-done.6.refs_1_), channel_id=1, source_target_pairs={{0,16},{16,0},{1,17},{17,1},{2,18},{18,2},{3,19},{19,3},{4,20},{20... | collective-permute-start | bytes 786440 | tf_op jit(solution)/shard_map/ppermute | solution.py:150
  46.8 4.6 %collective-permute-start.9 = (bf16[32,2,8,256]{3,2,1,0:T(8,128)(2,1)S(1)}, bf16[32,2,8,256]{3,2,1,0:T(8,128)(2,1)S(1)}, u32[]{:S(2)}, u32[]{:S(2)}) collective-permute-start(bf16[32,2,8,256]{3,2,1,0:T(8,128)(2,1)S(1)} %collective-permute-done.7.refs_2_), channel_id=1, source_target_pairs={{0,16},{16,0},{1,17},{17,1},{2,18},{18,2},{3,19},{19,3},{4,20},{20... | collective-permute-start | bytes 786440 | tf_op jit(solution)/shard_map/ppermute | solution.py:150
  46.8 8.9 %collective-permute-start.5 = (bf16[32,2,8,256]{3,2,1,0:T(8,128)(2,1)S(1)}, bf16[32,2,8,256]{3,2,1,0:T(8,128)(2,1)S(1)}, u32[]{:S(2)}, u32[]{:S(2)}) collective-permute-start(bf16[32,2,8,256]{3,2,1,0:T(8,128)(2,1)S(1)} %bitcast.6), channel_id=1, source_target_pairs={{0,64},{32,96},{64,0},{96,32},{1,65},{33,97},{65,1},{97,33},{2,66}... | collective-permute-start | bytes 786440 | tf_op jit(solution)/shard_map/ppermute | solution.py:150
  55.6 2.9 %collective-permute-start.10 = (bf16[32,2,8,256]{3,2,1,0:T(8,128)(2,1)S(1)}, bf16[32,2,8,256]{3,2,1,0:T(8,128)(2,1)S(1)}, u32[]{:S(2)}, u32[]{:S(2)}) collective-permute-start(bf16[32,2,8,256]{3,2,1,0:T(8,128)(2,1)S(1)} %collective-permute-done.5.refs_1_), channel_id=1, source_target_pairs={{0,16},{16,0},{1,17},{17,1},{2,18},{18,2},{3,19},{19,3},{4,20},{20... | collective-permute-start | bytes 786440 | tf_op jit(solution)/shard_map/ppermute | solution.py:150
where the time goes:
time: 61.2 us; the launch traced here: 60.7 us
  starting transfers between devices  30.2 us (49%)
  Pallas kernels  16.9 us (28%)
  waiting for transfers between devices  8.26 us (13%)
  other arithmetic  3.76 us (6%)
  between operations  0.8 us (1%)
  local copies, waits for them, and re-layouts  0.7 us (1%)
    ppermute x11, starting transfers between devices, shift(): return lax.ppermute(x, axis, [(i, (i + step) % size) for i in range(size)])  16.4 us
    pallas_call x5, Pallas kernels, translate(): pl.pallas_call(functools.partial(class_kernel, k), out_shape=out, in_spec...  10.6 us
    all_to_all x1, starting transfers between devices, local(): x = lax.all_to_all(x, SAMP, split_axis=0, concat_axis=0, tiled=True)  8.43 us
    all_to_all x1, starting transfers between devices, local(): mine = lax.all_to_all(mine, SAMP, split_axis=0, concat_axis=0, tiled=True)  5.38 us
    ppermute x11, waiting for transfers between devices, shift(): return lax.ppermute(x, axis, [(i, (i + step) % size) for i in range(size)])  3.73 us
    all_to_all x1, waiting for transfers between devices, local(): mine = lax.all_to_all(mine, SAMP, split_axis=0, concat_axis=0, tiled=True)  3.05 us
    pallas_call x1, Pallas kernels, plan_lists(): pl.pallas_call(plan_kernel, out_shape=pltpu.SMEM((2 * boxes, WIDTH), jnp....  2.04 us
    pallas_call x1, Pallas kernels, local(): pl.pallas_call(aggregate_kernel, out_shape=jax.ShapeDtypeStruct((samp_cou...  2.03 us
  transfers between devices with their start and end apart: 13, of which 5 were waited for; matrix products, arithmetic and copies ran while one was open for 7% of the time, Pallas kernels for 21%

commit v1 on v0

--- a/solution.py
+++ b/solution.py
@@ -13,8 +13,8 @@
 SAMP = ("x", "z")
 BOX = ("y", "c")
 WIDTH = 128
-ROWS = (0, 2, 4, 6, 7)
-CUTS = (0, 14, 28, 46, 54, 64)
+ROWS = (0, 2, 3, 4, 5, 6, 7)
+CUTS = (0, 14, 22, 30, 38, 46, 54, 64)
 CHUNK = 16
 VMEM = pl.BlockSpec(memory_space=pltpu.VMEM)
 SMEM = pl.BlockSpec(memory_space=pltpu.SMEM)
@@ -113,28 +113,32 @@
         tr, ti = trans_ref[kind, 0], trans_ref[kind, 1]
         return acc[0] + (tr * sr - ti * si), acc[1] + (tr * si + ti * sr)
 
-    def box(b, carry):
+    def start(b):
         if first:
             zero = jnp.zeros(out_ref.shape[2:], jnp.float32)
-            acc = (zero, zero)
-        else:
-            acc = (sum_ref[b, 0], sum_ref[b, 1])
-            begin = list_ref[boxes + b, k - 1]
-            end = CUTS[k] if last else jnp.minimum(list_ref[boxes + b, k], CUTS[k])
-            acc = lax.fori_loop(begin, end, lambda j, acc: add(b, j, acc), acc)
+            return zero, zero
+        begin = list_ref[boxes + b, k - 1]
+        end = CUTS[k] if last else jnp.minimum(list_ref[boxes + b, k], CUTS[k])
+        acc = (sum_ref[b, 0], sum_ref[b, 1])
+        return lax.fori_loop(begin, end, lambda j, acc: add(b, j, acc), acc)
+
+    def pair(i, carry):
+        places = (2 * i, 2 * i + 1)
+        acc = [start(b) for b in places]
         for j in range(CUTS[k], CUTS[k + 1]):
-            acc = add(b, CUTS[-1] + j, acc)
-        out_ref[b, 0], out_ref[b, 1] = acc
+            acc = [add(b, CUTS[-1] + j, a) for b, a in zip(places, acc)]
+        for b, a in zip(places, acc):
+            out_ref[b, 0], out_ref[b, 1] = a
         return carry
 
     if not last:
-        lax.fori_loop(0, boxes, box, 0)
+        lax.fori_loop(0, boxes // 2, pair, 0)
     else:
         parts = sems.shape[0]
         size = boxes // parts
         copies = []
         for i in range(parts):
-            lax.fori_loop(i * size, (i + 1) * size, box, 0)
+            lax.fori_loop(i * size // 2, (i + 1) * size // 2, pair, 0)
             rows = pl.ds(i * size, size)
             out = pltpu.make_async_copy(out_ref.at[rows], final_ref.at[rows], sems.at[i])
             out.start()
@@ -162,20 +166,15 @@
     code = (dy * cores + dc) * cap + (slots & (cap - 1))
     is_me = lax.broadcasted_iota(jnp.int32, (receivers, cap), 0) == me[:receivers, :cap]
     pieces = []
-    for table, block, step in (
-        (own_ref, 0, 1),
-        (after_ref, 2, 2),
-        (far_ref, 6, 1),
-        (before_ref, 3, 2),
-    ):
+    for table, block in ((own_ref, 0), (after_ref, 4), (far_ref, 6), (before_ref, 2)):
         for core in range(cores):
             mine = jnp.sum(jnp.where(is_me, table[core], 0), axis=0, keepdims=True)
-            pieces.append(mine + (block + step * core) * boxes)
+            pieces.append(mine + (block + core) * boxes)
     table = jnp.broadcast_to(jnp.concatenate(pieces, axis=1), (boxes, WIDTH))
     row = jnp.take_along_axis(table, jnp.concatenate([code, code], axis=1), axis=1)
     row = row[:, :entries]
-    far = dy == 2
-    klass = jnp.where(dy == 0, 0, jnp.where(far, 3, 1) + dc)
+    klass = jnp.where(dy == 3, 1, jnp.where(dy == 1, 3, 5)) + dc
+    klass = jnp.where(dy == 0, 0, klass)
     first = lax.broadcasted_iota(jnp.int32, (entries, entries), 0)
     second = lax.broadcasted_iota(jnp.int32, (entries, entries), 1)
     ahead = (first < second).astype(jnp.float32)
@@ -288,7 +287,6 @@
     )(staged)
     own, wide, far_table = lax.optimization_barrier((own, wide, far_table))
     lists = plan_lists((*near_tables, far_table), list_slots, list_kinds)
-    own, lists = lax.optimization_barrier((own, lists))
     far = shift(own, "y", 2)
 
     shape = (parent_boxes,) + pattern
@@ -320,14 +318,12 @@
         )(lists, wide, *operands)
 
     *state, parents = translate(0, [own, other], None)
-    after, before, *state = lax.optimization_barrier((after, before, *state))
-    across = [shift(after, "c", 1), shift(before, "c", 1)]
-    state = translate(1, [after, before], state)
-    state = translate(2, across, state)
-    far, *state = lax.optimization_barrier((far, *state))
-    across = shift(far, "c", 1)
-    state = translate(3, [far], state)
-    field, _ = translate(4, [across], state)
+    for k, block in ((1, before), (3, after), (5, far)):
+        block, *state = lax.optimization_barrier((block, *state))
+        across = shift(block, "c", 1)
+        state = translate(k, [block], state)
+        state = translate(k + 1, [across], state)
+    field, _ = state
     return parents, field
 
 

time: 61.2 us -> 72.3 us (1.18)
  waiting for transfers between devices: 8.26 us -> 24.9 us
  starting transfers between devices: 30.2 us -> 24.9 us
    ppermute x11, waiting for transfers between devices: 3.73 us -> 21.6 us  [shift(): return lax.ppermute(x, axis, [(i, (i + step) % size) for i in range(size)])]
    ppermute x11, starting transfers between devices: 16.4 us -> 10.8 us  [shift(): return lax.ppermute(x, axis, [(i, (i + step) % size) for i in range(size)])]
    all_to_all x1, waiting for transfers between devices: 1.48 us -> 0.01 us  [local(): x = lax.all_to_all(x, SAMP, split_axis=0, concat_axis=0, tiled=True)]
    all_to_all x1, starting transfers between devices: 5.38 us -> 6.37 us  [local(): mine = lax.all_to_all(mine, SAMP, split_axis=0, concat_axis=0, tiled=True)]
    pallas_call x5 -> x7, Pallas kernels: 10.6 us -> 10.5 us  [translate(): pl.pallas_call(functools.partial(class_kernel, k), out_shape=out, in_spec...]
  transfers between devices with their start and end apart: 13 -> 13, of which waited for: 5 -> 7; matrix products, arithmetic and copies ran while one was open for 7% -> 6% of each run, Pallas kernels for 21% -> 18%
where the time goes in v1:
time: 72.3 us; the launch traced here: 71.8 us
  starting transfers between devices  24.9 us (34%)
  waiting for transfers between devices  24.9 us (34%)
  Pallas kernels  16.8 us (23%)
  other arithmetic  3.75 us (5%)
  between operations  0.8 us (1%)
    ppermute x11, waiting for transfers between devices, shift(): return lax.ppermute(x, axis, [(i, (i + step) % size) for i in range(size)])  21.6 us
    ppermute x11, starting transfers between devices, shift(): return lax.ppermute(x, axis, [(i, (i + step) % size) for i in range(size)])  10.8 us
    pallas_call x7, Pallas kernels, translate(): pl.pallas_call(functools.partial(class_kernel, k), out_shape=out, in_spec...  10.5 us
    all_to_all x1, starting transfers between devices, local(): x = lax.all_to_all(x, SAMP, split_axis=0, concat_axis=0, tiled=True)  7.71 us
    all_to_all x1, starting transfers between devices, local(): mine = lax.all_to_all(mine, SAMP, split_axis=0, concat_axis=0, tiled=True)  6.37 us
    all_to_all x1, waiting for transfers between devices, local(): mine = lax.all_to_all(mine, SAMP, split_axis=0, concat_axis=0, tiled=True)  3.28 us
    pallas_call x1, Pallas kernels, plan_lists(): pl.pallas_call(plan_kernel, out_shape=pltpu.SMEM((2 * boxes, WIDTH), jnp....  2.05 us
    pallas_call x1, Pallas kernels, local(): pl.pallas_call(aggregate_kernel, out_shape=jax.ShapeDtypeStruct((samp_cou...  2.03 us
  transfers between devices with their start and end apart: 13, of which 7 were waited for; matrix products, arithmetic and copies ran while one was open for 6% of the time, Pallas kernels for 18%

profile of v1, /device:TPU:1, one launch (start us, length us, event | category | flops | bytes accessed | tf_op | source)
XLA Modules:
  0.0 71.8 jit_solution(11729035376572945674)
XLA Ops:
  0.6 1.5 %collective-permute-start = (s32[1,8,16]{2,1,0:T(8,128)}, s32[1,8,16]{2,1,0:T(8,128)S(1)}, u32[]{:S(2)}, u32[]{:S(2)}) collective-permute-start(s32[1,8,16]{2,1,0:T(8,128)} %param.11), channel_id=1, source_target_pairs={{0,16},{16,0},{1,17},{17,1},{2,18},{18,2},{3,19},{19,3},{4,20},{20... | collective-permute-start | bytes 1544 | tf_op jit(solution)/shard_map/ppermute | solution.py:154
  2.1 7.7 %all-to-all-start = ((bf16[16,16,2,4,128]{4,3,2,1,0:T(4,128)(2,1)}), bf16[16,16,2,4,128]{4,3,2,1,0:T(4,128)(2,1)S(1)}, u32[]{:S(2)}, u32[]{:S(2)}) async-start(bf16[16,16,2,4,128]{4,3,2,1,0:T(4,128)(2,1)} %bitcast.7), calls=%async_computation | async-start | bytes 1048576 | tf_op jit(solution)/shard_map/all_to_all | solution.py:239
  10.0 0.1 broadcast_multiply_fusion.1
  10.0 2.0 %fusion = (f32[4,128,256]{2,1,0:T(8,128)S(1)}, f32[4,128,256]{2,1,0:T(8,128)S(1)}) fusion(f32[128]{0:T(128)S(1)} %fusion.4, f32[128,256]{1,0:T(8,128)S(1)} %get-tuple-element.83, f32[4]{0:T(128)S(1)} %get-tuple-element.86, f32[128,256]{1,0:T(8,128)S(1)} %get-tuple-element.82, f32[4]{0:T(128)S(1)} %get-tuple-element.87), kind=kLoop, calls=%fused_computation.1 | loop fusion | flops 655360 | bytes 1311264 | tf_op jit(solution)/shard_map/sin | solution.py:38
  12.0 0.8 %broadcast_add_fusion.phi_ref = bf16[128,256]{1,0:T(8,128)(2,1)S(1)} fusion(bf16[128,256]{1,0:T(8,128)(2,1)} %param.9, bf16[]{:T(256)} %constant.10.clone.1), kind=kLoop, calls=%fused_computation.5 | loop fusion | flops 32768 | bytes 131074 | tf_op jit(solution)/shard_map/add | solution.py:243
  12.9 0.7 constant_dynamic-update-slice_fusion.1
  13.6 0.0 collective-permute-done
  13.6 2.7 %collective-permute-start.1 = (s32[2,8,16]{2,1,0:T(8,128)S(1)}, s32[2,8,16]{2,1,0:T(8,128)S(1)}, u32[]{:S(2)}, u32[]{:S(2)}) collective-permute-start(s32[2,8,16]{2,1,0:T(8,128)S(1)} %constant_dynamic-update-slice_fusion.own_ref), channel_id=1, source_target_pairs={{0,96},{32,0},{64,32},{96,64},{1,97},{33,1},{65,33},{97,65},{2,98}... | collective-permute-start | bytes 3080 | tf_op jit(solution)/shard_map/ppermute | solution.py:154
  16.3 0.0 collective-permute-start.2
  16.3 0.7 %broadcast_add_fusion.1.theta_ref = bf16[64,128]{1,0:T(8,128)(2,1)S(1)} fusion(bf16[64,128]{1,0:T(8,128)(2,1)} %param.8, bf16[]{:T(256)} %constant.10.clone.1), kind=kLoop, calls=%fused_computation.6 | loop fusion | flops 8192 | bytes 32770 | tf_op jit(solution)/shard_map/add | solution.py:243
  17.0 0.1 collective-permute-done.1.after_ref
  17.1 3.2 %collective-permute-done.2.before_ref = s32[2,8,16]{2,1,0:T(8,128)S(1)} collective-permute-done((s32[2,8,16]{2,1,0:T(8,128)S(1)}, s32[2,8,16]{2,1,0:T(8,128)S(1)}, u32[]{:S(2)}, u32[]{:S(2)}) %collective-permute-start.2) | collective-permute-done | bytes 1056 | tf_op jit(solution)/shard_map/ppermute | solution.py:154
  20.3 0.0 all-to-all-done.x_ref
  20.3 2.0 %aggregate.1 = bf16[16,2,2,8,256]{4,3,2,1,0:T(8,128)(2,1)} custom-call(bf16[16,16,2,4,128]{4,3,2,1,0:T(4,128)(2,1)S(1)} %all-to-all-done.x_ref, bf16[64,128]{1,0:T(8,128)(2,1)S(1)} %broadcast_add_fusion.1.theta_ref, bf16[128,256]{1,0:T(8,128)(2,1)S(1)} %broadcast_add_fusion.phi_ref, f32[4,128,256]{2,1,0:T(8,128)S(1)} %get-tuple-element.81.cos_ref, ...), custom_call_target="tpu_custom_call" | custom-call | flops 351272960 | bytes 4194304 | tf_op jit(solution)/shard_map/aggregate/pallas_call | solution.py:246
  22.3 6.4 %all-to-all-start.1 = ((bf16[16,2,2,8,256]{4,3,2,1,0:T(8,128)(2,1)}), bf16[16,2,2,8,256]{4,3,2,1,0:T(8,128)(2,1)S(1)}, u32[]{:S(2)}, u32[]{:S(2)}) async-start(bf16[16,2,2,8,256]{4,3,2,1,0:T(8,128)(2,1)} %aggregate.1), calls=%async_computation.1 | async-start | bytes 524288 | tf_op jit(solution)/shard_map/all_to_all | solution.py:259
  28.7 0.6 collective-permute-start.3
  29.3 1.7 %stage.1.x_ref = bf16[316,2,8,256]{3,2,1,0:T(8,128)(2,1)S(1)} custom-call(bf16[316,2,8,256]{3,2,1,0:T(8,128)(2,1)} %x_ref), custom_call_target="tpu_custom_call" | custom-call | flops 1 | bytes 5242880 | tf_op jit(solution)/shard_map/stage/pallas_call | solution.py:260
  31.1 0.0 copy-start
  31.1 0.0 copy-start.1
  31.1 1.7 %collective-permute-done.3.far_ref = s32[2,8,16]{2,1,0:T(8,128)S(1)} collective-permute-done((s32[2,8,16]{2,1,0:T(8,128)S(1)}, s32[2,8,16]{2,1,0:T(8,128)S(1)}, u32[]{:S(2)}, u32[]{:S(2)}) %collective-permute-start.3) | collective-permute-done | bytes 1056 | tf_op jit(solution)/shard_map/ppermute | solution.py:154
  32.8 3.3 %all-to-all-done.1 = bf16[16,2,2,8,256]{4,3,2,1,0:T(8,128)(2,1)S(1)} async-done(((bf16[16,2,2,8,256]{4,3,2,1,0:T(8,128)(2,1)}), bf16[16,2,2,8,256]{4,3,2,1,0:T(8,128)(2,1)S(1)}, u32[]{:S(2)}, u32[]{:S(2)}) %all-to-all-start.1) | async-done | bytes 262176 | tf_op jit(solution)/shard_map/all_to_all | solution.py:259
  36.1 3.4 %collective-permute-start.4 = (bf16[32,2,8,256]{3,2,1,0:T(8,128)(2,1)S(1)}, bf16[32,2,8,256]{3,2,1,0:T(8,128)(2,1)S(1)}, u32[]{:S(2)}, u32[]{:S(2)}) collective-permute-start(bf16[32,2,8,256]{3,2,1,0:T(8,128)(2,1)S(1)} %bitcast.2), channel_id=1, source_target_pairs={{0,16},{16,0},{1,17},{17,1},{2,18},{18,2},{3,19},{19,3},{4,20},{20... | collective-permute-start | bytes 786440 | tf_op jit(solution)/shard_map/ppermute | solution.py:154
  39.5 0.0 collective-permute-start.7
  39.5 0.5 widen.1.trans_ref
  40.0 0.0 copy-done
  40.0 0.0 copy-done.1
  40.1 2.1 %plan.1.list_ref = s32[64,128]{1,0:T(8,128)S(4)} custom-call(s32[32,128]{1,0:T(8,128)S(1)} %broadcast_in_dim.2.me_ref, s32[2,8,16]{2,1,0:T(8,128)S(1)} %constant_dynamic-update-slice_fusion.own_ref, s32[2,8,16]{2,1,0:T(8,128)S(1)} %collective-permute-done.1.after_ref, s32[2,8,16]{2,1,0:T(8,128)S(1)} %collective-permute-done.2.before_ref, ...), custom_call_target="tpu_custom_call" | custom-call | flops 1048576 | bytes 1048576 | tf_op jit(solution)/shard_map/plan/pallas_call | solution.py:216
  42.1 0.0 collective-permute-done.4.refs_1_
  42.1 1.4 %shard_map.86 = (f32[32,2,8,256]{3,2,1,0:T(8,128)S(1)}, f32[257,2,8,256]{3,2,1,0:T(8,128)S(1)}, bf16[32,2,8,256]{3,2,1,0:T(8,128)(2,1)}) custom-call(s32[64,128]{1,0:T(8,128)S(4)} %plan.1.list_ref, f32[316,2,8,256]{3,2,1,0:T(8,128)S(1)} %widen.1.trans_ref, bf16[32,2,8,256]{3,2,1,0:T(8,128)(2,1)S(1)} %bitcast.4, ...), custom_call_target="tpu_custom_call" | custom-call | flops 16777216 | bytes 8388608 | tf_op jit(solution)/shard_map/pallas_call | solution.py:309
  43.5 5.0 %collective-permute-done.7.refs_1_ = bf16[32,2,8,256]{3,2,1,0:T(8,128)(2,1)S(1)} collective-permute-done((bf16[32,2,8,256]{3,2,1,0:T(8,128)(2,1)S(1)}, bf16[32,2,8,256]{3,2,1,0:T(8,128)(2,1)S(1)}, u32[]{:S(2)}, u32[]{:S(2)}) %collective-permute-start.7) | collective-permute-done | bytes 262176 | tf_op jit(solution)/shard_map/ppermute | solution.py:154
  48.5 0.9 %collective-permute-start.8 = (bf16[32,2,8,256]{3,2,1,0:T(8,128)(2,1)S(1)}, bf16[32,2,8,256]{3,2,1,0:T(8,128)(2,1)S(1)}, u32[]{:S(2)}, u32[]{:S(2)}) collective-permute-start(bf16[32,2,8,256]{3,2,1,0:T(8,128)(2,1)S(1)} %collective-permute-done.7.refs_1_), channel_id=1, source_target_pairs={{0,16},{16,0},{1,17},{17,1},{2,18},{18,2},{3,19},{19,3},{4,20},{20... | collective-permute-start | bytes 786440 | tf_op jit(solution)/shard_map/ppermute | solution.py:154
  49.4 0.0 collective-permute-start.6
  49.4 1.4 %shard_map.87 = (f32[32,2,8,256]{3,2,1,0:T(8,128)S(1)}, f32[257,2,8,256]{3,2,1,0:T(8,128)S(1)}) custom-call(s32[64,128]{1,0:T(8,128)S(4)} %plan.1.list_ref, f32[316,2,8,256]{3,2,1,0:T(8,128)S(1)} %widen.1.trans_ref, f32[32,2,8,256]{3,2,1,0:T(8,128)S(1)} %get-tuple-element.60.refs_0_, ...), custom_call_target="tpu_custom_call", output_to_operand_aliasing={{1}: (4, {})} | custom-call | flops 16777216 | bytes 8388608 | tf_op jit(solution)/shard_map/pallas_call | solution.py:309
  50.8 0.0 collective-permute-done.8.refs_1_
  50.8 1.3 %shard_map.88 = (f32[32,2,8,256]{3,2,1,0:T(8,128)S(1)}, f32[257,2,8,256]{3,2,1,0:T(8,128)S(1)}) custom-call(s32[64,128]{1,0:T(8,128)S(4)} %plan.1.list_ref, f32[316,2,8,256]{3,2,1,0:T(8,128)S(1)} %widen.1.trans_ref, f32[32,2,8,256]{3,2,1,0:T(8,128)S(1)} %get-tuple-element.63.refs_0_, ...), custom_call_target="tpu_custom_call", output_to_operand_aliasing={{1}: (4, {})} | custom-call | flops 16777216 | bytes 8388608 | tf_op jit(solution)/shard_map/pallas_call | solution.py:309
  52.2 5.1 %collective-permute-done.6.refs_1_ = bf16[32,2,8,256]{3,2,1,0:T(8,128)(2,1)S(1)} collective-permute-done((bf16[32,2,8,256]{3,2,1,0:T(8,128)(2,1)S(1)}, bf16[32,2,8,256]{3,2,1,0:T(8,128)(2,1)S(1)}, u32[]{:S(2)}, u32[]{:S(2)}) %collective-permute-start.6) | collective-permute-done | bytes 262176 | tf_op jit(solution)/shard_map/ppermute | solution.py:154
  57.3 0.9 %collective-permute-start.9 = (bf16[32,2,8,256]{3,2,1,0:T(8,128)(2,1)S(1)}, bf16[32,2,8,256]{3,2,1,0:T(8,128)(2,1)S(1)}, u32[]{:S(2)}, u32[]{:S(2)}) collective-permute-start(bf16[32,2,8,256]{3,2,1,0:T(8,128)(2,1)S(1)} %collective-permute-done.6.refs_1_), channel_id=1, source_target_pairs={{0,16},{16,0},{1,17},{17,1},{2,18},{18,2},{3,19},{19,3},{4,20},{20... | collective-permute-start | bytes 786440 | tf_op jit(solution)/shard_map/ppermute | solution.py:154
  58.1 0.0 collective-permute-start.5
  58.1 1.3 %shard_map.89 = (f32[32,2,8,256]{3,2,1,0:T(8,128)S(1)}, f32[257,2,8,256]{3,2,1,0:T(8,128)S(1)}) custom-call(s32[64,128]{1,0:T(8,128)S(4)} %plan.1.list_ref, f32[316,2,8,256]{3,2,1,0:T(8,128)S(1)} %widen.1.trans_ref, f32[32,2,8,256]{3,2,1,0:T(8,128)S(1)} %get-tuple-element.67.refs_0_, ...), custom_call_target="tpu_custom_call", output_to_operand_aliasing={{1}: (4, {})} | custom-call | flops 16777216 | bytes 8388608 | tf_op jit(solution)/shard_map/pallas_call | solution.py:309
  59.5 0.0 collective-permute-done.9.refs_1_
  59.5 1.5 %shard_map.90 = (f32[32,2,8,256]{3,2,1,0:T(8,128)S(1)}, f32[257,2,8,256]{3,2,1,0:T(8,128)S(1)}) custom-call(s32[64,128]{1,0:T(8,128)S(4)} %plan.1.list_ref, f32[316,2,8,256]{3,2,1,0:T(8,128)S(1)} %widen.1.trans_ref, f32[32,2,8,256]{3,2,1,0:T(8,128)S(1)} %get-tuple-element.70.refs_0_, ...), custom_call_target="tpu_custom_call", output_to_operand_aliasing={{1}: (4, {})} | custom-call | flops 16777216 | bytes 8388608 | tf_op jit(solution)/shard_map/pallas_call | solution.py:309
  61.0 6.5 %collective-permute-done.5.refs_1_ = bf16[32,2,8,256]{3,2,1,0:T(8,128)(2,1)S(1)} collective-permute-done((bf16[32,2,8,256]{3,2,1,0:T(8,128)(2,1)S(1)}, bf16[32,2,8,256]{3,2,1,0:T(8,128)(2,1)S(1)}, u32[]{:S(2)}, u32[]{:S(2)}) %collective-permute-start.5) | collective-permute-done | bytes 262176 | tf_op jit(solution)/shard_map/ppermute | solution.py:154
  67.5 0.9 %collective-permute-start.10 = (bf16[32,2,8,256]{3,2,1,0:T(8,128)(2,1)S(1)}, bf16[32,2,8,256]{3,2,1,0:T(8,128)(2,1)S(1)}, u32[]{:S(2)}, u32[]{:S(2)}) collective-permute-start(bf16[32,2,8,256]{3,2,1,0:T(8,128)(2,1)S(1)} %collective-permute-done.5.refs_1_), channel_id=1, source_target_pairs={{0,16},{16,0},{1,17},{17,1},{2,18},{18,2},{3,19},{19,3},{4,20},{20... | collective-permute-start | bytes 786440 | tf_op jit(solution)/shard_map/ppermute | solution.py:154
  68.4 1.4 %shard_map.91 = (f32[32,2,8,256]{3,2,1,0:T(8,128)S(1)}, f32[257,2,8,256]{3,2,1,0:T(8,128)S(1)}) custom-call(s32[64,128]{1,0:T(8,128)S(4)} %plan.1.list_ref, f32[316,2,8,256]{3,2,1,0:T(8,128)S(1)} %widen.1.trans_ref, f32[32,2,8,256]{3,2,1,0:T(8,128)S(1)} %get-tuple-element.74.refs_0_, ...), custom_call_target="tpu_custom_call", output_to_operand_aliasing={{1}: (4, {})} | custom-call | flops 16777216 | bytes 8388608 | tf_op jit(solution)/shard_map/pallas_call | solution.py:309
  69.8 0.0 collective-permute-done.10.refs_1_
  69.8 2.0 %shard_map.92 = (f32[32,2,8,256]{3,2,1,0:T(8,128)}, f32[257,2,8,256]{3,2,1,0:T(8,128)S(1)}) custom-call(s32[64,128]{1,0:T(8,128)S(4)} %plan.1.list_ref, f32[316,2,8,256]{3,2,1,0:T(8,128)S(1)} %widen.1.trans_ref, f32[32,2,8,256]{3,2,1,0:T(8,128)S(1)} %get-tuple-element.77.refs_0_, ...), custom_call_target="tpu_custom_call", output_to_operand_aliasing={{1}: (4, {})} | custom-call | flops 16777216 | bytes 8388608 | tf_op jit(solution)/shard_map/pallas_call | solution.py:309
  (6 shorter events, 0.1 us)
Async XLA Ops:
  0.6 12.9 %collective-permute-start = (s32[1,8,16]{2,1,0:T(8,128)}, s32[1,8,16]{2,1,0:T(8,128)S(1)}, u32[]{:S(2)}, u32[]{:S(2)}) collective-permute-start(s32[1,8,16]{2,1,0:T(8,128)} %param.11), channel_id=1, source_target_pairs={{0,16},{16,0},{1,17},{17,1},{2,18},{18,2},{3,19},{19,3},{4,20},{20... | collective-permute-start | bytes 1544 | tf_op jit(solution)/shard_map/ppermute | solution.py:154
  2.1 18.2 %all-to-all-start = ((bf16[16,16,2,4,128]{4,3,2,1,0:T(4,128)(2,1)}), bf16[16,16,2,4,128]{4,3,2,1,0:T(4,128)(2,1)S(1)}, u32[]{:S(2)}, u32[]{:S(2)}) async-start(bf16[16,16,2,4,128]{4,3,2,1,0:T(4,128)(2,1)} %bitcast.7), calls=%async_computation | async-start | bytes 1048576 | tf_op jit(solution)/shard_map/all_to_all | solution.py:239
  13.6 3.5 %collective-permute-start.1 = (s32[2,8,16]{2,1,0:T(8,128)S(1)}, s32[2,8,16]{2,1,0:T(8,128)S(1)}, u32[]{:S(2)}, u32[]{:S(2)}) collective-permute-start(s32[2,8,16]{2,1,0:T(8,128)S(1)} %constant_dynamic-update-slice_fusion.own_ref), channel_id=1, source_target_pairs={{0,96},{32,0},{64,32},{96,64},{1,97},{33,1},{65,33},{97,65},{2,98}... | collective-permute-start | bytes 3080 | tf_op jit(solution)/shard_map/ppermute | solution.py:154
  16.3 4.0 %collective-permute-start.2 = (s32[2,8,16]{2,1,0:T(8,128)S(1)}, s32[2,8,16]{2,1,0:T(8,128)S(1)}, u32[]{:S(2)}, u32[]{:S(2)}) collective-permute-start(s32[2,8,16]{2,1,0:T(8,128)S(1)} %constant_dynamic-update-slice_fusion.own_ref), channel_id=1, source_target_pairs={{0,32},{32,64},{64,96},{96,0},{1,33},{33,65},{65,97},{97,1},{2,34}... | collective-permute-start | bytes 3080 | tf_op jit(solution)/shard_map/ppermute | solution.py:154
  22.3 13.7 %all-to-all-start.1 = ((bf16[16,2,2,8,256]{4,3,2,1,0:T(8,128)(2,1)}), bf16[16,2,2,8,256]{4,3,2,1,0:T(8,128)(2,1)S(1)}, u32[]{:S(2)}, u32[]{:S(2)}) async-start(bf16[16,2,2,8,256]{4,3,2,1,0:T(8,128)(2,1)} %aggregate.1), calls=%async_computation.1 | async-start | bytes 524288 | tf_op jit(solution)/shard_map/all_to_all | solution.py:259
  28.7 4.1 %collective-permute-start.3 = (s32[2,8,16]{2,1,0:T(8,128)S(1)}, s32[2,8,16]{2,1,0:T(8,128)S(1)}, u32[]{:S(2)}, u32[]{:S(2)}) collective-permute-start(s32[2,8,16]{2,1,0:T(8,128)S(1)} %constant_dynamic-update-slice_fusion.own_ref), channel_id=1, source_target_pairs={{0,64},{32,96},{64,0},{96,32},{1,65},{33,97},{65,1},{97,33},{2,66}... | collective-permute-start | bytes 3080 | tf_op jit(solution)/shard_map/ppermute | solution.py:154
  31.1 9.0 %copy-start = (s32[32,64]{1,0:T(8,128)S(1)}, s32[32,64]{1,0:T(8,128)}, u32[]{:S(2)}) copy-start(s32[32,64]{1,0:T(8,128)} %slots_ref.1) | copy-start | bytes 24580
  31.1 9.0 %copy-start.1 = (s32[32,64]{1,0:T(8,128)S(1)}, s32[32,64]{1,0:T(8,128)}, u32[]{:S(2)}) copy-start(s32[32,64]{1,0:T(8,128)} %kinds_ref.1) | copy-start | bytes 24580
  36.1 6.0 %collective-permute-start.4 = (bf16[32,2,8,256]{3,2,1,0:T(8,128)(2,1)S(1)}, bf16[32,2,8,256]{3,2,1,0:T(8,128)(2,1)S(1)}, u32[]{:S(2)}, u32[]{:S(2)}) collective-permute-start(bf16[32,2,8,256]{3,2,1,0:T(8,128)(2,1)S(1)} %bitcast.2), channel_id=1, source_target_pairs={{0,16},{16,0},{1,17},{17,1},{2,18},{18,2},{3,19},{19,3},{4,20},{20... | collective-permute-start | bytes 786440 | tf_op jit(solution)/shard_map/ppermute | solution.py:154
  39.5 9.1 %collective-permute-start.7 = (bf16[32,2,8,256]{3,2,1,0:T(8,128)(2,1)S(1)}, bf16[32,2,8,256]{3,2,1,0:T(8,128)(2,1)S(1)}, u32[]{:S(2)}, u32[]{:S(2)}) collective-permute-start(bf16[32,2,8,256]{3,2,1,0:T(8,128)(2,1)S(1)} %bitcast.3), channel_id=1, source_target_pairs={{0,32},{32,64},{64,96},{96,0},{1,33},{33,65},{65,97},{97,1},{2,34}... | collective-permute-start | bytes 786440 | tf_op jit(solution)/shard_map/ppermute | solution.py:154
  48.5 2.3 %collective-permute-start.8 = (bf16[32,2,8,256]{3,2,1,0:T(8,128)(2,1)S(1)}, bf16[32,2,8,256]{3,2,1,0:T(8,128)(2,1)S(1)}, u32[]{:S(2)}, u32[]{:S(2)}) collective-permute-start(bf16[32,2,8,256]{3,2,1,0:T(8,128)(2,1)S(1)} %collective-permute-done.7.refs_1_), channel_id=1, source_target_pairs={{0,16},{16,0},{1,17},{17,1},{2,18},{18,2},{3,19},{19,3},{4,20},{20... | collective-permute-start | bytes 786440 | tf_op jit(solution)/shard_map/ppermute | solution.py:154
  49.4 7.9 %collective-permute-start.6 = (bf16[32,2,8,256]{3,2,1,0:T(8,128)(2,1)S(1)}, bf16[32,2,8,256]{3,2,1,0:T(8,128)(2,1)S(1)}, u32[]{:S(2)}, u32[]{:S(2)}) collective-permute-start(bf16[32,2,8,256]{3,2,1,0:T(8,128)(2,1)S(1)} %bitcast.5), channel_id=1, source_target_pairs={{0,96},{32,0},{64,32},{96,64},{1,97},{33,1},{65,33},{97,65},{2,98}... | collective-permute-start | bytes 786440 | tf_op jit(solution)/shard_map/ppermute | solution.py:154
  57.3 2.2 %collective-permute-start.9 = (bf16[32,2,8,256]{3,2,1,0:T(8,128)(2,1)S(1)}, bf16[32,2,8,256]{3,2,1,0:T(8,128)(2,1)S(1)}, u32[]{:S(2)}, u32[]{:S(2)}) collective-permute-start(bf16[32,2,8,256]{3,2,1,0:T(8,128)(2,1)S(1)} %collective-permute-done.6.refs_1_), channel_id=1, source_target_pairs={{0,16},{16,0},{1,17},{17,1},{2,18},{18,2},{3,19},{19,3},{4,20},{20... | collective-permute-start | bytes 786440 | tf_op jit(solution)/shard_map/ppermute | solution.py:154
  58.1 9.4 %collective-permute-start.5 = (bf16[32,2,8,256]{3,2,1,0:T(8,128)(2,1)S(1)}, bf16[32,2,8,256]{3,2,1,0:T(8,128)(2,1)S(1)}, u32[]{:S(2)}, u32[]{:S(2)}) collective-permute-start(bf16[32,2,8,256]{3,2,1,0:T(8,128)(2,1)S(1)} %bitcast.6), channel_id=1, source_target_pairs={{0,64},{32,96},{64,0},{96,32},{1,65},{33,97},{65,1},{97,33},{2,66}... | collective-permute-start | bytes 786440 | tf_op jit(solution)/shard_map/ppermute | solution.py:154
  67.5 2.3 %collective-permute-start.10 = (bf16[32,2,8,256]{3,2,1,0:T(8,128)(2,1)S(1)}, bf16[32,2,8,256]{3,2,1,0:T(8,128)(2,1)S(1)}, u32[]{:S(2)}, u32[]{:S(2)}) collective-permute-start(bf16[32,2,8,256]{3,2,1,0:T(8,128)(2,1)S(1)} %collective-permute-done.5.refs_1_), channel_id=1, source_target_pairs={{0,16},{16,0},{1,17},{17,1},{2,18},{18,2},{3,19},{19,3},{4,20},{20... | collective-permute-start | bytes 786440 | tf_op jit(solution)/shard_map/ppermute | solution.py:154

commit v2 on v1

--- a/solution.py
+++ b/solution.py
@@ -13,8 +13,8 @@
 SAMP = ("x", "z")
 BOX = ("y", "c")
 WIDTH = 128
-ROWS = (0, 2, 3, 4, 5, 6, 7)
-CUTS = (0, 14, 22, 30, 38, 46, 54, 64)
+ROWS = (0, 2, 4, 6, 7)
+CUTS = (0, 14, 28, 46, 54, 64)
 CHUNK = 16
 VMEM = pl.BlockSpec(memory_space=pltpu.VMEM)
 SMEM = pl.BlockSpec(memory_space=pltpu.SMEM)
@@ -28,18 +28,36 @@
     azimuth = jnp.arange(azimuth_total, dtype=jnp.int32).astype(jnp.float32) * (
         2.0 * math.pi / azimuth_total
     )
+    along_x = KAPPA_H * jnp.sin(polar)[:, None] * jnp.cos(azimuth)[None, :]
+    along_y = KAPPA_H * jnp.sin(polar)[:, None] * jnp.sin(azimuth)[None, :]
+    along_z = (KAPPA_H * jnp.cos(polar))[:, None]
+    parts = (jnp.cos(along_x), jnp.sin(along_x), jnp.cos(along_y), jnp.sin(along_y))
+    cos_x, sin_x, cos_y, sin_y = lax.optimization_barrier(parts)
     octant = jnp.arange(4, dtype=jnp.int32)
     sign_x = ((octant & 1) * 2 - 1).astype(jnp.float32)[:, None, None]
     sign_y = ((octant >> 1 & 1) * 2 - 1).astype(jnp.float32)[:, None, None]
-    along_x = jnp.sin(polar)[:, None] * jnp.cos(azimuth)[None, :]
-    along_y = jnp.sin(polar)[:, None] * jnp.sin(azimuth)[None, :]
-    along_z = jnp.cos(polar)[:, None] + jnp.zeros((1, azimuth_total), jnp.float32)
-    phase = KAPPA_H * (sign_x * along_x + sign_y * along_y - along_z)
-    return jnp.cos(phase), jnp.sin(phase)
+    x, y = (cos_x[None], sign_x * sin_x), (cos_y[None], sign_y * sin_y)
+    return turn(turn(x, y), (jnp.cos(along_z), -jnp.sin(along_z)))
+
+
+def turn(a, b):
+    return a[0] * b[0] - a[1] * b[1], a[1] * b[0] + a[0] * b[1]
+
+
+def prepare_kernel(theta_hbm, phi_hbm, turned_ref, phi_ref, theta_ref, sems):
+    copies = [
+        pltpu.make_async_copy(theta_hbm, theta_ref, sems.at[0]),
+        pltpu.make_async_copy(phi_hbm, phi_ref, sems.at[1]),
+    ]
+    for copy in copies:
+        copy.start()
+    for copy in copies:
+        copy.wait()
+    turned_ref[...] = jnp.transpose(theta_ref[...].astype(jnp.float32)).astype(jnp.bfloat16)
 
 
 def aggregate_kernel(x_ref, theta_ref, phi_ref, cos_ref, sin_ref, out_ref, mid_ref):
-    theta = jnp.transpose(theta_ref[...].astype(jnp.float32)).astype(jnp.bfloat16)
+    theta = theta_ref[...]
     phi = phi_ref[...]
     chunks = theta.shape[0] // CHUNK
     for p in range(out_ref.shape[1]):
@@ -96,10 +114,11 @@
     else:
         sum_ref, *blocks, _, out_ref, pool_ref = refs
     boxes = out_ref.shape[0]
-    for i, block in enumerate(blocks):
-
-        def widen(n, carry, block=block, start=(ROWS[k] + i) * boxes):
-            pool_ref[start + n] = block[n].astype(jnp.float32)
+    groups = [blocks] if k > 2 else [[block] for block in blocks]
+    for i, group in enumerate(groups):
+
+        def widen(n, carry, group=group, start=(ROWS[k] + i) * boxes):
+            pool_ref[start + n] = sum(block[n].astype(jnp.float32) for block in group)
             return carry
 
         lax.fori_loop(0, boxes, widen, 0, unroll=4)
@@ -166,15 +185,15 @@
     code = (dy * cores + dc) * cap + (slots & (cap - 1))
     is_me = lax.broadcasted_iota(jnp.int32, (receivers, cap), 0) == me[:receivers, :cap]
     pieces = []
-    for table, block in ((own_ref, 0), (after_ref, 4), (far_ref, 6), (before_ref, 2)):
+    side = me[:1, :cap] & 1
+    for table, block in ((own_ref, (0, 1)), (after_ref, (2, 4)), (far_ref, None), (before_ref, (3, 5))):
         for core in range(cores):
             mine = jnp.sum(jnp.where(is_me, table[core], 0), axis=0, keepdims=True)
-            pieces.append(mine + (block + core) * boxes)
+            pieces.append(mine + ((6 + (side ^ core)) if block is None else block[core]) * boxes)
     table = jnp.broadcast_to(jnp.concatenate(pieces, axis=1), (boxes, WIDTH))
     row = jnp.take_along_axis(table, jnp.concatenate([code, code], axis=1), axis=1)
     row = row[:, :entries]
-    klass = jnp.where(dy == 3, 1, jnp.where(dy == 1, 3, 5)) + dc
-    klass = jnp.where(dy == 0, 0, klass)
+    klass = jnp.where(dy == 2, 3 + (sender & 1), jnp.where(dy == 0, 0, 1 + dc))
     first = lax.broadcasted_iota(jnp.int32, (entries, entries), 0)
     second = lax.broadcasted_iota(jnp.int32, (entries, entries), 1)
     ahead = (first < second).astype(jnp.float32)
@@ -204,15 +223,19 @@
     copy.wait()
 
 
+def some_pairs(x, pairs, core):
+    cores = lax.axis_size("c")
+    pairs = [(a * cores + core, b * cores + core) for a, b in pairs]
+    return lax.ppermute(x, BOX, pairs)
+
+
 def slot_tables(send_index):
     own = jnp.concatenate([send_index, shift(send_index, "c", 1)], axis=0)
     return own, shift(own, "y", -1), shift(own, "y", 1)
 
 
-def plan_lists(tables, list_slots, list_kinds):
+def plan_lists(me, tables, list_slots, list_kinds):
     boxes = list_slots.shape[0]
-    me = lax.axis_index("y") * lax.axis_size("c") + lax.axis_index("c")
-    me = jnp.broadcast_to(me.astype(jnp.int32), (boxes, WIDTH))
     return pl.pallas_call(
         plan_kernel,
         out_shape=pltpu.SMEM((2 * boxes, WIDTH), jnp.int32),
@@ -239,10 +262,26 @@
     x = lax.all_to_all(x, SAMP, split_axis=0, concat_axis=0, tiled=True)
 
     cosine, sine = phase_tables(polar_total, azimuth_total)
-    nothing = lax.optimization_barrier(jnp.zeros((), jnp.bfloat16))
-    theta, phi = interp_theta + nothing, interp_phi + nothing
+    theta, phi = pl.pallas_call(
+        prepare_kernel,
+        out_shape=[
+            pltpu.VMEM(interp_theta.shape[::-1], jnp.bfloat16),
+            pltpu.VMEM(interp_phi.shape, jnp.bfloat16),
+        ],
+        in_specs=[HBM] * 2,
+        out_specs=[VMEM] * 2,
+        scratch_shapes=[
+            pltpu.VMEM(interp_theta.shape, jnp.bfloat16),
+            pltpu.SemaphoreType.DMA((2,)),
+        ],
+        compiler_params=pltpu.CompilerParams(vmem_limit_bytes=61 << 20),
+        cost_estimate=pl.CostEstimate(flops=1 << 20, bytes_accessed=1 << 18, transcendentals=0),
+        name="prepare",
+    )(interp_theta, interp_phi)
+    me = lax.axis_index("y") * lax.axis_size("c") + lax.axis_index("c")
+    me = jnp.broadcast_to(me.astype(jnp.int32), (parent_boxes, WIDTH))
     near_tables = slot_tables(send_index)
-    x, theta, phi, *near_tables = lax.optimization_barrier((x, theta, phi, *near_tables))
+    x, theta, phi, me, *near_tables = lax.optimization_barrier((x, theta, phi, me, *near_tables))
     mine = pl.pallas_call(
         aggregate_kernel,
         out_shape=jax.ShapeDtypeStruct((samp_count, own_children // 8) + pattern, jnp.bfloat16),
@@ -286,8 +325,8 @@
         name="widen",
     )(staged)
     own, wide, far_table = lax.optimization_barrier((own, wide, far_table))
-    lists = plan_lists((*near_tables, far_table), list_slots, list_kinds)
-    far = shift(own, "y", 2)
+    lists = plan_lists(me, (*near_tables, far_table), list_slots, list_kinds)
+    far = some_pairs(own, [(y, (y + 2) % 4) for y in range(4)], 0)
 
     shape = (parent_boxes,) + pattern
 
@@ -318,12 +357,19 @@
         )(lists, wide, *operands)
 
     *state, parents = translate(0, [own, other], None)
-    for k, block in ((1, before), (3, after), (5, far)):
-        block, *state = lax.optimization_barrier((block, *state))
-        across = shift(block, "c", 1)
-        state = translate(k, [block], state)
-        state = translate(k + 1, [across], state)
-    field, _ = state
+    after, before, *state = lax.optimization_barrier((after, before, *state))
+    up = some_pairs(before, ((1, 2), (2, 3)), 1)
+    down = some_pairs(after, ((1, 0), (2, 1)), 1)
+    across = [shift(after, "c", 1), shift(before, "c", 1)]
+    state = translate(1, [after, before], state)
+    far, *state = lax.optimization_barrier((far, *state))
+    far_across = shift(far, "c", 1)
+    state = translate(2, across, state)
+    state = translate(3, [far, far_across], state)
+    up, down, *state = lax.optimization_barrier((up, down, *state))
+    relayed = [up, down]
+    relayed += [shift(v, "c", 1) for v in relayed]
+    field, _ = translate(4, relayed, state)
     return parents, field
 
 

time: 72.3 us -> 65.6 us (0.907)
  waiting for transfers between devices: 24.9 us -> 18.1 us
  starting transfers between devices: 24.9 us -> 28 us
  other arithmetic: 3.75 us -> 1.49 us
  Pallas kernels: 16.8 us -> 16 us
    ppermute x11 -> x12, waiting for transfers between devices: 21.6 us -> 12 us  [shift(): return lax.ppermute(x, axis, [(i, (i + step) % size) for i in range(size)])]
    ppermute x0 -> x3, starting transfers between devices: none -> 2.63 us  [some_pairs(): return lax.ppermute(x, BOX, pairs)]
    ppermute x0 -> x3, waiting for transfers between devices: none -> 2.22 us  [some_pairs(): return lax.ppermute(x, BOX, pairs)]
    pallas_call x7 -> x5, Pallas kernels: 10.5 us -> 8.77 us  [translate(): pl.pallas_call(functools.partial(class_kernel, k), out_shape=out, in_spec...]
    add x2 -> x1, other arithmetic: 1.57 us -> 0.31 us  [turn(): return (a[0] * b[0] - a[1] * b[1], a[1] * b[0] + a[0] * b[1])]
    sin x3 -> x2, other arithmetic: 2.04 us -> 1.03 us  [the longest x1 0.99 us: phase_tables(): jnp.sin(along_y)]
    pallas_call x0 -> x1, Pallas kernels: none -> 0.98 us  [local(): pl.pallas_call(prepare_kernel, out_shape=[pltpu.VMEM(interp_theta.shape[:...]
    ppermute x11 -> x12, starting transfers between devices: 10.8 us -> 11 us  [shift(): return lax.ppermute(x, axis, [(i, (i + step) % size) for i in range(size)])]
  transfers between devices with their start and end apart: 13 -> 17, of which waited for: 7 -> 9; matrix products, arithmetic and copies ran while one was open for 6% -> 3% of each run, Pallas kernels for 18% -> 18%
where the time goes in v2:
time: 65.6 us; the launch traced here: 65.2 us
  starting transfers between devices  28 us (43%)
  waiting for transfers between devices  18.1 us (28%)
  Pallas kernels  16 us (24%)
  other arithmetic  1.49 us (2%)
  between operations  0.89 us (1%)
  local copies, waits for them, and re-layouts  0.71 us (1%)
    ppermute x12, waiting for transfers between devices, shift(): return lax.ppermute(x, axis, [(i, (i + step) % size) for i in range(size)])  12 us
    ppermute x12, starting transfers between devices, shift(): return lax.ppermute(x, axis, [(i, (i + step) % size) for i in range(size)])  11 us
    pallas_call x5, Pallas kernels, translate(): pl.pallas_call(functools.partial(class_kernel, k), out_shape=out, in_spec...  8.77 us
    all_to_all x1, starting transfers between devices, local(): x = lax.all_to_all(x, SAMP, split_axis=0, concat_axis=0, tiled=True)  8.43 us
    all_to_all x1, starting transfers between devices, local(): mine = lax.all_to_all(mine, SAMP, split_axis=0, concat_axis=0, tiled=True)  5.98 us
    all_to_all x1, waiting for transfers between devices, local(): mine = lax.all_to_all(mine, SAMP, split_axis=0, concat_axis=0, tiled=True)  3.23 us
    ppermute x3, starting transfers between devices, some_pairs(): return lax.ppermute(x, BOX, pairs)  2.63 us
    ppermute x3, waiting for transfers between devices, some_pairs(): return lax.ppermute(x, BOX, pairs)  2.22 us
  transfers between devices with their start and end apart: 17, of which 9 were waited for; matrix products, arithmetic and copies ran while one was open for 3% of the time, Pallas kernels for 18%

profile of v2, /device:TPU:1, one launch (start us, length us, event | category | flops | bytes accessed | tf_op | source)
XLA Modules:
  0.0 65.2 jit_solution(787135064246056476)
XLA Ops:
  0.6 8.4 %all-to-all-start = ((bf16[16,16,2,4,128]{4,3,2,1,0:T(4,128)(2,1)}), bf16[16,16,2,4,128]{4,3,2,1,0:T(4,128)(2,1)S(1)}, u32[]{:S(2)}, u32[]{:S(2)}) async-start(bf16[16,16,2,4,128]{4,3,2,1,0:T(4,128)(2,1)} %bitcast.7), calls=%async_computation | async-start | bytes 1048576 | tf_op jit(solution)/shard_map/all_to_all | solution.py:262
  9.1 1.0 %collective-permute-start = (s32[1,8,16]{2,1,0:T(8,128)}, s32[1,8,16]{2,1,0:T(8,128)S(1)}, u32[]{:S(2)}, u32[]{:S(2)}) collective-permute-start(s32[1,8,16]{2,1,0:T(8,128)} %param.11), channel_id=1, source_target_pairs={{0,16},{16,0},{1,17},{17,1},{2,18},{18,2},{3,19},{19,3},{4,20},{20... | collective-permute-start | bytes 1544 | tf_op jit(solution)/shard_map/ppermute | solution.py:173
  10.1 0.7 %constant_dynamic-update-slice_fusion.1 = s32[2,8,16]{2,1,0:T(8,128)S(1)} fusion(s32[1,8,16]{2,1,0:T(8,128)} %param.11), kind=kLoop, calls=%fused_computation.16 | loop fusion | bytes 4608
  10.8 0.1 sine_negate_fusion
  11.0 1.0 %multiply_sine_fusion = (f32[128,256]{1,0:T(8,128)S(1)}, f32[128,256]{1,0:T(8,128)S(1)}, f32[128,256]{1,0:T(8,128)S(1)}, f32[128,256]{1,0:T(8,128)S(1)}) fusion(f32[256]{0:T(256)S(1)} %get-tuple-element.98, f32[128]{0:T(128)S(1)} %sine_multiply_fusion, f32[256]{0:T(256)S(1)} %get-tuple-element.99), kind=kLoop, calls=%fused_computation.11 | loop fusion | flops 65536 | bytes 526848 | tf_op jit(solution)/shard_map/sin | solution.py:34
  12.0 0.0 collective-permute-done
  12.0 2.8 %collective-permute-start.1 = (s32[2,8,16]{2,1,0:T(8,128)S(1)}, s32[2,8,16]{2,1,0:T(8,128)S(1)}, u32[]{:S(2)}, u32[]{:S(2)}) collective-permute-start(s32[2,8,16]{2,1,0:T(8,128)S(1)} %constant_dynamic-update-slice_fusion.own_ref), channel_id=1, source_target_pairs={{0,96},{32,0},{64,32},{96,64},{1,97},{33,1},{65,33},{97,65},{2,98}... | collective-permute-start | bytes 3080 | tf_op jit(solution)/shard_map/ppermute | solution.py:173
  14.8 0.0 collective-permute-start.2
  14.8 0.3 fusion.5
  15.2 1.0 %prepare.1 = (bf16[128,64]{1,0:T(8,128)(2,1)S(1)}, bf16[128,256]{1,0:T(8,128)(2,1)S(1)}) custom-call(bf16[64,128]{1,0:T(8,128)(2,1)} %theta_hbm.1, bf16[128,256]{1,0:T(8,128)(2,1)} %phi_hbm.1), custom_call_target="tpu_custom_call" | custom-call | flops 1048576 | bytes 262144 | tf_op jit(solution)/shard_map/prepare/pallas_call | solution.py:265
  16.1 0.0 collective-permute-done.1.after_ref
  16.2 2.7 %collective-permute-done.2.before_ref = s32[2,8,16]{2,1,0:T(8,128)S(1)} collective-permute-done((s32[2,8,16]{2,1,0:T(8,128)S(1)}, s32[2,8,16]{2,1,0:T(8,128)S(1)}, u32[]{:S(2)}, u32[]{:S(2)}) %collective-permute-start.2) | collective-permute-done | bytes 1056 | tf_op jit(solution)/shard_map/ppermute | solution.py:173
  18.8 0.6 all-to-all-done.x_ref
  19.4 1.9 %aggregate.1 = bf16[16,2,2,8,256]{4,3,2,1,0:T(8,128)(2,1)} custom-call(bf16[16,16,2,4,128]{4,3,2,1,0:T(4,128)(2,1)S(1)} %all-to-all-done.x_ref, bf16[128,64]{1,0:T(8,128)(2,1)S(1)} %get-tuple-element.53.theta_ref, bf16[128,256]{1,0:T(8,128)(2,1)S(1)} %get-tuple-element.54.phi_ref, f32[4,128,256]{2,1,0:T(8,128)S(1)} %get-tuple-element.91.cos_ref, ...), custom_call_target="tpu_custom_call" | custom-call | flops 351272960 | bytes 4194304 | tf_op jit(solution)/shard_map/aggregate/pallas_call | solution.py:285
  21.3 6.0 %all-to-all-start.1 = ((bf16[16,2,2,8,256]{4,3,2,1,0:T(8,128)(2,1)}), bf16[16,2,2,8,256]{4,3,2,1,0:T(8,128)(2,1)S(1)}, u32[]{:S(2)}, u32[]{:S(2)}) async-start(bf16[16,2,2,8,256]{4,3,2,1,0:T(8,128)(2,1)} %aggregate.1), calls=%async_computation.1 | async-start | bytes 524288 | tf_op jit(solution)/shard_map/all_to_all | solution.py:298
  27.3 0.6 collective-permute-start.3
  27.9 1.7 %stage.1.x_ref = bf16[316,2,8,256]{3,2,1,0:T(8,128)(2,1)S(1)} custom-call(bf16[316,2,8,256]{3,2,1,0:T(8,128)(2,1)} %x_ref), custom_call_target="tpu_custom_call" | custom-call | flops 1 | bytes 5242880 | tf_op jit(solution)/shard_map/stage/pallas_call | solution.py:299
  29.6 0.0 copy-start
  29.6 0.0 copy-start.1
  29.6 1.8 %collective-permute-done.3.far_ref = s32[2,8,16]{2,1,0:T(8,128)S(1)} collective-permute-done((s32[2,8,16]{2,1,0:T(8,128)S(1)}, s32[2,8,16]{2,1,0:T(8,128)S(1)}, u32[]{:S(2)}, u32[]{:S(2)}) %collective-permute-start.3) | collective-permute-done | bytes 1056 | tf_op jit(solution)/shard_map/ppermute | solution.py:173
  31.4 3.2 %all-to-all-done.1 = bf16[16,2,2,8,256]{4,3,2,1,0:T(8,128)(2,1)S(1)} async-done(((bf16[16,2,2,8,256]{4,3,2,1,0:T(8,128)(2,1)}), bf16[16,2,2,8,256]{4,3,2,1,0:T(8,128)(2,1)S(1)}, u32[]{:S(2)}, u32[]{:S(2)}) %all-to-all-start.1) | async-done | bytes 262176 | tf_op jit(solution)/shard_map/all_to_all | solution.py:298
  34.6 2.9 %collective-permute-start.4 = (bf16[32,2,8,256]{3,2,1,0:T(8,128)(2,1)S(1)}, bf16[32,2,8,256]{3,2,1,0:T(8,128)(2,1)S(1)}, u32[]{:S(2)}, u32[]{:S(2)}) collective-permute-start(bf16[32,2,8,256]{3,2,1,0:T(8,128)(2,1)S(1)} %bitcast.2), channel_id=1, source_target_pairs={{0,16},{16,0},{1,17},{17,1},{2,18},{18,2},{3,19},{19,3},{4,20},{20... | collective-permute-start | bytes 786440 | tf_op jit(solution)/shard_map/ppermute | solution.py:173
  37.5 0.6 collective-permute-start.5
  38.1 0.9 %collective-permute-start.6 = (bf16[32,2,8,256]{3,2,1,0:T(8,128)(2,1)S(1)}, bf16[32,2,8,256]{3,2,1,0:T(8,128)(2,1)S(1)}, u32[]{:S(2)}, u32[]{:S(2)}) collective-permute-start(bf16[32,2,8,256]{3,2,1,0:T(8,128)(2,1)S(1)} %bitcast.4), channel_id=1, source_target_pairs={{0,32},{32,64},{64,96},{96,0},{1,33},{33,65},{65,97},{97,1},{2,34}... | collective-permute-start | bytes 786440 | tf_op jit(solution)/shard_map/ppermute | solution.py:173
  39.0 0.5 widen.1.trans_ref
  39.5 0.7 %collective-permute-start.9 = (bf16[32,2,8,256]{3,2,1,0:T(8,128)(2,1)S(1)}, bf16[32,2,8,256]{3,2,1,0:T(8,128)(2,1)S(1)}, u32[]{:S(2)}, u32[]{:S(2)}) collective-permute-start(bf16[32,2,8,256]{3,2,1,0:T(8,128)(2,1)S(1)} %bitcast.5), channel_id=1, source_target_pairs={{0,64},{32,96},{64,0},{96,32},{1,65},{33,97},{65,1},{97,33},{2,66}... | collective-permute-start | bytes 786440 | tf_op jit(solution)/shard_map/ppermute | solution.py:229
  40.2 2.0 %plan.1.list_ref = s32[64,128]{1,0:T(8,128)S(4)} custom-call(s32[32,128]{1,0:T(8,128)S(1)} %broadcast_in_dim.2.me_ref, s32[2,8,16]{2,1,0:T(8,128)S(1)} %constant_dynamic-update-slice_fusion.own_ref, s32[2,8,16]{2,1,0:T(8,128)S(1)} %collective-permute-done.1.after_ref, s32[2,8,16]{2,1,0:T(8,128)S(1)} %collective-permute-done.2.before_ref, ...), custom_call_target="tpu_custom_call" | custom-call | flops 1048576 | bytes 1048576 | tf_op jit(solution)/shard_map/plan/pallas_call | solution.py:239
  42.3 0.0 collective-permute-done.4.refs_1_
  42.3 1.3 %shard_map.86 = (f32[32,2,8,256]{3,2,1,0:T(8,128)S(1)}, f32[257,2,8,256]{3,2,1,0:T(8,128)S(1)}, bf16[32,2,8,256]{3,2,1,0:T(8,128)(2,1)}) custom-call(s32[64,128]{1,0:T(8,128)S(4)} %plan.1.list_ref, f32[316,2,8,256]{3,2,1,0:T(8,128)S(1)} %widen.1.trans_ref, bf16[32,2,8,256]{3,2,1,0:T(8,128)(2,1)S(1)} %bitcast.6, ...), custom_call_target="tpu_custom_call" | custom-call | flops 16777216 | bytes 8388608 | tf_op jit(solution)/shard_map/pallas_call | solution.py:348
  43.5 1.8 %collective-permute-done.5.refs_1_ = bf16[32,2,8,256]{3,2,1,0:T(8,128)(2,1)S(1)} collective-permute-done((bf16[32,2,8,256]{3,2,1,0:T(8,128)(2,1)S(1)}, bf16[32,2,8,256]{3,2,1,0:T(8,128)(2,1)S(1)}, u32[]{:S(2)}, u32[]{:S(2)}) %collective-permute-start.5) | collective-permute-done | bytes 262176 | tf_op jit(solution)/shard_map/ppermute | solution.py:173
  45.4 4.4 %collective-permute-done.6.refs_2_ = bf16[32,2,8,256]{3,2,1,0:T(8,128)(2,1)S(1)} collective-permute-done((bf16[32,2,8,256]{3,2,1,0:T(8,128)(2,1)S(1)}, bf16[32,2,8,256]{3,2,1,0:T(8,128)(2,1)S(1)}, u32[]{:S(2)}, u32[]{:S(2)}) %collective-permute-start.6) | collective-permute-done | bytes 262176 | tf_op jit(solution)/shard_map/ppermute | solution.py:173
  49.7 1.1 %collective-permute-start.10 = (bf16[32,2,8,256]{3,2,1,0:T(8,128)(2,1)S(1)}, bf16[32,2,8,256]{3,2,1,0:T(8,128)(2,1)S(1)}, u32[]{:S(2)}, u32[]{:S(2)}) collective-permute-start(bf16[32,2,8,256]{3,2,1,0:T(8,128)(2,1)S(1)} %collective-permute-done.5.refs_1_), channel_id=1, source_target_pairs={{0,16},{16,0},{1,17},{17,1},{2,18},{18,2},{3,19},{19,3},{4,20},{20... | collective-permute-start | bytes 786440 | tf_op jit(solution)/shard_map/ppermute | solution.py:173
  50.9 0.0 collective-permute-start.11
  50.9 1.8 %shard_map.87 = (f32[32,2,8,256]{3,2,1,0:T(8,128)S(1)}, f32[257,2,8,256]{3,2,1,0:T(8,128)S(1)}) custom-call(s32[64,128]{1,0:T(8,128)S(4)} %plan.1.list_ref, f32[316,2,8,256]{3,2,1,0:T(8,128)S(1)} %widen.1.trans_ref, f32[32,2,8,256]{3,2,1,0:T(8,128)S(1)} %get-tuple-element.74.refs_0_, ...), custom_call_target="tpu_custom_call", output_to_operand_aliasing={{1}: (5, {})} | custom-call | flops 16777216 | bytes 8388608 | tf_op jit(solution)/shard_map/pallas_call | solution.py:348
  52.7 0.0 collective-permute-done.9.refs_1_
  52.7 0.6 collective-permute-start.12
  53.3 0.7 %collective-permute-start.7 = (bf16[32,2,8,256]{3,2,1,0:T(8,128)(2,1)S(1)}, bf16[32,2,8,256]{3,2,1,0:T(8,128)(2,1)S(1)}, u32[]{:S(2)}, u32[]{:S(2)}) collective-permute-start(bf16[32,2,8,256]{3,2,1,0:T(8,128)(2,1)S(1)} %collective-permute-done.6.refs_2_), channel_id=1, source_target_pairs={{48,80},{80,112},{49,81},{81,113},{50,82},{82,114},{51,83},{83,115... | collective-permute-start | bytes 786440 | tf_op jit(solution)/shard_map/ppermute | solution.py:229
  54.0 1.3 %collective-permute-start.8 = (bf16[32,2,8,256]{3,2,1,0:T(8,128)(2,1)S(1)}, bf16[32,2,8,256]{3,2,1,0:T(8,128)(2,1)S(1)}, u32[]{:S(2)}, u32[]{:S(2)}) collective-permute-start(bf16[32,2,8,256]{3,2,1,0:T(8,128)(2,1)S(1)} %collective-permute-done.5.refs_1_), channel_id=1, source_target_pairs={{48,16},{80,48},{49,17},{81,49},{50,18},{82,50},{51,19},{83,51},{5... | collective-permute-start | bytes 786440 | tf_op jit(solution)/shard_map/ppermute | solution.py:229
  55.3 0.0 collective-permute-done.11.refs_2_
  55.3 2.1 %shard_map.88 = (f32[32,2,8,256]{3,2,1,0:T(8,128)S(1)}, f32[257,2,8,256]{3,2,1,0:T(8,128)S(1)}) custom-call(s32[64,128]{1,0:T(8,128)S(4)} %plan.1.list_ref, f32[316,2,8,256]{3,2,1,0:T(8,128)S(1)} %widen.1.trans_ref, f32[32,2,8,256]{3,2,1,0:T(8,128)S(1)} %get-tuple-element.78.refs_0_, ...), custom_call_target="tpu_custom_call", output_to_operand_aliasing={{1}: (5, {})} | custom-call | flops 16777216 | bytes 8388608 | tf_op jit(solution)/shard_map/pallas_call | solution.py:348
  57.5 1.4 %shard_map.89 = (f32[32,2,8,256]{3,2,1,0:T(8,128)S(1)}, f32[257,2,8,256]{3,2,1,0:T(8,128)S(1)}) custom-call(s32[64,128]{1,0:T(8,128)S(4)} %plan.1.list_ref, f32[316,2,8,256]{3,2,1,0:T(8,128)S(1)} %widen.1.trans_ref, f32[32,2,8,256]{3,2,1,0:T(8,128)S(1)} %get-tuple-element.80.refs_0_, ...), custom_call_target="tpu_custom_call", output_to_operand_aliasing={{1}: (5, {})} | custom-call | flops 16777216 | bytes 8388608 | tf_op jit(solution)/shard_map/pallas_call | solution.py:348
  58.9 0.0 collective-permute-done.7.refs_1_
  58.9 2.2 %collective-permute-done.8.refs_2_ = bf16[32,2,8,256]{3,2,1,0:T(8,128)(2,1)S(1)} collective-permute-done((bf16[32,2,8,256]{3,2,1,0:T(8,128)(2,1)S(1)}, bf16[32,2,8,256]{3,2,1,0:T(8,128)(2,1)S(1)}, u32[]{:S(2)}, u32[]{:S(2)}) %collective-permute-start.8) | collective-permute-done | bytes 262176 | tf_op jit(solution)/shard_map/ppermute | solution.py:229
  61.1 0.0 collective-permute-start.13
  61.1 0.5 collective-permute-start.14
  61.6 1.0 %collective-permute-done.13.refs_3_ = bf16[32,2,8,256]{3,2,1,0:T(8,128)(2,1)S(1)} collective-permute-done((bf16[32,2,8,256]{3,2,1,0:T(8,128)(2,1)S(1)}, bf16[32,2,8,256]{3,2,1,0:T(8,128)(2,1)S(1)}, u32[]{:S(2)}, u32[]{:S(2)}) %collective-permute-start.13) | collective-permute-done | bytes 262176 | tf_op jit(solution)/shard_map/ppermute | solution.py:173
  62.6 0.4 collective-permute-done.14.refs_4_
  63.0 2.1 %shard_map.90 = (f32[32,2,8,256]{3,2,1,0:T(8,128)}, f32[257,2,8,256]{3,2,1,0:T(8,128)S(1)}) custom-call(s32[64,128]{1,0:T(8,128)S(4)} %plan.1.list_ref, f32[316,2,8,256]{3,2,1,0:T(8,128)S(1)} %widen.1.trans_ref, f32[32,2,8,256]{3,2,1,0:T(8,128)S(1)} %get-tuple-element.85.refs_0_, ...), custom_call_target="tpu_custom_call", output_to_operand_aliasing={{1}: (7, {})} | custom-call | flops 16777216 | bytes 8388608 | tf_op jit(solution)/shard_map/pallas_call | solution.py:348
  (10 shorter events, 0.1 us)
Async XLA Ops:
  0.6 18.8 %all-to-all-start = ((bf16[16,16,2,4,128]{4,3,2,1,0:T(4,128)(2,1)}), bf16[16,16,2,4,128]{4,3,2,1,0:T(4,128)(2,1)S(1)}, u32[]{:S(2)}, u32[]{:S(2)}) async-start(bf16[16,16,2,4,128]{4,3,2,1,0:T(4,128)(2,1)} %bitcast.7), calls=%async_computation | async-start | bytes 1048576 | tf_op jit(solution)/shard_map/all_to_all | solution.py:262
  9.1 2.9 %collective-permute-start = (s32[1,8,16]{2,1,0:T(8,128)}, s32[1,8,16]{2,1,0:T(8,128)S(1)}, u32[]{:S(2)}, u32[]{:S(2)}) collective-permute-start(s32[1,8,16]{2,1,0:T(8,128)} %param.11), channel_id=1, source_target_pairs={{0,16},{16,0},{1,17},{17,1},{2,18},{18,2},{3,19},{19,3},{4,20},{20... | collective-permute-start | bytes 1544 | tf_op jit(solution)/shard_map/ppermute | solution.py:173
  12.0 4.1 %collective-permute-start.1 = (s32[2,8,16]{2,1,0:T(8,128)S(1)}, s32[2,8,16]{2,1,0:T(8,128)S(1)}, u32[]{:S(2)}, u32[]{:S(2)}) collective-permute-start(s32[2,8,16]{2,1,0:T(8,128)S(1)} %constant_dynamic-update-slice_fusion.own_ref), channel_id=1, source_target_pairs={{0,96},{32,0},{64,32},{96,64},{1,97},{33,1},{65,33},{97,65},{2,98}... | collective-permute-start | bytes 3080 | tf_op jit(solution)/shard_map/ppermute | solution.py:173
  14.8 4.0 %collective-permute-start.2 = (s32[2,8,16]{2,1,0:T(8,128)S(1)}, s32[2,8,16]{2,1,0:T(8,128)S(1)}, u32[]{:S(2)}, u32[]{:S(2)}) collective-permute-start(s32[2,8,16]{2,1,0:T(8,128)S(1)} %constant_dynamic-update-slice_fusion.own_ref), channel_id=1, source_target_pairs={{0,32},{32,64},{64,96},{96,0},{1,33},{33,65},{65,97},{97,1},{2,34}... | collective-permute-start | bytes 3080 | tf_op jit(solution)/shard_map/ppermute | solution.py:173
  21.3 13.3 %all-to-all-start.1 = ((bf16[16,2,2,8,256]{4,3,2,1,0:T(8,128)(2,1)}), bf16[16,2,2,8,256]{4,3,2,1,0:T(8,128)(2,1)S(1)}, u32[]{:S(2)}, u32[]{:S(2)}) async-start(bf16[16,2,2,8,256]{4,3,2,1,0:T(8,128)(2,1)} %aggregate.1), calls=%async_computation.1 | async-start | bytes 524288 | tf_op jit(solution)/shard_map/all_to_all | solution.py:298
  27.3 4.1 %collective-permute-start.3 = (s32[2,8,16]{2,1,0:T(8,128)S(1)}, s32[2,8,16]{2,1,0:T(8,128)S(1)}, u32[]{:S(2)}, u32[]{:S(2)}) collective-permute-start(s32[2,8,16]{2,1,0:T(8,128)S(1)} %constant_dynamic-update-slice_fusion.own_ref), channel_id=1, source_target_pairs={{0,64},{32,96},{64,0},{96,32},{1,65},{33,97},{65,1},{97,33},{2,66}... | collective-permute-start | bytes 3080 | tf_op jit(solution)/shard_map/ppermute | solution.py:173
  29.6 10.6 %copy-start = (s32[32,64]{1,0:T(8,128)S(1)}, s32[32,64]{1,0:T(8,128)}, u32[]{:S(2)}) copy-start(s32[32,64]{1,0:T(8,128)} %slots_ref.1) | copy-start | bytes 24580
  29.6 10.6 %copy-start.1 = (s32[32,64]{1,0:T(8,128)S(1)}, s32[32,64]{1,0:T(8,128)}, u32[]{:S(2)}) copy-start(s32[32,64]{1,0:T(8,128)} %kinds_ref.1) | copy-start | bytes 24580
  34.6 7.6 %collective-permute-start.4 = (bf16[32,2,8,256]{3,2,1,0:T(8,128)(2,1)S(1)}, bf16[32,2,8,256]{3,2,1,0:T(8,128)(2,1)S(1)}, u32[]{:S(2)}, u32[]{:S(2)}) collective-permute-start(bf16[32,2,8,256]{3,2,1,0:T(8,128)(2,1)S(1)} %bitcast.2), channel_id=1, source_target_pairs={{0,16},{16,0},{1,17},{17,1},{2,18},{18,2},{3,19},{19,3},{4,20},{20... | collective-permute-start | bytes 786440 | tf_op jit(solution)/shard_map/ppermute | solution.py:173
  37.5 7.9 %collective-permute-start.5 = (bf16[32,2,8,256]{3,2,1,0:T(8,128)(2,1)S(1)}, bf16[32,2,8,256]{3,2,1,0:T(8,128)(2,1)S(1)}, u32[]{:S(2)}, u32[]{:S(2)}) collective-permute-start(bf16[32,2,8,256]{3,2,1,0:T(8,128)(2,1)S(1)} %bitcast.3), channel_id=1, source_target_pairs={{0,96},{32,0},{64,32},{96,64},{1,97},{33,1},{65,33},{97,65},{2,98}... | collective-permute-start | bytes 786440 | tf_op jit(solution)/shard_map/ppermute | solution.py:173
  38.1 11.6 %collective-permute-start.6 = (bf16[32,2,8,256]{3,2,1,0:T(8,128)(2,1)S(1)}, bf16[32,2,8,256]{3,2,1,0:T(8,128)(2,1)S(1)}, u32[]{:S(2)}, u32[]{:S(2)}) collective-permute-start(bf16[32,2,8,256]{3,2,1,0:T(8,128)(2,1)S(1)} %bitcast.4), channel_id=1, source_target_pairs={{0,32},{32,64},{64,96},{96,0},{1,33},{33,65},{65,97},{97,1},{2,34}... | collective-permute-start | bytes 786440 | tf_op jit(solution)/shard_map/ppermute | solution.py:173
  39.5 13.2 %collective-permute-start.9 = (bf16[32,2,8,256]{3,2,1,0:T(8,128)(2,1)S(1)}, bf16[32,2,8,256]{3,2,1,0:T(8,128)(2,1)S(1)}, u32[]{:S(2)}, u32[]{:S(2)}) collective-permute-start(bf16[32,2,8,256]{3,2,1,0:T(8,128)(2,1)S(1)} %bitcast.5), channel_id=1, source_target_pairs={{0,64},{32,96},{64,0},{96,32},{1,65},{33,97},{65,1},{97,33},{2,66}... | collective-permute-start | bytes 786440 | tf_op jit(solution)/shard_map/ppermute | solution.py:229
  49.7 5.6 %collective-permute-start.10 = (bf16[32,2,8,256]{3,2,1,0:T(8,128)(2,1)S(1)}, bf16[32,2,8,256]{3,2,1,0:T(8,128)(2,1)S(1)}, u32[]{:S(2)}, u32[]{:S(2)}) collective-permute-start(bf16[32,2,8,256]{3,2,1,0:T(8,128)(2,1)S(1)} %collective-permute-done.5.refs_1_), channel_id=1, source_target_pairs={{0,16},{16,0},{1,17},{17,1},{2,18},{18,2},{3,19},{19,3},{4,20},{20... | collective-permute-start | bytes 786440 | tf_op jit(solution)/shard_map/ppermute | solution.py:173
  50.9 4.4 %collective-permute-start.11 = (bf16[32,2,8,256]{3,2,1,0:T(8,128)(2,1)S(1)}, bf16[32,2,8,256]{3,2,1,0:T(8,128)(2,1)S(1)}, u32[]{:S(2)}, u32[]{:S(2)}) collective-permute-start(bf16[32,2,8,256]{3,2,1,0:T(8,128)(2,1)S(1)} %collective-permute-done.6.refs_2_), channel_id=1, source_target_pairs={{0,16},{16,0},{1,17},{17,1},{2,18},{18,2},{3,19},{19,3},{4,20},{20... | collective-permute-start | bytes 786440 | tf_op jit(solution)/shard_map/ppermute | solution.py:173
  52.7 4.7 %collective-permute-start.12 = (bf16[32,2,8,256]{3,2,1,0:T(8,128)(2,1)S(1)}, bf16[32,2,8,256]{3,2,1,0:T(8,128)(2,1)S(1)}, u32[]{:S(2)}, u32[]{:S(2)}) collective-permute-start(bf16[32,2,8,256]{3,2,1,0:T(8,128)(2,1)S(1)} %collective-permute-done.9.refs_1_), channel_id=1, source_target_pairs={{0,16},{16,0},{1,17},{17,1},{2,18},{18,2},{3,19},{19,3},{4,20},{20... | collective-permute-start | bytes 786440 | tf_op jit(solution)/shard_map/ppermute | solution.py:173
  53.3 5.6 %collective-permute-start.7 = (bf16[32,2,8,256]{3,2,1,0:T(8,128)(2,1)S(1)}, bf16[32,2,8,256]{3,2,1,0:T(8,128)(2,1)S(1)}, u32[]{:S(2)}, u32[]{:S(2)}) collective-permute-start(bf16[32,2,8,256]{3,2,1,0:T(8,128)(2,1)S(1)} %collective-permute-done.6.refs_2_), channel_id=1, source_target_pairs={{48,80},{80,112},{49,81},{81,113},{50,82},{82,114},{51,83},{83,115... | collective-permute-start | bytes 786440 | tf_op jit(solution)/shard_map/ppermute | solution.py:229
  54.0 7.1 %collective-permute-start.8 = (bf16[32,2,8,256]{3,2,1,0:T(8,128)(2,1)S(1)}, bf16[32,2,8,256]{3,2,1,0:T(8,128)(2,1)S(1)}, u32[]{:S(2)}, u32[]{:S(2)}) collective-permute-start(bf16[32,2,8,256]{3,2,1,0:T(8,128)(2,1)S(1)} %collective-permute-done.5.refs_1_), channel_id=1, source_target_pairs={{48,16},{80,48},{49,17},{81,49},{50,18},{82,50},{51,19},{83,51},{5... | collective-permute-start | bytes 786440 | tf_op jit(solution)/shard_map/ppermute | solution.py:229
  61.1 1.5 %collective-permute-start.13 = (bf16[32,2,8,256]{3,2,1,0:T(8,128)(2,1)S(1)}, bf16[32,2,8,256]{3,2,1,0:T(8,128)(2,1)S(1)}, u32[]{:S(2)}, u32[]{:S(2)}) collective-permute-start(bf16[32,2,8,256]{3,2,1,0:T(8,128)(2,1)S(1)} %collective-permute-done.7.refs_1_), channel_id=1, source_target_pairs={{0,16},{16,0},{1,17},{17,1},{2,18},{18,2},{3,19},{19,3},{4,20},{20... | collective-permute-start | bytes 786440 | tf_op jit(solution)/shard_map/ppermute | solution.py:173
  61.1 1.9 %collective-permute-start.14 = (bf16[32,2,8,256]{3,2,1,0:T(8,128)(2,1)S(1)}, bf16[32,2,8,256]{3,2,1,0:T(8,128)(2,1)S(1)}, u32[]{:S(2)}, u32[]{:S(2)}) collective-permute-start(bf16[32,2,8,256]{3,2,1,0:T(8,128)(2,1)S(1)} %collective-permute-done.8.refs_2_), channel_id=1, source_target_pairs={{0,16},{16,0},{1,17},{17,1},{2,18},{18,2},{3,19},{19,3},{4,20},{20... | collective-permute-start | bytes 786440 | tf_op jit(solution)/shard_map/ppermute | solution.py:173

commit v3 on v2

--- a/solution.py
+++ b/solution.py
@@ -13,7 +13,8 @@
 SAMP = ("x", "z")
 BOX = ("y", "c")
 WIDTH = 128
-ROWS = (0, 2, 4, 6, 7)
+ROWS = (0, 2, 4, 0, 1)
+FAR = 3
 CUTS = (0, 14, 28, 46, 54, 64)
 CHUNK = 16
 VMEM = pl.BlockSpec(memory_space=pltpu.VMEM)
@@ -111,18 +112,19 @@
         store.start()
     elif last:
         sum_ref, *blocks, _, final_ref, pool_ref, out_ref, sems = refs
+    elif k == FAR:
+        sum_ref, *blocks, out_ref, pool_ref = refs
     else:
         sum_ref, *blocks, _, out_ref, pool_ref = refs
     boxes = out_ref.shape[0]
-    groups = [blocks] if k > 2 else [[block] for block in blocks]
-    for i, group in enumerate(groups):
-
-        def widen(n, carry, group=group, start=(ROWS[k] + i) * boxes):
-            pool_ref[start + n] = sum(block[n].astype(jnp.float32) for block in group)
+    for i, block in enumerate(blocks):
+
+        def widen(n, carry, block=block, start=(ROWS[k] + i) * boxes):
+            pool_ref[start + n] = block[n].astype(jnp.float32)
             return carry
 
         lax.fori_loop(0, boxes, widen, 0, unroll=4)
-    if first:
+    if k in (0, FAR):
         pool_ref[pool_ref.shape[0] - 1] = jnp.zeros(pool_ref.shape[1:], jnp.float32)
 
     def add(b, j, acc):
@@ -139,7 +141,11 @@
         begin = list_ref[boxes + b, k - 1]
         end = CUTS[k] if last else jnp.minimum(list_ref[boxes + b, k], CUTS[k])
         acc = (sum_ref[b, 0], sum_ref[b, 1])
-        return lax.fori_loop(begin, end, lambda j, acc: add(b, j, acc), acc)
+        acc = lax.fori_loop(begin, end, lambda j, acc: add(b, j, acc), acc)
+        if k == FAR - 1:
+            end = list_ref[boxes + b, k]
+            acc = lax.fori_loop(CUTS[FAR], end, lambda j, acc: add(b, j, acc), acc)
+        return acc
 
     def pair(i, carry):
         places = (2 * i, 2 * i + 1)
@@ -185,15 +191,19 @@
     code = (dy * cores + dc) * cap + (slots & (cap - 1))
     is_me = lax.broadcasted_iota(jnp.int32, (receivers, cap), 0) == me[:receivers, :cap]
     pieces = []
-    side = me[:1, :cap] & 1
-    for table, block in ((own_ref, (0, 1)), (after_ref, (2, 4)), (far_ref, None), (before_ref, (3, 5))):
+    for table, block, step in (
+        (own_ref, 0, 1),
+        (after_ref, 2, 2),
+        (far_ref, 0, 1),
+        (before_ref, 3, 2),
+    ):
         for core in range(cores):
             mine = jnp.sum(jnp.where(is_me, table[core], 0), axis=0, keepdims=True)
-            pieces.append(mine + ((6 + (side ^ core)) if block is None else block[core]) * boxes)
+            pieces.append(mine + (block + step * core) * boxes)
     table = jnp.broadcast_to(jnp.concatenate(pieces, axis=1), (boxes, WIDTH))
     row = jnp.take_along_axis(table, jnp.concatenate([code, code], axis=1), axis=1)
     row = row[:, :entries]
-    klass = jnp.where(dy == 2, 3 + (sender & 1), jnp.where(dy == 0, 0, 1 + dc))
+    klass = jnp.where(dy == 0, 0, jnp.where(dy == 2, 3, 1) + dc)
     first = lax.broadcasted_iota(jnp.int32, (entries, entries), 0)
     second = lax.broadcasted_iota(jnp.int32, (entries, entries), 1)
     ahead = (first < second).astype(jnp.float32)
@@ -208,7 +218,12 @@
         inside = jnp.dot(mine.astype(jnp.float32), ahead, preferred_element_type=jnp.float32)
         spot = jnp.where(mine, begin + inside.astype(jnp.int32), spot)
         begin = begin + jnp.sum(mine.astype(jnp.int32), axis=1, keepdims=True)
-        keep = keep | ((slot >= CUTS[k]) & (slot < CUTS[k + 1]) & (slot < begin))
+        here = (slot >= CUTS[k]) & (slot < CUTS[k + 1]) & (slot < begin)
+        if k < FAR:
+            near_end = begin
+        else:
+            here = here & (slot >= near_end)
+        keep = keep | here
         ends = jnp.where(lane == k, begin, ends)
     value = jnp.transpose((row * 512 + kinds_ref[...]).astype(jnp.float32)).astype(jnp.int32)
     spot = jnp.transpose(spot.astype(jnp.float32)).astype(jnp.int32)
@@ -216,17 +231,12 @@
     for b in range(boxes):
         got = jnp.where(spot[:, b : b + 1] == target, value[:, b : b + 1], 0)
         list_ref[b : b + 1, :] = jnp.sum(got, axis=0, keepdims=True)
-    list_ref[:boxes, :] = jnp.where(keep, list_ref[:boxes, :], 8 * boxes * 512)
+    zero_row = jnp.where(slot < CUTS[FAR], 6 * boxes, 2 * boxes)
+    list_ref[:boxes, :] = jnp.where(keep, list_ref[:boxes, :], zero_row * 512)
     list_ref[boxes:, :] = ends
     copy = pltpu.make_async_copy(list_ref, out_ref, sem)
     copy.start()
     copy.wait()
-
-
-def some_pairs(x, pairs, core):
-    cores = lax.axis_size("c")
-    pairs = [(a * cores + core, b * cores + core) for a, b in pairs]
-    return lax.ppermute(x, BOX, pairs)
 
 
 def slot_tables(send_index):
@@ -295,7 +305,9 @@
         name="aggregate",
     )(x, theta, phi, cosine, sine)
     source, mine = lax.optimization_barrier((translator, mine))
-    mine = lax.all_to_all(mine, SAMP, split_axis=0, concat_axis=0, tiled=True)
+    whole = mine
+    mine = lax.all_to_all(whole, SAMP, split_axis=0, concat_axis=0, tiled=True)
+    far_whole = shift(whole, "y", 2)
     staged = pl.pallas_call(
         stage_kernel,
         out_shape=pltpu.VMEM(translator.shape, translator.dtype),
@@ -307,39 +319,44 @@
         name="stage",
     )(source)
     far_table = shift(near_tables[0], "y", 2)
-    mine, far_table, staged = lax.optimization_barrier((mine, far_table, staged))
+    lists = plan_lists(me, (*near_tables, far_table), list_slots, list_kinds)
+    mine, lists, staged = lax.optimization_barrier((mine, lists, staged))
     own = mine.reshape((parent_boxes,) + pattern)
     after = shift(own, "y", -1)
     before = shift(own, "y", 1)
     other = shift(own, "c", 1)
-    staged, own = lax.optimization_barrier((staged, own))
+    far_whole, staged, own = lax.optimization_barrier((far_whole, staged, own))
+    far = lax.all_to_all(far_whole, SAMP, split_axis=0, concat_axis=0, tiled=True)
+    far = far.reshape((parent_boxes,) + pattern)
     params = pltpu.CompilerParams(vmem_limit_bytes=4 << 20)
     cost = pl.CostEstimate(flops=16 << 20, bytes_accessed=8 << 20, transcendentals=0)
-    wide = pl.pallas_call(
-        widen_kernel,
-        out_shape=pltpu.VMEM(translator.shape, jnp.float32),
-        in_specs=[VMEM],
-        out_specs=VMEM,
-        compiler_params=params,
-        cost_estimate=cost,
-        name="widen",
-    )(staged)
-    own, wide, far_table = lax.optimization_barrier((own, wide, far_table))
-    lists = plan_lists(me, (*near_tables, far_table), list_slots, list_kinds)
-    far = some_pairs(own, [(y, (y + 2) % 4) for y in range(4)], 0)
-
+
+    def widen_tables(tables):
+        return pl.pallas_call(
+            widen_kernel,
+            out_shape=pltpu.VMEM(translator.shape, jnp.float32),
+            in_specs=[VMEM],
+            out_specs=VMEM,
+            compiler_params=params,
+            cost_estimate=cost,
+        )(tables)
+
+    wide = widen_tables(staged)
     shape = (parent_boxes,) + pattern
 
-    def translate(k, blocks, so_far):
+    def translate(k, wide, blocks, so_far):
         first, last = k == 0, k == len(CUTS) - 2
         field = (jax.ShapeDtypeStruct if last else pltpu.VMEM)(shape, jnp.float32)
-        out = [field, pltpu.VMEM((8 * parent_boxes + 1,) + pattern, jnp.float32)]
+        rows = (2 if k >= FAR else 6) * parent_boxes + 1
+        out = [field, pltpu.VMEM((rows,) + pattern, jnp.float32)]
         out_specs, scratch, aliases = [HBM if last else VMEM, VMEM], [], {}
         if first:
             out.append(jax.ShapeDtypeStruct(shape, jnp.bfloat16))
             out_specs.append(HBM)
             scratch = [pltpu.SemaphoreType.DMA]
             operands = blocks
+        elif k == FAR:
+            operands = [so_far[0], *blocks]
         else:
             operands = [so_far[0], *blocks, so_far[1]]
             aliases = {1 + len(operands): 1}
@@ -356,20 +373,16 @@
             cost_estimate=cost,
         )(lists, wide, *operands)
 
-    *state, parents = translate(0, [own, other], None)
+    *state, parents = translate(0, wide, [own, other], None)
     after, before, *state = lax.optimization_barrier((after, before, *state))
-    up = some_pairs(before, ((1, 2), (2, 3)), 1)
-    down = some_pairs(after, ((1, 0), (2, 1)), 1)
     across = [shift(after, "c", 1), shift(before, "c", 1)]
-    state = translate(1, [after, before], state)
-    far, *state = lax.optimization_barrier((far, *state))
-    far_across = shift(far, "c", 1)
-    state = translate(2, across, state)
-    state = translate(3, [far, far_across], state)
-    up, down, *state = lax.optimization_barrier((up, down, *state))
-    relayed = [up, down]
-    relayed += [shift(v, "c", 1) for v in relayed]
-    field, _ = translate(4, relayed, state)
+    state = translate(1, wide, [after, before], state)
+    state = translate(2, wide, across, state)
+    far, staged, *state = lax.optimization_barrier((far, staged, *state))
+    across = shift(far, "c", 1)
+    wide = widen_tables(staged)
+    state = translate(3, wide, [far], state)
+    field, _ = translate(4, wide, [across], state)
     return parents, field
 
 

time: 65.6 us -> 75 us (1.14)
  local copies, waits for them, and re-layouts: 0.71 us -> 12.8 us
  waiting for transfers between devices: 18.1 us -> 6.75 us
  starting transfers between devices: 28 us -> 32.5 us
  Pallas kernels: 16 us -> 19.9 us
    unnamed x5 -> x19, local copies, waits for them, and re-layouts: 0.7 us -> 12.8 us
    ppermute x12 -> x11, waiting for transfers between devices: 12 us -> 3.55 us  [shift(): return lax.ppermute(x, axis, [(i, (i + step) % size) for i in range(size)])]
    all_to_all x1 -> x2, starting transfers between devices: 5.98 us -> 10.4 us  [the longest x1 6.58 us: local(): lax.all_to_all(far_whole, SAMP, split_axis=0, concat_axis=0, tiled=True)]
    pallas_call x5, Pallas kernels: 8.77 us -> 12.2 us  [translate(): pl.pallas_call(functools.partial(class_kernel, k), out_shape=out, in_spec...]
    all_to_all x1 -> x2, waiting for transfers between devices: 3.23 us -> 0.01 us  [the longest x1 0.01 us: local(): mine = lax.all_to_all(whole, SAMP, split_axis=0, concat_axis=0, tiled=True)]
    ppermute x12 -> x11, starting transfers between devices: 11 us -> 13.7 us  [shift(): return lax.ppermute(x, axis, [(i, (i + step) % size) for i in range(size)])]
    ppermute x3 -> x0, starting transfers between devices: 2.63 us -> none  [some_pairs(): return lax.ppermute(x, BOX, pairs)]
    all_to_all x1, waiting for transfers between devices: 0.59 us -> 3.2 us  [local(): x = lax.all_to_all(x, SAMP, split_axis=0, concat_axis=0, tiled=True)]
  transfers between devices with their start and end apart: 17 -> 14, of which waited for: 9 -> 3; matrix products, arithmetic and copies ran while one was open for 3% -> 3% of each run, Pallas kernels for 18% -> 22%
where the time goes in v3:
time: 75 us; the launch traced here: 74.3 us
  starting transfers between devices  32.5 us (43%)
  Pallas kernels  19.9 us (27%)
  local copies, waits for them, and re-layouts  12.8 us (17%)
  waiting for transfers between devices  6.75 us (9%)
  other arithmetic  1.48 us (2%)
  between operations  0.86 us (1%)
    ppermute x11, starting transfers between devices, shift(): return lax.ppermute(x, axis, [(i, (i + step) % size) for i in range(size)])  13.7 us
    unnamed x19, local copies, waits for them, and re-layouts  12.8 us
    pallas_call x5, Pallas kernels, translate(): pl.pallas_call(functools.partial(class_kernel, k), out_shape=out, in_spec...  12.2 us
    all_to_all x1, starting transfers between devices, local(): x = lax.all_to_all(x, SAMP, split_axis=0, concat_axis=0, tiled=True)  8.43 us
    all_to_all x1, starting transfers between devices, local(): lax.all_to_all(far_whole, SAMP, split_axis=0, concat_axis=0, tiled=True)  6.58 us
    all_to_all x1, starting transfers between devices, local(): mine = lax.all_to_all(whole, SAMP, split_axis=0, concat_axis=0, tiled=True)  3.81 us
    ppermute x11, waiting for transfers between devices, shift(): return lax.ppermute(x, axis, [(i, (i + step) % size) for i in range(size)])  3.55 us
    all_to_all x1, waiting for transfers between devices, local(): x = lax.all_to_all(x, SAMP, split_axis=0, concat_axis=0, tiled=True)  3.2 us
  transfers between devices with their start and end apart: 14, of which 3 were waited for; matrix products, arithmetic and copies ran while one was open for 3% of the time, Pallas kernels for 22%

profile of v3, /device:TPU:1, one launch (start us, length us, event | category | flops | bytes accessed | tf_op | source)
XLA Modules:
  0.0 74.3 jit_solution(16136162341882406709)
XLA Ops:
  0.6 8.4 %all-to-all-start = ((bf16[16,16,2,4,128]{4,3,2,1,0:T(4,128)(2,1)}), bf16[16,16,2,4,128]{4,3,2,1,0:T(4,128)(2,1)S(1)}, u32[]{:S(2)}, u32[]{:S(2)}) async-start(bf16[16,16,2,4,128]{4,3,2,1,0:T(4,128)(2,1)} %bitcast.9), calls=%async_computation | async-start | bytes 1048576 | tf_op jit(solution)/shard_map/all_to_all | solution.py:272
  9.1 1.0 %collective-permute-start = (s32[1,8,16]{2,1,0:T(8,128)}, s32[1,8,16]{2,1,0:T(8,128)S(1)}, u32[]{:S(2)}, u32[]{:S(2)}) collective-permute-start(s32[1,8,16]{2,1,0:T(8,128)} %param.11), channel_id=1, source_target_pairs={{0,16},{16,0},{1,17},{17,1},{2,18},{18,2},{3,19},{19,3},{4,20},{20... | collective-permute-start | bytes 1544 | tf_op jit(solution)/shard_map/ppermute | solution.py:179
  10.2 0.7 constant_dynamic-update-slice_fusion.1
  10.9 1.0 %multiply_sine_fusion = (f32[128,256]{1,0:T(8,128)S(1)}, f32[128,256]{1,0:T(8,128)S(1)}, f32[128,256]{1,0:T(8,128)S(1)}, f32[128,256]{1,0:T(8,128)S(1)}) fusion(f32[256]{0:T(256)S(1)} %get-tuple-element.84, f32[128]{0:T(128)S(1)} %sine_multiply_fusion, f32[256]{0:T(256)S(1)} %get-tuple-element.85), kind=kLoop, calls=%fused_computation.11 | loop fusion | flops 65536 | bytes 526848 | tf_op jit(solution)/shard_map/sin | solution.py:35
  11.9 0.1 sine_negate_fusion
  12.0 0.0 collective-permute-done
  12.0 1.4 %collective-permute-start.2 = (s32[2,8,16]{2,1,0:T(8,128)S(1)}, s32[2,8,16]{2,1,0:T(8,128)S(1)}, u32[]{:S(2)}, u32[]{:S(2)}) collective-permute-start(s32[2,8,16]{2,1,0:T(8,128)S(1)} %constant_dynamic-update-slice_fusion.own_ref), channel_id=1, source_target_pairs={{0,32},{32,64},{64,96},{96,0},{1,33},{33,65},{65,97},{97,1},{2,34}... | collective-permute-start | bytes 3080 | tf_op jit(solution)/shard_map/ppermute | solution.py:179
  13.4 1.5 %collective-permute-start.1 = (s32[2,8,16]{2,1,0:T(8,128)S(1)}, s32[2,8,16]{2,1,0:T(8,128)S(1)}, u32[]{:S(2)}, u32[]{:S(2)}) collective-permute-start(s32[2,8,16]{2,1,0:T(8,128)S(1)} %constant_dynamic-update-slice_fusion.own_ref), channel_id=1, source_target_pairs={{0,96},{32,0},{64,32},{96,64},{1,97},{33,1},{65,33},{97,65},{2,98}... | collective-permute-start | bytes 3080 | tf_op jit(solution)/shard_map/ppermute | solution.py:179
  14.9 0.3 fusion.5
  15.2 1.0 %prepare.1 = (bf16[128,64]{1,0:T(8,128)(2,1)S(1)}, bf16[128,256]{1,0:T(8,128)(2,1)S(1)}) custom-call(bf16[64,128]{1,0:T(8,128)(2,1)} %theta_hbm.1, bf16[128,256]{1,0:T(8,128)(2,1)} %phi_hbm.1), custom_call_target="tpu_custom_call" | custom-call | flops 1048576 | bytes 262144 | tf_op jit(solution)/shard_map/prepare/pallas_call | solution.py:275
  16.2 0.0 collective-permute-done.2.before_ref
  16.2 0.0 collective-permute-done.1.after_ref
  16.2 3.2 %all-to-all-done.x_ref = bf16[16,16,2,4,128]{4,3,2,1,0:T(4,128)(2,1)S(1)} async-done(((bf16[16,16,2,4,128]{4,3,2,1,0:T(4,128)(2,1)}), bf16[16,16,2,4,128]{4,3,2,1,0:T(4,128)(2,1)S(1)}, u32[]{:S(2)}, u32[]{:S(2)}) %all-to-all-start) | async-done | bytes 524320 | tf_op jit(solution)/shard_map/all_to_all | solution.py:272
  19.4 1.9 %aggregate.1 = bf16[16,2,2,8,256]{4,3,2,1,0:T(8,128)(2,1)} custom-call(bf16[16,16,2,4,128]{4,3,2,1,0:T(4,128)(2,1)S(1)} %all-to-all-done.x_ref, bf16[128,64]{1,0:T(8,128)(2,1)S(1)} %get-tuple-element.42.theta_ref, bf16[128,256]{1,0:T(8,128)(2,1)S(1)} %get-tuple-element.43.phi_ref, f32[4,128,256]{2,1,0:T(8,128)S(1)} %get-tuple-element.77.cos_ref, ...), custom_call_target="tpu_custom_call" | custom-call | flops 351272960 | bytes 4194304 | tf_op jit(solution)/shard_map/aggregate/pallas_call | solution.py:295
  21.3 3.8 %all-to-all-start.1 = ((bf16[16,2,2,8,256]{4,3,2,1,0:T(8,128)(2,1)}), bf16[16,2,2,8,256]{4,3,2,1,0:T(8,128)(2,1)S(1)}, u32[]{:S(2)}, u32[]{:S(2)}) async-start(bf16[16,2,2,8,256]{4,3,2,1,0:T(8,128)(2,1)} %aggregate.1), calls=%async_computation.1 | async-start | bytes 524288 | tf_op jit(solution)/shard_map/all_to_all | solution.py:309
  25.2 2.8 %collective-permute-start.4 = (bf16[16,2,2,8,256]{4,3,2,1,0:T(8,128)(2,1)}, bf16[16,2,2,8,256]{4,3,2,1,0:T(8,128)(2,1)S(1)}, u32[]{:S(2)}, u32[]{:S(2)}) collective-permute-start(bf16[16,2,2,8,256]{4,3,2,1,0:T(8,128)(2,1)} %aggregate.1), channel_id=1, source_target_pairs={{0,64},{32,96},{64,0},{96,32},{1,65},{33,97},{65,1},{97,33},{2,66}... | collective-permute-start | bytes 786440 | tf_op jit(solution)/shard_map/ppermute | solution.py:179
  28.0 0.2 collective-permute-start.3
  28.2 1.7 %stage.1.x_ref = bf16[316,2,8,256]{3,2,1,0:T(8,128)(2,1)S(1)} custom-call(bf16[316,2,8,256]{3,2,1,0:T(8,128)(2,1)} %x_ref), custom_call_target="tpu_custom_call" | custom-call | flops 1 | bytes 5242880 | tf_op jit(solution)/shard_map/stage/pallas_call | solution.py:311
  30.0 3.1 %collective-permute-done.3.far_ref = s32[2,8,16]{2,1,0:T(8,128)S(1)} collective-permute-done((s32[2,8,16]{2,1,0:T(8,128)S(1)}, s32[2,8,16]{2,1,0:T(8,128)S(1)}, u32[]{:S(2)}, u32[]{:S(2)}) %collective-permute-start.3) | collective-permute-done | bytes 1056 | tf_op jit(solution)/shard_map/ppermute | solution.py:179
  33.1 2.0 %plan.1.list_ref = s32[64,128]{1,0:T(8,128)S(4)} custom-call(s32[32,128]{1,0:T(8,128)S(1)} %broadcast_in_dim.2.me_ref, s32[2,8,16]{2,1,0:T(8,128)S(1)} %constant_dynamic-update-slice_fusion.own_ref, s32[2,8,16]{2,1,0:T(8,128)S(1)} %collective-permute-done.1.after_ref, s32[2,8,16]{2,1,0:T(8,128)S(1)} %collective-permute-done.2.before_ref, ...), custom_call_target="tpu_custom_call" | custom-call | flops 1048576 | bytes 1048576 | tf_op jit(solution)/shard_map/plan/pallas_call | solution.py:249
  35.1 0.0 all-to-all-done.1
  35.1 2.9 %collective-permute-start.5 = (bf16[32,2,8,256]{3,2,1,0:T(8,128)(2,1)S(1)}, bf16[32,2,8,256]{3,2,1,0:T(8,128)(2,1)S(1)}, u32[]{:S(2)}, u32[]{:S(2)}) collective-permute-start(bf16[32,2,8,256]{3,2,1,0:T(8,128)(2,1)S(1)} %bitcast.3), channel_id=1, source_target_pairs={{0,16},{16,0},{1,17},{17,1},{2,18},{18,2},{3,19},{19,3},{4,20},{20... | collective-permute-start | bytes 786440 | tf_op jit(solution)/shard_map/ppermute | solution.py:179
  38.0 1.2 %collective-permute-start.7 = (bf16[32,2,8,256]{3,2,1,0:T(8,128)(2,1)S(1)}, bf16[32,2,8,256]{3,2,1,0:T(8,128)(2,1)}, u32[]{:S(2)}, u32[]{:S(2)}) collective-permute-start(bf16[32,2,8,256]{3,2,1,0:T(8,128)(2,1)S(1)} %bitcast.4), channel_id=1, source_target_pairs={{0,32},{32,64},{64,96},{96,0},{1,33},{33,65},{65,97},{97,1},{2,34}... | collective-permute-start | bytes 786440 | tf_op jit(solution)/shard_map/ppermute | solution.py:179
  39.2 1.4 %collective-permute-start.6 = (bf16[32,2,8,256]{3,2,1,0:T(8,128)(2,1)S(1)}, bf16[32,2,8,256]{3,2,1,0:T(8,128)(2,1)}, u32[]{:S(2)}, u32[]{:S(2)}) collective-permute-start(bf16[32,2,8,256]{3,2,1,0:T(8,128)(2,1)S(1)} %bitcast.5), channel_id=1, source_target_pairs={{0,96},{32,0},{64,32},{96,64},{1,97},{33,1},{65,33},{97,65},{2,98}... | collective-permute-start | bytes 786440 | tf_op jit(solution)/shard_map/ppermute | solution.py:179
  40.7 0.0 collective-permute-done.4
  40.7 0.5 shard_map.86.trans_ref
  41.2 0.2 copy-done.8
  41.4 1.3 %shard_map.87 = (f32[32,2,8,256]{3,2,1,0:T(8,128)S(1)}, f32[193,2,8,256]{3,2,1,0:T(8,128)S(1)}, bf16[32,2,8,256]{3,2,1,0:T(8,128)(2,1)}) custom-call(s32[64,128]{1,0:T(8,128)S(4)} %plan.1.list_ref, f32[316,2,8,256]{3,2,1,0:T(8,128)S(1)} %shard_map.86.trans_ref, bf16[32,2,8,256]{3,2,1,0:T(8,128)(2,1)S(1)} %bitcast.6, ...), custom_call_target="tpu_custom_call" | custom-call | flops 16777216 | bytes 8388608 | tf_op jit(solution)/shard_map/pallas_call | solution.py:365
  42.6 2.3 %copy-done = f32[316,2,8,256]{3,2,1,0:T(8,128)} copy-done((f32[316,2,8,256]{3,2,1,0:T(8,128)}, f32[316,2,8,256]{3,2,1,0:T(8,128)S(1)}, u32[]{:S(2)}) %copy-start) | copy-done | bytes 5177368
  45.0 1.7 %copy-done.2 = f32[193,2,8,256]{3,2,1,0:T(8,128)} copy-done((f32[193,2,8,256]{3,2,1,0:T(8,128)}, f32[193,2,8,256]{3,2,1,0:T(8,128)S(1)}, u32[]{:S(2)}) %copy-start.2) | copy-done | bytes 3162136
  46.7 0.4 collective-permute-done.7.refs_2_
  47.1 1.0 %collective-permute-start.8 = (bf16[32,2,8,256]{3,2,1,0:T(8,128)(2,1)}, bf16[32,2,8,256]{3,2,1,0:T(8,128)(2,1)}, u32[]{:S(2)}, u32[]{:S(2)}) collective-permute-start(bf16[32,2,8,256]{3,2,1,0:T(8,128)(2,1)} %collective-permute-done.6.refs_1_), channel_id=1, source_target_pairs={{0,16},{16,0},{1,17},{17,1},{2,18},{18,2},{3,19},{19,3},{4,20},{20... | collective-permute-start | bytes 786440 | tf_op jit(solution)/shard_map/ppermute | solution.py:179
  48.0 0.0 collective-permute-start.9
  48.1 6.6 %all-to-all-start.2 = ((bf16[16,2,2,8,256]{4,3,2,1,0:T(8,128)(2,1)}), bf16[16,2,2,8,256]{4,3,2,1,0:T(8,128)(2,1)S(1)}, u32[]{:S(2)}, u32[]{:S(2)}) async-start(bf16[16,2,2,8,256]{4,3,2,1,0:T(8,128)(2,1)} %copy-done.8), calls=%async_computation.2 | async-start | bytes 524288 | tf_op jit(solution)/shard_map/all_to_all | solution.py:329
  54.6 2.5 %copy-done.1 = f32[316,2,8,256]{3,2,1,0:T(8,128)S(1)} copy-done((f32[316,2,8,256]{3,2,1,0:T(8,128)S(1)}, f32[316,2,8,256]{3,2,1,0:T(8,128)}, u32[]{:S(2)}) %copy-start.1) | copy-done | bytes 5177368
  57.1 1.9 %copy-done.3 = f32[193,2,8,256]{3,2,1,0:T(8,128)S(1)} copy-done((f32[193,2,8,256]{3,2,1,0:T(8,128)S(1)}, f32[193,2,8,256]{3,2,1,0:T(8,128)}, u32[]{:S(2)}) %copy-start.3) | copy-done | bytes 3162136
  59.0 2.9 %shard_map.88 = (f32[32,2,8,256]{3,2,1,0:T(8,128)S(1)}, f32[193,2,8,256]{3,2,1,0:T(8,128)S(1)}) custom-call(s32[64,128]{1,0:T(8,128)S(4)} %plan.1.list_ref, f32[316,2,8,256]{3,2,1,0:T(8,128)S(1)} %copy-done.1, f32[32,2,8,256]{3,2,1,0:T(8,128)S(1)} %get-tuple-element.63.refs_0_, ...), custom_call_target="tpu_custom_call", output_to_operand_aliasing={{1}: (5, {})} | custom-call | flops 16777216 | bytes 8388608 | tf_op jit(solution)/shard_map/pallas_call | solution.py:365
  61.9 1.6 %copy-done.4 = f32[193,2,8,256]{3,2,1,0:T(8,128)} copy-done((f32[193,2,8,256]{3,2,1,0:T(8,128)}, f32[193,2,8,256]{3,2,1,0:T(8,128)S(1)}, u32[]{:S(2)}) %copy-start.4) | copy-done | bytes 3162136
  63.5 0.0 collective-permute-done.8.refs_1_
  63.5 0.0 collective-permute-done.9.refs_2_
  63.5 1.9 %copy-done.5 = f32[193,2,8,256]{3,2,1,0:T(8,128)S(1)} copy-done((f32[193,2,8,256]{3,2,1,0:T(8,128)S(1)}, f32[193,2,8,256]{3,2,1,0:T(8,128)}, u32[]{:S(2)}) %copy-start.5) | copy-done | bytes 3162136
  65.4 4.7 %shard_map.89 = (f32[32,2,8,256]{3,2,1,0:T(8,128)S(1)}, f32[193,2,8,256]{3,2,1,0:T(8,128)S(1)}) custom-call(s32[64,128]{1,0:T(8,128)S(4)} %plan.1.list_ref, f32[316,2,8,256]{3,2,1,0:T(8,128)S(1)} %copy-done.1, f32[32,2,8,256]{3,2,1,0:T(8,128)S(1)} %get-tuple-element.67.refs_0_, ...), custom_call_target="tpu_custom_call", output_to_operand_aliasing={{1}: (5, {})} | custom-call | flops 16777216 | bytes 8388608 | tf_op jit(solution)/shard_map/pallas_call | solution.py:365
  70.1 0.0 all-to-all-done.2
  70.1 0.2 collective-permute-start.10
  70.4 0.5 shard_map.90.trans_ref
  70.9 1.4 %shard_map.91 = (f32[32,2,8,256]{3,2,1,0:T(8,128)S(1)}, f32[65,2,8,256]{3,2,1,0:T(8,128)S(1)}) custom-call(s32[64,128]{1,0:T(8,128)S(4)} %plan.1.list_ref, f32[316,2,8,256]{3,2,1,0:T(8,128)S(1)} %shard_map.90.trans_ref, f32[32,2,8,256]{3,2,1,0:T(8,128)S(1)} %get-tuple-element.71.refs_0_, bf16[32,2,8,256]{3,2,1,0:T(8,128)(2,1)S(1)} %bitcast.8), custom_call_target="tpu_custom_call" | custom-call | flops 16777216 | bytes 8388608 | tf_op jit(solution)/shard_map/pallas_call | solution.py:365
  72.3 0.0 collective-permute-done.10.refs_1_
  72.3 2.0 %shard_map.92 = (f32[32,2,8,256]{3,2,1,0:T(8,128)}, f32[65,2,8,256]{3,2,1,0:T(8,128)S(1)}) custom-call(s32[64,128]{1,0:T(8,128)S(4)} %plan.1.list_ref, f32[316,2,8,256]{3,2,1,0:T(8,128)S(1)} %shard_map.90.trans_ref, f32[32,2,8,256]{3,2,1,0:T(8,128)S(1)} %get-tuple-element.73.refs_0_, ...), custom_call_target="tpu_custom_call", output_to_operand_aliasing={{1}: (4, {})} | custom-call | flops 16777216 | bytes 8388608 | tf_op jit(solution)/shard_map/pallas_call | solution.py:365
  (19 shorter events, 0.1 us)
Async XLA Ops:
  0.6 18.8 %all-to-all-start = ((bf16[16,16,2,4,128]{4,3,2,1,0:T(4,128)(2,1)}), bf16[16,16,2,4,128]{4,3,2,1,0:T(4,128)(2,1)S(1)}, u32[]{:S(2)}, u32[]{:S(2)}) async-start(bf16[16,16,2,4,128]{4,3,2,1,0:T(4,128)(2,1)} %bitcast.9), calls=%async_computation | async-start | bytes 1048576 | tf_op jit(solution)/shard_map/all_to_all | solution.py:272
  9.1 2.9 %collective-permute-start = (s32[1,8,16]{2,1,0:T(8,128)}, s32[1,8,16]{2,1,0:T(8,128)S(1)}, u32[]{:S(2)}, u32[]{:S(2)}) collective-permute-start(s32[1,8,16]{2,1,0:T(8,128)} %param.11), channel_id=1, source_target_pairs={{0,16},{16,0},{1,17},{17,1},{2,18},{18,2},{3,19},{19,3},{4,20},{20... | collective-permute-start | bytes 1544 | tf_op jit(solution)/shard_map/ppermute | solution.py:179
  12.0 4.2 %collective-permute-start.2 = (s32[2,8,16]{2,1,0:T(8,128)S(1)}, s32[2,8,16]{2,1,0:T(8,128)S(1)}, u32[]{:S(2)}, u32[]{:S(2)}) collective-permute-start(s32[2,8,16]{2,1,0:T(8,128)S(1)} %constant_dynamic-update-slice_fusion.own_ref), channel_id=1, source_target_pairs={{0,32},{32,64},{64,96},{96,0},{1,33},{33,65},{65,97},{97,1},{2,34}... | collective-permute-start | bytes 3080 | tf_op jit(solution)/shard_map/ppermute | solution.py:179
  13.4 2.8 %collective-permute-start.1 = (s32[2,8,16]{2,1,0:T(8,128)S(1)}, s32[2,8,16]{2,1,0:T(8,128)S(1)}, u32[]{:S(2)}, u32[]{:S(2)}) collective-permute-start(s32[2,8,16]{2,1,0:T(8,128)S(1)} %constant_dynamic-update-slice_fusion.own_ref), channel_id=1, source_target_pairs={{0,96},{32,0},{64,32},{96,64},{1,97},{33,1},{65,33},{97,65},{2,98}... | collective-permute-start | bytes 3080 | tf_op jit(solution)/shard_map/ppermute | solution.py:179
  21.3 11.7 %copy-start.6 = (s32[32,64]{1,0:T(8,128)S(1)}, s32[32,64]{1,0:T(8,128)}, u32[]{:S(2)}) copy-start(s32[32,64]{1,0:T(8,128)} %slots_ref.1) | copy-start | bytes 24580
  21.3 11.7 %copy-start.7 = (s32[32,64]{1,0:T(8,128)S(1)}, s32[32,64]{1,0:T(8,128)}, u32[]{:S(2)}) copy-start(s32[32,64]{1,0:T(8,128)} %kinds_ref.1) | copy-start | bytes 24580
  21.3 13.8 %all-to-all-start.1 = ((bf16[16,2,2,8,256]{4,3,2,1,0:T(8,128)(2,1)}), bf16[16,2,2,8,256]{4,3,2,1,0:T(8,128)(2,1)S(1)}, u32[]{:S(2)}, u32[]{:S(2)}) async-start(bf16[16,2,2,8,256]{4,3,2,1,0:T(8,128)(2,1)} %aggregate.1), calls=%async_computation.1 | async-start | bytes 524288 | tf_op jit(solution)/shard_map/all_to_all | solution.py:309
  25.2 15.5 %collective-permute-start.4 = (bf16[16,2,2,8,256]{4,3,2,1,0:T(8,128)(2,1)}, bf16[16,2,2,8,256]{4,3,2,1,0:T(8,128)(2,1)S(1)}, u32[]{:S(2)}, u32[]{:S(2)}) collective-permute-start(bf16[16,2,2,8,256]{4,3,2,1,0:T(8,128)(2,1)} %aggregate.1), channel_id=1, source_target_pairs={{0,64},{32,96},{64,0},{96,32},{1,65},{33,97},{65,1},{97,33},{2,66}... | collective-permute-start | bytes 786440 | tf_op jit(solution)/shard_map/ppermute | solution.py:179
  28.0 5.0 %collective-permute-start.3 = (s32[2,8,16]{2,1,0:T(8,128)S(1)}, s32[2,8,16]{2,1,0:T(8,128)S(1)}, u32[]{:S(2)}, u32[]{:S(2)}) collective-permute-start(s32[2,8,16]{2,1,0:T(8,128)S(1)} %constant_dynamic-update-slice_fusion.own_ref), channel_id=1, source_target_pairs={{0,64},{32,96},{64,0},{96,32},{1,65},{33,97},{65,1},{97,33},{2,66}... | collective-permute-start | bytes 3080 | tf_op jit(solution)/shard_map/ppermute | solution.py:179
  35.1 6.3 %collective-permute-start.5 = (bf16[32,2,8,256]{3,2,1,0:T(8,128)(2,1)S(1)}, bf16[32,2,8,256]{3,2,1,0:T(8,128)(2,1)S(1)}, u32[]{:S(2)}, u32[]{:S(2)}) collective-permute-start(bf16[32,2,8,256]{3,2,1,0:T(8,128)(2,1)S(1)} %bitcast.3), channel_id=1, source_target_pairs={{0,16},{16,0},{1,17},{17,1},{2,18},{18,2},{3,19},{19,3},{4,20},{20... | collective-permute-start | bytes 786440 | tf_op jit(solution)/shard_map/ppermute | solution.py:179
  38.0 9.1 %collective-permute-start.7 = (bf16[32,2,8,256]{3,2,1,0:T(8,128)(2,1)S(1)}, bf16[32,2,8,256]{3,2,1,0:T(8,128)(2,1)}, u32[]{:S(2)}, u32[]{:S(2)}) collective-permute-start(bf16[32,2,8,256]{3,2,1,0:T(8,128)(2,1)S(1)} %bitcast.4), channel_id=1, source_target_pairs={{0,32},{32,64},{64,96},{96,0},{1,33},{33,65},{65,97},{97,1},{2,34}... | collective-permute-start | bytes 786440 | tf_op jit(solution)/shard_map/ppermute | solution.py:179
  39.2 7.9 %collective-permute-start.6 = (bf16[32,2,8,256]{3,2,1,0:T(8,128)(2,1)S(1)}, bf16[32,2,8,256]{3,2,1,0:T(8,128)(2,1)}, u32[]{:S(2)}, u32[]{:S(2)}) collective-permute-start(bf16[32,2,8,256]{3,2,1,0:T(8,128)(2,1)S(1)} %bitcast.5), channel_id=1, source_target_pairs={{0,96},{32,0},{64,32},{96,64},{1,97},{33,1},{65,33},{97,65},{2,98}... | collective-permute-start | bytes 786440 | tf_op jit(solution)/shard_map/ppermute | solution.py:179
  40.7 0.7 copy-start.8
  42.6 2.3 %copy-start = (f32[316,2,8,256]{3,2,1,0:T(8,128)}, f32[316,2,8,256]{3,2,1,0:T(8,128)S(1)}, u32[]{:S(2)}) copy-start(f32[316,2,8,256]{3,2,1,0:T(8,128)S(1)} %shard_map.86.trans_ref) | copy-start | bytes 15532036
  45.0 1.7 %copy-start.2 = (f32[193,2,8,256]{3,2,1,0:T(8,128)}, f32[193,2,8,256]{3,2,1,0:T(8,128)S(1)}, u32[]{:S(2)}) copy-start(f32[193,2,8,256]{3,2,1,0:T(8,128)S(1)} %get-tuple-element.66.refs_3_) | copy-start | bytes 9486340
  47.1 16.4 %collective-permute-start.8 = (bf16[32,2,8,256]{3,2,1,0:T(8,128)(2,1)}, bf16[32,2,8,256]{3,2,1,0:T(8,128)(2,1)}, u32[]{:S(2)}, u32[]{:S(2)}) collective-permute-start(bf16[32,2,8,256]{3,2,1,0:T(8,128)(2,1)} %collective-permute-done.6.refs_1_), channel_id=1, source_target_pairs={{0,16},{16,0},{1,17},{17,1},{2,18},{18,2},{3,19},{19,3},{4,20},{20... | collective-permute-start | bytes 786440 | tf_op jit(solution)/shard_map/ppermute | solution.py:179
  48.0 15.5 %collective-permute-start.9 = (bf16[32,2,8,256]{3,2,1,0:T(8,128)(2,1)}, bf16[32,2,8,256]{3,2,1,0:T(8,128)(2,1)}, u32[]{:S(2)}, u32[]{:S(2)}) collective-permute-start(bf16[32,2,8,256]{3,2,1,0:T(8,128)(2,1)} %collective-permute-done.7.refs_2_), channel_id=1, source_target_pairs={{0,16},{16,0},{1,17},{17,1},{2,18},{18,2},{3,19},{19,3},{4,20},{20... | collective-permute-start | bytes 786440 | tf_op jit(solution)/shard_map/ppermute | solution.py:179
  48.1 22.1 %all-to-all-start.2 = ((bf16[16,2,2,8,256]{4,3,2,1,0:T(8,128)(2,1)}), bf16[16,2,2,8,256]{4,3,2,1,0:T(8,128)(2,1)S(1)}, u32[]{:S(2)}, u32[]{:S(2)}) async-start(bf16[16,2,2,8,256]{4,3,2,1,0:T(8,128)(2,1)} %copy-done.8), calls=%async_computation.2 | async-start | bytes 524288 | tf_op jit(solution)/shard_map/all_to_all | solution.py:329
  54.6 2.5 %copy-start.1 = (f32[316,2,8,256]{3,2,1,0:T(8,128)S(1)}, f32[316,2,8,256]{3,2,1,0:T(8,128)}, u32[]{:S(2)}) copy-start(f32[316,2,8,256]{3,2,1,0:T(8,128)} %copy-done) | copy-start | bytes 15532036
  57.1 1.9 %copy-start.3 = (f32[193,2,8,256]{3,2,1,0:T(8,128)S(1)}, f32[193,2,8,256]{3,2,1,0:T(8,128)}, u32[]{:S(2)}) copy-start(f32[193,2,8,256]{3,2,1,0:T(8,128)} %copy-done.2) | copy-start | bytes 9486340
  61.9 1.6 %copy-start.4 = (f32[193,2,8,256]{3,2,1,0:T(8,128)}, f32[193,2,8,256]{3,2,1,0:T(8,128)S(1)}, u32[]{:S(2)}) copy-start(f32[193,2,8,256]{3,2,1,0:T(8,128)S(1)} %get-tuple-element.68.refs_3_) | copy-start | bytes 9486340
  63.5 1.9 %copy-start.5 = (f32[193,2,8,256]{3,2,1,0:T(8,128)S(1)}, f32[193,2,8,256]{3,2,1,0:T(8,128)}, u32[]{:S(2)}) copy-start(f32[193,2,8,256]{3,2,1,0:T(8,128)} %copy-done.4) | copy-start | bytes 9486340
  70.1 2.2 %collective-permute-start.10 = (bf16[32,2,8,256]{3,2,1,0:T(8,128)(2,1)S(1)}, bf16[32,2,8,256]{3,2,1,0:T(8,128)(2,1)S(1)}, u32[]{:S(2)}, u32[]{:S(2)}) collective-permute-start(bf16[32,2,8,256]{3,2,1,0:T(8,128)(2,1)S(1)} %bitcast.7), channel_id=1, source_target_pairs={{0,16},{16,0},{1,17},{17,1},{2,18},{18,2},{3,19},{19,3},{4,20},{20... | collective-permute-start | bytes 786440 | tf_op jit(solution)/shard_map/ppermute | solution.py:179

commit v4 on v3

--- a/solution.py
+++ b/solution.py
@@ -241,7 +241,7 @@
 
 def slot_tables(send_index):
     own = jnp.concatenate([send_index, shift(send_index, "c", 1)], axis=0)
-    return own, shift(own, "y", -1), shift(own, "y", 1)
+    return own, shift(own, "y", -1), shift(own, "y", 1), shift(own, "y", 2)
 
 
 def plan_lists(me, tables, list_slots, list_kinds):
@@ -290,8 +290,8 @@
     )(interp_theta, interp_phi)
     me = lax.axis_index("y") * lax.axis_size("c") + lax.axis_index("c")
     me = jnp.broadcast_to(me.astype(jnp.int32), (parent_boxes, WIDTH))
-    near_tables = slot_tables(send_index)
-    x, theta, phi, me, *near_tables = lax.optimization_barrier((x, theta, phi, me, *near_tables))
+    tables = slot_tables(send_index)
+    x, theta, phi, me, *tables = lax.optimization_barrier((x, theta, phi, me, *tables))
     mine = pl.pallas_call(
         aggregate_kernel,
         out_shape=jax.ShapeDtypeStruct((samp_count, own_children // 8) + pattern, jnp.bfloat16),
@@ -318,8 +318,7 @@
         cost_estimate=pl.CostEstimate(flops=1, bytes_accessed=5 << 20, transcendentals=0),
         name="stage",
     )(source)
-    far_table = shift(near_tables[0], "y", 2)
-    lists = plan_lists(me, (*near_tables, far_table), list_slots, list_kinds)
+    lists = plan_lists(me, tables, list_slots, list_kinds)
     mine, lists, staged = lax.optimization_barrier((mine, lists, staged))
     own = mine.reshape((parent_boxes,) + pattern)
     after = shift(own, "y", -1)

time: 75 us -> 72.8 us (0.971)
  waiting for transfers between devices: 6.75 us -> 3.92 us
  starting transfers between devices: 32.5 us -> 33.9 us
    all_to_all x1, waiting for transfers between devices: 3.2 us -> 0.75 us  [local(): x = lax.all_to_all(x, SAMP, split_axis=0, concat_axis=0, tiled=True)]
    ppermute x11, waiting for transfers between devices: 3.55 us -> 1.14 us  [shift(): return lax.ppermute(x, axis, [(i, (i + step) % size) for i in range(size)])]
    all_to_all x1, starting transfers between devices: 3.81 us -> 5.94 us  [local(): mine = lax.all_to_all(whole, SAMP, split_axis=0, concat_axis=0, tiled=True)]
    all_to_all x1, waiting for transfers between devices: 0.01 us -> 2.03 us  [local(): mine = lax.all_to_all(whole, SAMP, split_axis=0, concat_axis=0, tiled=True)]
    all_to_all x1, starting transfers between devices: 6.58 us -> 4.69 us  [local(): lax.all_to_all(far_whole, SAMP, split_axis=0, concat_axis=0, tiled=True)]
    ppermute x11, starting transfers between devices: 13.7 us -> 14.8 us  [shift(): return lax.ppermute(x, axis, [(i, (i + step) % size) for i in range(size)])]
    unnamed x19 -> x21, local copies, waits for them, and re-layouts: 12.8 us -> 12.1 us
  transfers between devices with their start and end apart: 14 -> 14, of which waited for: 3 -> 4; matrix products, arithmetic and copies ran while one was open for 3% -> 2% of each run, Pallas kernels for 22% -> 22%
where the time goes in v4:
time: 72.8 us; the launch traced here: 72.2 us
  starting transfers between devices  33.9 us (47%)
  Pallas kernels  19.9 us (27%)
  local copies, waits for them, and re-layouts  12.1 us (17%)
  waiting for transfers between devices  3.92 us (5%)
  other arithmetic  1.49 us (2%)
  between operations  0.88 us (1%)
    ppermute x11, starting transfers between devices, shift(): return lax.ppermute(x, axis, [(i, (i + step) % size) for i in range(size)])  14.8 us
    pallas_call x5, Pallas kernels, translate(): pl.pallas_call(functools.partial(class_kernel, k), out_shape=out, in_spec...  12.2 us
    unnamed x21, local copies, waits for them, and re-layouts  12.1 us
    all_to_all x1, starting transfers between devices, local(): x = lax.all_to_all(x, SAMP, split_axis=0, concat_axis=0, tiled=True)  8.43 us
    all_to_all x1, starting transfers between devices, local(): mine = lax.all_to_all(whole, SAMP, split_axis=0, concat_axis=0, tiled=True)  5.94 us
    all_to_all x1, starting transfers between devices, local(): lax.all_to_all(far_whole, SAMP, split_axis=0, concat_axis=0, tiled=True)  4.69 us
    pallas_call x1, Pallas kernels, plan_lists(): pl.pallas_call(plan_kernel, out_shape=pltpu.SMEM((2 * boxes, WIDTH), jnp....  2.04 us
    all_to_all x1, waiting for transfers between devices, local(): mine = lax.all_to_all(whole, SAMP, split_axis=0, concat_axis=0, tiled=True)  2.03 us
  transfers between devices with their start and end apart: 14, of which 4 were waited for; matrix products, arithmetic and copies ran while one was open for 2% of the time, Pallas kernels for 22%

profile of v4, /device:TPU:1, one launch (start us, length us, event | category | flops | bytes accessed | tf_op | source)
XLA Modules:
  0.0 72.2 jit_solution(18041883795976233091)
XLA Ops:
  0.6 8.4 %all-to-all-start = ((bf16[16,16,2,4,128]{4,3,2,1,0:T(4,128)(2,1)}), bf16[16,16,2,4,128]{4,3,2,1,0:T(4,128)(2,1)S(1)}, u32[]{:S(2)}, u32[]{:S(2)}) async-start(bf16[16,16,2,4,128]{4,3,2,1,0:T(4,128)(2,1)} %bitcast.9), calls=%async_computation | async-start | bytes 1048576 | tf_op jit(solution)/shard_map/all_to_all | solution.py:272
  9.1 1.0 %collective-permute-start = (s32[1,8,16]{2,1,0:T(8,128)}, s32[1,8,16]{2,1,0:T(8,128)S(1)}, u32[]{:S(2)}, u32[]{:S(2)}) collective-permute-start(s32[1,8,16]{2,1,0:T(8,128)} %param.11), channel_id=1, source_target_pairs={{0,16},{16,0},{1,17},{17,1},{2,18},{18,2},{3,19},{19,3},{4,20},{20... | collective-permute-start | bytes 1544 | tf_op jit(solution)/shard_map/ppermute | solution.py:179
  10.2 0.1 sine_negate_fusion
  10.3 1.0 %multiply_sine_fusion = (f32[128,256]{1,0:T(8,128)S(1)}, f32[128,256]{1,0:T(8,128)S(1)}, f32[128,256]{1,0:T(8,128)S(1)}, f32[128,256]{1,0:T(8,128)S(1)}) fusion(f32[256]{0:T(256)S(1)} %get-tuple-element.86, f32[128]{0:T(128)S(1)} %sine_multiply_fusion, f32[256]{0:T(256)S(1)} %get-tuple-element.87), kind=kLoop, calls=%fused_computation.11 | loop fusion | flops 65536 | bytes 526848 | tf_op jit(solution)/shard_map/sin | solution.py:35
  11.3 0.3 fusion.5
  11.7 0.0 collective-permute-done
  11.7 3.0 %collective-permute-start.3 = (s32[2,8,16]{2,1,0:T(8,128)S(1)}, s32[2,8,16]{2,1,0:T(8,128)S(1)}, u32[]{:S(2)}, u32[]{:S(2)}) collective-permute-start(s32[2,8,16]{2,1,0:T(8,128)S(1)} %constant_dynamic-update-slice_fusion.own_ref), channel_id=1, source_target_pairs={{0,64},{32,96},{64,0},{96,32},{1,65},{33,97},{65,1},{97,33},{2,66}... | collective-permute-start | bytes 3080 | tf_op jit(solution)/shard_map/ppermute | solution.py:179
  14.7 0.4 collective-permute-start.2
  15.1 2.3 %collective-permute-start.1 = (s32[2,8,16]{2,1,0:T(8,128)S(1)}, s32[2,8,16]{2,1,0:T(8,128)S(1)}, u32[]{:S(2)}, u32[]{:S(2)}) collective-permute-start(s32[2,8,16]{2,1,0:T(8,128)S(1)} %constant_dynamic-update-slice_fusion.own_ref), channel_id=1, source_target_pairs={{0,96},{32,0},{64,32},{96,64},{1,97},{33,1},{65,33},{97,65},{2,98}... | collective-permute-start | bytes 3080 | tf_op jit(solution)/shard_map/ppermute | solution.py:179
  17.4 1.0 %prepare.1 = (bf16[128,64]{1,0:T(8,128)(2,1)S(1)}, bf16[128,256]{1,0:T(8,128)(2,1)S(1)}) custom-call(bf16[64,128]{1,0:T(8,128)(2,1)} %theta_hbm.1, bf16[128,256]{1,0:T(8,128)(2,1)} %phi_hbm.1), custom_call_target="tpu_custom_call" | custom-call | flops 1048576 | bytes 262144 | tf_op jit(solution)/shard_map/prepare/pallas_call | solution.py:275
  18.3 0.0 collective-permute-done.3.far_ref
  18.3 0.3 collective-permute-done.2.before_ref
  18.7 0.0 collective-permute-done.1.after_ref
  18.7 0.8 %all-to-all-done.x_ref = bf16[16,16,2,4,128]{4,3,2,1,0:T(4,128)(2,1)S(1)} async-done(((bf16[16,16,2,4,128]{4,3,2,1,0:T(4,128)(2,1)}), bf16[16,16,2,4,128]{4,3,2,1,0:T(4,128)(2,1)S(1)}, u32[]{:S(2)}, u32[]{:S(2)}) %all-to-all-start) | async-done | bytes 524320 | tf_op jit(solution)/shard_map/all_to_all | solution.py:272
  19.4 1.9 %aggregate.1 = bf16[16,2,2,8,256]{4,3,2,1,0:T(8,128)(2,1)} custom-call(bf16[16,16,2,4,128]{4,3,2,1,0:T(4,128)(2,1)S(1)} %all-to-all-done.x_ref, bf16[128,64]{1,0:T(8,128)(2,1)S(1)} %get-tuple-element.43.theta_ref, bf16[128,256]{1,0:T(8,128)(2,1)S(1)} %get-tuple-element.44.phi_ref, f32[4,128,256]{2,1,0:T(8,128)S(1)} %get-tuple-element.79.cos_ref, ...), custom_call_target="tpu_custom_call" | custom-call | flops 351272960 | bytes 4194304 | tf_op jit(solution)/shard_map/aggregate/pallas_call | solution.py:295
  21.4 5.9 %all-to-all-start.1 = ((bf16[16,2,2,8,256]{4,3,2,1,0:T(8,128)(2,1)}), bf16[16,2,2,8,256]{4,3,2,1,0:T(8,128)(2,1)S(1)}, u32[]{:S(2)}, u32[]{:S(2)}) async-start(bf16[16,2,2,8,256]{4,3,2,1,0:T(8,128)(2,1)} %aggregate.1), calls=%async_computation.1 | async-start | bytes 524288 | tf_op jit(solution)/shard_map/all_to_all | solution.py:309
  27.3 1.5 %collective-permute-start.4 = (bf16[16,2,2,8,256]{4,3,2,1,0:T(8,128)(2,1)}, bf16[16,2,2,8,256]{4,3,2,1,0:T(8,128)(2,1)S(1)}, u32[]{:S(2)}, u32[]{:S(2)}) collective-permute-start(bf16[16,2,2,8,256]{4,3,2,1,0:T(8,128)(2,1)} %aggregate.1), channel_id=1, source_target_pairs={{0,64},{32,96},{64,0},{96,32},{1,65},{33,97},{65,1},{97,33},{2,66}... | collective-permute-start | bytes 786440 | tf_op jit(solution)/shard_map/ppermute | solution.py:179
  28.8 1.7 %stage.1.x_ref = bf16[316,2,8,256]{3,2,1,0:T(8,128)(2,1)S(1)} custom-call(bf16[316,2,8,256]{3,2,1,0:T(8,128)(2,1)} %x_ref), custom_call_target="tpu_custom_call" | custom-call | flops 1 | bytes 5242880 | tf_op jit(solution)/shard_map/stage/pallas_call | solution.py:311
  30.5 2.0 %plan.1.list_ref = s32[64,128]{1,0:T(8,128)S(4)} custom-call(s32[32,128]{1,0:T(8,128)S(1)} %broadcast_in_dim.2.me_ref, s32[2,8,16]{2,1,0:T(8,128)S(1)} %constant_dynamic-update-slice_fusion.own_ref, s32[2,8,16]{2,1,0:T(8,128)S(1)} %collective-permute-done.1.after_ref, s32[2,8,16]{2,1,0:T(8,128)S(1)} %collective-permute-done.2.before_ref, ...), custom_call_target="tpu_custom_call" | custom-call | flops 1048576 | bytes 1048576 | tf_op jit(solution)/shard_map/plan/pallas_call | solution.py:249
  32.6 2.0 %all-to-all-done.1 = bf16[16,2,2,8,256]{4,3,2,1,0:T(8,128)(2,1)S(1)} async-done(((bf16[16,2,2,8,256]{4,3,2,1,0:T(8,128)(2,1)}), bf16[16,2,2,8,256]{4,3,2,1,0:T(8,128)(2,1)S(1)}, u32[]{:S(2)}, u32[]{:S(2)}) %all-to-all-start.1) | async-done | bytes 262176 | tf_op jit(solution)/shard_map/all_to_all | solution.py:309
  34.6 2.9 %collective-permute-start.5 = (bf16[32,2,8,256]{3,2,1,0:T(8,128)(2,1)S(1)}, bf16[32,2,8,256]{3,2,1,0:T(8,128)(2,1)S(1)}, u32[]{:S(2)}, u32[]{:S(2)}) collective-permute-start(bf16[32,2,8,256]{3,2,1,0:T(8,128)(2,1)S(1)} %bitcast.3), channel_id=1, source_target_pairs={{0,16},{16,0},{1,17},{17,1},{2,18},{18,2},{3,19},{19,3},{4,20},{20... | collective-permute-start | bytes 786440 | tf_op jit(solution)/shard_map/ppermute | solution.py:179
  37.5 0.0 collective-permute-start.7
  37.5 2.9 %collective-permute-start.6 = (bf16[32,2,8,256]{3,2,1,0:T(8,128)(2,1)S(1)}, bf16[32,2,8,256]{3,2,1,0:T(8,128)(2,1)}, u32[]{:S(2)}, u32[]{:S(2)}) collective-permute-start(bf16[32,2,8,256]{3,2,1,0:T(8,128)(2,1)S(1)} %bitcast.5), channel_id=1, source_target_pairs={{0,96},{32,0},{64,32},{96,64},{1,97},{33,1},{65,33},{97,65},{2,98}... | collective-permute-start | bytes 786440 | tf_op jit(solution)/shard_map/ppermute | solution.py:179
  40.5 0.0 collective-permute-done.4
  40.5 0.5 shard_map.86.trans_ref
  41.0 0.2 copy-done.8
  41.2 0.0 collective-permute-done.5.refs_1_
  41.2 1.3 %shard_map.87 = (f32[32,2,8,256]{3,2,1,0:T(8,128)S(1)}, f32[193,2,8,256]{3,2,1,0:T(8,128)S(1)}, bf16[32,2,8,256]{3,2,1,0:T(8,128)(2,1)}) custom-call(s32[64,128]{1,0:T(8,128)S(4)} %plan.1.list_ref, f32[316,2,8,256]{3,2,1,0:T(8,128)S(1)} %shard_map.86.trans_ref, bf16[32,2,8,256]{3,2,1,0:T(8,128)(2,1)S(1)} %bitcast.6, ...), custom_call_target="tpu_custom_call" | custom-call | flops 16777216 | bytes 8388608 | tf_op jit(solution)/shard_map/pallas_call | solution.py:364
  42.4 2.3 %copy-done = f32[316,2,8,256]{3,2,1,0:T(8,128)} copy-done((f32[316,2,8,256]{3,2,1,0:T(8,128)}, f32[316,2,8,256]{3,2,1,0:T(8,128)S(1)}, u32[]{:S(2)}) %copy-start) | copy-done | bytes 5177368
  44.7 1.7 %copy-done.2 = f32[193,2,8,256]{3,2,1,0:T(8,128)} copy-done((f32[193,2,8,256]{3,2,1,0:T(8,128)}, f32[193,2,8,256]{3,2,1,0:T(8,128)S(1)}, u32[]{:S(2)}) %copy-start.2) | copy-done | bytes 3162136
  46.4 0.8 %collective-permute-done.7.refs_2_ = bf16[32,2,8,256]{3,2,1,0:T(8,128)(2,1)} collective-permute-done((bf16[32,2,8,256]{3,2,1,0:T(8,128)(2,1)S(1)}, bf16[32,2,8,256]{3,2,1,0:T(8,128)(2,1)}, u32[]{:S(2)}, u32[]{:S(2)}) %collective-permute-start.7) | collective-permute-done | bytes 262176 | tf_op jit(solution)/shard_map/ppermute | solution.py:179
  47.2 0.6 collective-permute-start.8
  47.8 0.0 collective-permute-start.9
  47.8 4.7 %all-to-all-start.2 = ((bf16[16,2,2,8,256]{4,3,2,1,0:T(8,128)(2,1)}), bf16[16,2,2,8,256]{4,3,2,1,0:T(8,128)(2,1)S(1)}, u32[]{:S(2)}, u32[]{:S(2)}) async-start(bf16[16,2,2,8,256]{4,3,2,1,0:T(8,128)(2,1)} %copy-done.8), calls=%async_computation.2 | async-start | bytes 524288 | tf_op jit(solution)/shard_map/all_to_all | solution.py:328
  52.5 2.5 %copy-done.1 = f32[316,2,8,256]{3,2,1,0:T(8,128)S(1)} copy-done((f32[316,2,8,256]{3,2,1,0:T(8,128)S(1)}, f32[316,2,8,256]{3,2,1,0:T(8,128)}, u32[]{:S(2)}) %copy-start.1) | copy-done | bytes 5177368
  55.0 1.9 %copy-done.3 = f32[193,2,8,256]{3,2,1,0:T(8,128)S(1)} copy-done((f32[193,2,8,256]{3,2,1,0:T(8,128)S(1)}, f32[193,2,8,256]{3,2,1,0:T(8,128)}, u32[]{:S(2)}) %copy-start.3) | copy-done | bytes 3162136
  56.9 2.9 %shard_map.88 = (f32[32,2,8,256]{3,2,1,0:T(8,128)S(1)}, f32[193,2,8,256]{3,2,1,0:T(8,128)S(1)}) custom-call(s32[64,128]{1,0:T(8,128)S(4)} %plan.1.list_ref, f32[316,2,8,256]{3,2,1,0:T(8,128)S(1)} %copy-done.1, f32[32,2,8,256]{3,2,1,0:T(8,128)S(1)} %get-tuple-element.65.refs_0_, ...), custom_call_target="tpu_custom_call", output_to_operand_aliasing={{1}: (5, {})} | custom-call | flops 16777216 | bytes 8388608 | tf_op jit(solution)/shard_map/pallas_call | solution.py:364
  59.8 1.6 %copy-done.4 = f32[193,2,8,256]{3,2,1,0:T(8,128)} copy-done((f32[193,2,8,256]{3,2,1,0:T(8,128)}, f32[193,2,8,256]{3,2,1,0:T(8,128)S(1)}, u32[]{:S(2)}) %copy-start.4) | copy-done | bytes 3162136
  61.4 0.0 collective-permute-done.8.refs_1_
  61.4 0.0 collective-permute-done.9.refs_2_
  61.4 1.9 %copy-done.5 = f32[193,2,8,256]{3,2,1,0:T(8,128)S(1)} copy-done((f32[193,2,8,256]{3,2,1,0:T(8,128)S(1)}, f32[193,2,8,256]{3,2,1,0:T(8,128)}, u32[]{:S(2)}) %copy-start.5) | copy-done | bytes 3162136
  63.3 4.7 %shard_map.89 = (f32[32,2,8,256]{3,2,1,0:T(8,128)S(1)}, f32[193,2,8,256]{3,2,1,0:T(8,128)S(1)}) custom-call(s32[64,128]{1,0:T(8,128)S(4)} %plan.1.list_ref, f32[316,2,8,256]{3,2,1,0:T(8,128)S(1)} %copy-done.1, f32[32,2,8,256]{3,2,1,0:T(8,128)S(1)} %get-tuple-element.69.refs_0_, ...), custom_call_target="tpu_custom_call", output_to_operand_aliasing={{1}: (5, {})} | custom-call | flops 16777216 | bytes 8388608 | tf_op jit(solution)/shard_map/pallas_call | solution.py:364
  68.0 0.0 all-to-all-done.2
  68.0 0.2 collective-permute-start.10
  68.2 0.5 shard_map.90.trans_ref
  68.8 1.4 %shard_map.91 = (f32[32,2,8,256]{3,2,1,0:T(8,128)S(1)}, f32[65,2,8,256]{3,2,1,0:T(8,128)S(1)}) custom-call(s32[64,128]{1,0:T(8,128)S(4)} %plan.1.list_ref, f32[316,2,8,256]{3,2,1,0:T(8,128)S(1)} %shard_map.90.trans_ref, f32[32,2,8,256]{3,2,1,0:T(8,128)S(1)} %get-tuple-element.73.refs_0_, bf16[32,2,8,256]{3,2,1,0:T(8,128)(2,1)S(1)} %bitcast.8), custom_call_target="tpu_custom_call" | custom-call | flops 16777216 | bytes 8388608 | tf_op jit(solution)/shard_map/pallas_call | solution.py:364
  70.2 0.0 collective-permute-done.10.refs_1_
  70.2 2.0 %shard_map.92 = (f32[32,2,8,256]{3,2,1,0:T(8,128)}, f32[65,2,8,256]{3,2,1,0:T(8,128)S(1)}) custom-call(s32[64,128]{1,0:T(8,128)S(4)} %plan.1.list_ref, f32[316,2,8,256]{3,2,1,0:T(8,128)S(1)} %shard_map.90.trans_ref, f32[32,2,8,256]{3,2,1,0:T(8,128)S(1)} %get-tuple-element.75.refs_0_, ...), custom_call_target="tpu_custom_call", output_to_operand_aliasing={{1}: (4, {})} | custom-call | flops 16777216 | bytes 8388608 | tf_op jit(solution)/shard_map/pallas_call | solution.py:364
  (21 shorter events, 0.1 us)
Async XLA Ops:
  0.6 11.0 %copy-start.9 = (s32[1,8,16]{2,1,0:T(8,128)S(1)}, s32[1,8,16]{2,1,0:T(8,128)}, u32[]{:S(2)}) copy-start(s32[1,8,16]{2,1,0:T(8,128)} %param.11) | copy-start | bytes 1540
  0.6 18.8 %all-to-all-start = ((bf16[16,16,2,4,128]{4,3,2,1,0:T(4,128)(2,1)}), bf16[16,16,2,4,128]{4,3,2,1,0:T(4,128)(2,1)S(1)}, u32[]{:S(2)}, u32[]{:S(2)}) async-start(bf16[16,16,2,4,128]{4,3,2,1,0:T(4,128)(2,1)} %bitcast.9), calls=%async_computation | async-start | bytes 1048576 | tf_op jit(solution)/shard_map/all_to_all | solution.py:272
  9.1 2.6 %collective-permute-start = (s32[1,8,16]{2,1,0:T(8,128)}, s32[1,8,16]{2,1,0:T(8,128)S(1)}, u32[]{:S(2)}, u32[]{:S(2)}) collective-permute-start(s32[1,8,16]{2,1,0:T(8,128)} %param.11), channel_id=1, source_target_pairs={{0,16},{16,0},{1,17},{17,1},{2,18},{18,2},{3,19},{19,3},{4,20},{20... | collective-permute-start | bytes 1544 | tf_op jit(solution)/shard_map/ppermute | solution.py:179
  11.7 6.7 %collective-permute-start.3 = (s32[2,8,16]{2,1,0:T(8,128)S(1)}, s32[2,8,16]{2,1,0:T(8,128)S(1)}, u32[]{:S(2)}, u32[]{:S(2)}) collective-permute-start(s32[2,8,16]{2,1,0:T(8,128)S(1)} %constant_dynamic-update-slice_fusion.own_ref), channel_id=1, source_target_pairs={{0,64},{32,96},{64,0},{96,32},{1,65},{33,97},{65,1},{97,33},{2,66}... | collective-permute-start | bytes 3080 | tf_op jit(solution)/shard_map/ppermute | solution.py:179
  14.7 4.0 %collective-permute-start.2 = (s32[2,8,16]{2,1,0:T(8,128)S(1)}, s32[2,8,16]{2,1,0:T(8,128)S(1)}, u32[]{:S(2)}, u32[]{:S(2)}) collective-permute-start(s32[2,8,16]{2,1,0:T(8,128)S(1)} %constant_dynamic-update-slice_fusion.own_ref), channel_id=1, source_target_pairs={{0,32},{32,64},{64,96},{96,0},{1,33},{33,65},{65,97},{97,1},{2,34}... | collective-permute-start | bytes 3080 | tf_op jit(solution)/shard_map/ppermute | solution.py:179
  15.1 3.6 %collective-permute-start.1 = (s32[2,8,16]{2,1,0:T(8,128)S(1)}, s32[2,8,16]{2,1,0:T(8,128)S(1)}, u32[]{:S(2)}, u32[]{:S(2)}) collective-permute-start(s32[2,8,16]{2,1,0:T(8,128)S(1)} %constant_dynamic-update-slice_fusion.own_ref), channel_id=1, source_target_pairs={{0,96},{32,0},{64,32},{96,64},{1,97},{33,1},{65,33},{97,65},{2,98}... | collective-permute-start | bytes 3080 | tf_op jit(solution)/shard_map/ppermute | solution.py:179
  21.3 9.2 %copy-start.6 = (s32[32,64]{1,0:T(8,128)S(1)}, s32[32,64]{1,0:T(8,128)}, u32[]{:S(2)}) copy-start(s32[32,64]{1,0:T(8,128)} %slots_ref.1) | copy-start | bytes 24580
  21.4 9.2 %copy-start.7 = (s32[32,64]{1,0:T(8,128)S(1)}, s32[32,64]{1,0:T(8,128)}, u32[]{:S(2)}) copy-start(s32[32,64]{1,0:T(8,128)} %kinds_ref.1) | copy-start | bytes 24580
  21.4 13.3 %all-to-all-start.1 = ((bf16[16,2,2,8,256]{4,3,2,1,0:T(8,128)(2,1)}), bf16[16,2,2,8,256]{4,3,2,1,0:T(8,128)(2,1)S(1)}, u32[]{:S(2)}, u32[]{:S(2)}) async-start(bf16[16,2,2,8,256]{4,3,2,1,0:T(8,128)(2,1)} %aggregate.1), calls=%async_computation.1 | async-start | bytes 524288 | tf_op jit(solution)/shard_map/all_to_all | solution.py:309
  27.3 13.2 %collective-permute-start.4 = (bf16[16,2,2,8,256]{4,3,2,1,0:T(8,128)(2,1)}, bf16[16,2,2,8,256]{4,3,2,1,0:T(8,128)(2,1)S(1)}, u32[]{:S(2)}, u32[]{:S(2)}) collective-permute-start(bf16[16,2,2,8,256]{4,3,2,1,0:T(8,128)(2,1)} %aggregate.1), channel_id=1, source_target_pairs={{0,64},{32,96},{64,0},{96,32},{1,65},{33,97},{65,1},{97,33},{2,66}... | collective-permute-start | bytes 786440 | tf_op jit(solution)/shard_map/ppermute | solution.py:179
  34.6 6.5 %collective-permute-start.5 = (bf16[32,2,8,256]{3,2,1,0:T(8,128)(2,1)S(1)}, bf16[32,2,8,256]{3,2,1,0:T(8,128)(2,1)S(1)}, u32[]{:S(2)}, u32[]{:S(2)}) collective-permute-start(bf16[32,2,8,256]{3,2,1,0:T(8,128)(2,1)S(1)} %bitcast.3), channel_id=1, source_target_pairs={{0,16},{16,0},{1,17},{17,1},{2,18},{18,2},{3,19},{19,3},{4,20},{20... | collective-permute-start | bytes 786440 | tf_op jit(solution)/shard_map/ppermute | solution.py:179
  37.5 9.7 %collective-permute-start.7 = (bf16[32,2,8,256]{3,2,1,0:T(8,128)(2,1)S(1)}, bf16[32,2,8,256]{3,2,1,0:T(8,128)(2,1)}, u32[]{:S(2)}, u32[]{:S(2)}) collective-permute-start(bf16[32,2,8,256]{3,2,1,0:T(8,128)(2,1)S(1)} %bitcast.4), channel_id=1, source_target_pairs={{0,32},{32,64},{64,96},{96,0},{1,33},{33,65},{65,97},{97,1},{2,34}... | collective-permute-start | bytes 786440 | tf_op jit(solution)/shard_map/ppermute | solution.py:179
  37.5 9.7 %collective-permute-start.6 = (bf16[32,2,8,256]{3,2,1,0:T(8,128)(2,1)S(1)}, bf16[32,2,8,256]{3,2,1,0:T(8,128)(2,1)}, u32[]{:S(2)}, u32[]{:S(2)}) collective-permute-start(bf16[32,2,8,256]{3,2,1,0:T(8,128)(2,1)S(1)} %bitcast.5), channel_id=1, source_target_pairs={{0,96},{32,0},{64,32},{96,64},{1,97},{33,1},{65,33},{97,65},{2,98}... | collective-permute-start | bytes 786440 | tf_op jit(solution)/shard_map/ppermute | solution.py:179
  40.5 0.7 copy-start.8
  42.4 2.3 %copy-start = (f32[316,2,8,256]{3,2,1,0:T(8,128)}, f32[316,2,8,256]{3,2,1,0:T(8,128)S(1)}, u32[]{:S(2)}) copy-start(f32[316,2,8,256]{3,2,1,0:T(8,128)S(1)} %shard_map.86.trans_ref) | copy-start | bytes 15532036
  44.7 1.7 %copy-start.2 = (f32[193,2,8,256]{3,2,1,0:T(8,128)}, f32[193,2,8,256]{3,2,1,0:T(8,128)S(1)}, u32[]{:S(2)}) copy-start(f32[193,2,8,256]{3,2,1,0:T(8,128)S(1)} %get-tuple-element.68.refs_3_) | copy-start | bytes 9486340
  47.2 14.2 %collective-permute-start.8 = (bf16[32,2,8,256]{3,2,1,0:T(8,128)(2,1)}, bf16[32,2,8,256]{3,2,1,0:T(8,128)(2,1)}, u32[]{:S(2)}, u32[]{:S(2)}) collective-permute-start(bf16[32,2,8,256]{3,2,1,0:T(8,128)(2,1)} %collective-permute-done.6.refs_1_), channel_id=1, source_target_pairs={{0,16},{16,0},{1,17},{17,1},{2,18},{18,2},{3,19},{19,3},{4,20},{20... | collective-permute-start | bytes 786440 | tf_op jit(solution)/shard_map/ppermute | solution.py:179
  47.8 13.6 %collective-permute-start.9 = (bf16[32,2,8,256]{3,2,1,0:T(8,128)(2,1)}, bf16[32,2,8,256]{3,2,1,0:T(8,128)(2,1)}, u32[]{:S(2)}, u32[]{:S(2)}) collective-permute-start(bf16[32,2,8,256]{3,2,1,0:T(8,128)(2,1)} %collective-permute-done.7.refs_2_), channel_id=1, source_target_pairs={{0,16},{16,0},{1,17},{17,1},{2,18},{18,2},{3,19},{19,3},{4,20},{20... | collective-permute-start | bytes 786440 | tf_op jit(solution)/shard_map/ppermute | solution.py:179
  47.8 20.2 %all-to-all-start.2 = ((bf16[16,2,2,8,256]{4,3,2,1,0:T(8,128)(2,1)}), bf16[16,2,2,8,256]{4,3,2,1,0:T(8,128)(2,1)S(1)}, u32[]{:S(2)}, u32[]{:S(2)}) async-start(bf16[16,2,2,8,256]{4,3,2,1,0:T(8,128)(2,1)} %copy-done.8), calls=%async_computation.2 | async-start | bytes 524288 | tf_op jit(solution)/shard_map/all_to_all | solution.py:328
  52.5 2.5 %copy-start.1 = (f32[316,2,8,256]{3,2,1,0:T(8,128)S(1)}, f32[316,2,8,256]{3,2,1,0:T(8,128)}, u32[]{:S(2)}) copy-start(f32[316,2,8,256]{3,2,1,0:T(8,128)} %copy-done) | copy-start | bytes 15532036
  55.0 1.9 %copy-start.3 = (f32[193,2,8,256]{3,2,1,0:T(8,128)S(1)}, f32[193,2,8,256]{3,2,1,0:T(8,128)}, u32[]{:S(2)}) copy-start(f32[193,2,8,256]{3,2,1,0:T(8,128)} %copy-done.2) | copy-start | bytes 9486340
  59.7 1.6 %copy-start.4 = (f32[193,2,8,256]{3,2,1,0:T(8,128)}, f32[193,2,8,256]{3,2,1,0:T(8,128)S(1)}, u32[]{:S(2)}) copy-start(f32[193,2,8,256]{3,2,1,0:T(8,128)S(1)} %get-tuple-element.70.refs_3_) | copy-start | bytes 9486340
  61.4 1.9 %copy-start.5 = (f32[193,2,8,256]{3,2,1,0:T(8,128)S(1)}, f32[193,2,8,256]{3,2,1,0:T(8,128)}, u32[]{:S(2)}) copy-start(f32[193,2,8,256]{3,2,1,0:T(8,128)} %copy-done.4) | copy-start | bytes 9486340
  68.0 2.2 %collective-permute-start.10 = (bf16[32,2,8,256]{3,2,1,0:T(8,128)(2,1)S(1)}, bf16[32,2,8,256]{3,2,1,0:T(8,128)(2,1)S(1)}, u32[]{:S(2)}, u32[]{:S(2)}) collective-permute-start(bf16[32,2,8,256]{3,2,1,0:T(8,128)(2,1)S(1)} %bitcast.7), channel_id=1, source_target_pairs={{0,16},{16,0},{1,17},{17,1},{2,18},{18,2},{3,19},{19,3},{4,20},{20... | collective-permute-start | bytes 786440 | tf_op jit(solution)/shard_map/ppermute | solution.py:179

commit v5 on v4

--- a/solution.py
+++ b/solution.py
@@ -15,7 +15,7 @@
 WIDTH = 128
 ROWS = (0, 2, 4, 0, 1)
 FAR = 3
-CUTS = (0, 14, 28, 46, 54, 64)
+CUTS = (0, 14, 22, 46, 54, 64)
 CHUNK = 16
 VMEM = pl.BlockSpec(memory_space=pltpu.VMEM)
 SMEM = pl.BlockSpec(memory_space=pltpu.SMEM)
@@ -112,18 +112,25 @@
         store.start()
     elif last:
         sum_ref, *blocks, _, final_ref, pool_ref, out_ref, sems = refs
+    elif k == 1:
+        sum_ref, *blocks, later, _, out_ref, pool_ref, later_ref, sem = refs
+        fetch = pltpu.make_async_copy(later, later_ref, sem)
+        fetch.start()
     elif k == FAR:
         sum_ref, *blocks, out_ref, pool_ref = refs
     else:
         sum_ref, *blocks, _, out_ref, pool_ref = refs
     boxes = out_ref.shape[0]
-    for i, block in enumerate(blocks):
-
-        def widen(n, carry, block=block, start=(ROWS[k] + i) * boxes):
+
+    def widen_block(block, start):
+        def widen(n, carry):
             pool_ref[start + n] = block[n].astype(jnp.float32)
             return carry
 
         lax.fori_loop(0, boxes, widen, 0, unroll=4)
+
+    for i, block in enumerate(blocks):
+        widen_block(block, (ROWS[k] + i) * boxes)
     if k in (0, FAR):
         pool_ref[pool_ref.shape[0] - 1] = jnp.zeros(pool_ref.shape[1:], jnp.float32)
 
@@ -172,6 +179,9 @@
             out.wait()
     if first:
         store.wait()
+    if k == 1:
+        fetch.wait()
+        widen_block(later_ref, (ROWS[k] + 1) * boxes)
 
 
 def shift(x, axis, step):
@@ -193,9 +203,9 @@
     pieces = []
     for table, block, step in (
         (own_ref, 0, 1),
-        (after_ref, 2, 2),
+        (after_ref, 3, 1),
         (far_ref, 0, 1),
-        (before_ref, 3, 2),
+        (before_ref, 2, 3),
     ):
         for core in range(cores):
             mine = jnp.sum(jnp.where(is_me, table[core], 0), axis=0, keepdims=True)
@@ -203,7 +213,8 @@
     table = jnp.broadcast_to(jnp.concatenate(pieces, axis=1), (boxes, WIDTH))
     row = jnp.take_along_axis(table, jnp.concatenate([code, code], axis=1), axis=1)
     row = row[:, :entries]
-    klass = jnp.where(dy == 0, 0, jnp.where(dy == 2, 3, 1) + dc)
+    klass = jnp.where((dy == 3) & (dc == 0), 1, 2)
+    klass = jnp.where(dy == 0, 0, jnp.where(dy == 2, 3 + dc, klass))
     first = lax.broadcasted_iota(jnp.int32, (entries, entries), 0)
     second = lax.broadcasted_iota(jnp.int32, (entries, entries), 1)
     ahead = (first < second).astype(jnp.float32)
@@ -359,12 +370,16 @@
         else:
             operands = [so_far[0], *blocks, so_far[1]]
             aliases = {1 + len(operands): 1}
+        kinds = [VMEM] * len(operands)
+        if k == 1:
+            kinds[-2] = HBM
+            scratch = [pltpu.VMEM(shape, jnp.bfloat16), pltpu.SemaphoreType.DMA]
         if last:
             scratch = [pltpu.VMEM(shape, jnp.float32), pltpu.SemaphoreType.DMA((4,))]
         return pl.pallas_call(
             functools.partial(class_kernel, k),
             out_shape=out,
-            in_specs=[SMEM] + [VMEM] * (1 + len(operands)),
+            in_specs=[SMEM, VMEM] + kinds,
             out_specs=out_specs,
             scratch_shapes=scratch,
             input_output_aliases=aliases,
@@ -375,7 +390,7 @@
     *state, parents = translate(0, wide, [own, other], None)
     after, before, *state = lax.optimization_barrier((after, before, *state))
     across = [shift(after, "c", 1), shift(before, "c", 1)]
-    state = translate(1, wide, [after, before], state)
+    state = translate(1, wide, [before, after], state)
     state = translate(2, wide, across, state)
     far, staged, *state = lax.optimization_barrier((far, staged, *state))
     across = shift(far, "c", 1)

time: 72.8 us -> 73 us (level)
  no operation moved by 1% of the time
where the time goes in v5:
time: 73 us; the launch traced here: 72.3 us
  starting transfers between devices  34.2 us (47%)
  Pallas kernels  19.8 us (27%)
  local copies, waits for them, and re-layouts  12.1 us (17%)
  waiting for transfers between devices  3.91 us (5%)
  other arithmetic  1.49 us (2%)
  between operations  0.88 us (1%)
    ppermute x11, starting transfers between devices, shift(): return lax.ppermute(x, axis, [(i, (i + step) % size) for i in range(size)])  15.1 us
    unnamed x21, local copies, waits for them, and re-layouts  12.1 us
    pallas_call x5, Pallas kernels, translate(): pl.pallas_call(functools.partial(class_kernel, k), out_shape=out, in_spec...  12 us
    all_to_all x1, starting transfers between devices, local(): x = lax.all_to_all(x, SAMP, split_axis=0, concat_axis=0, tiled=True)  8.43 us
    all_to_all x1, starting transfers between devices, local(): mine = lax.all_to_all(whole, SAMP, split_axis=0, concat_axis=0, tiled=True)  5.94 us
    all_to_all x1, starting transfers between devices, local(): lax.all_to_all(far_whole, SAMP, split_axis=0, concat_axis=0, tiled=True)  4.7 us
    pallas_call x1, Pallas kernels, plan_lists(): pl.pallas_call(plan_kernel, out_shape=pltpu.SMEM((2 * boxes, WIDTH), jnp....  2.05 us
    all_to_all x1, waiting for transfers between devices, local(): mine = lax.all_to_all(whole, SAMP, split_axis=0, concat_axis=0, tiled=True)  2.02 us
  transfers between devices with their start and end apart: 14, of which 4 were waited for; matrix products, arithmetic and copies ran while one was open for 2% of the time, Pallas kernels for 22%

profile of v5, /device:TPU:1, one launch (start us, length us, event | category | flops | bytes accessed | tf_op | source)
XLA Modules:
  0.0 72.3 jit_solution(10578373607535153863)
XLA Ops:
  0.6 8.4 %all-to-all-start = ((bf16[16,16,2,4,128]{4,3,2,1,0:T(4,128)(2,1)}), bf16[16,16,2,4,128]{4,3,2,1,0:T(4,128)(2,1)S(1)}, u32[]{:S(2)}, u32[]{:S(2)}) async-start(bf16[16,16,2,4,128]{4,3,2,1,0:T(4,128)(2,1)} %bitcast.9), calls=%async_computation | async-start | bytes 1048576 | tf_op jit(solution)/shard_map/all_to_all | solution.py:283
  9.1 1.0 %collective-permute-start = (s32[1,8,16]{2,1,0:T(8,128)}, s32[1,8,16]{2,1,0:T(8,128)S(1)}, u32[]{:S(2)}, u32[]{:S(2)}) collective-permute-start(s32[1,8,16]{2,1,0:T(8,128)} %param.11), channel_id=1, source_target_pairs={{0,16},{16,0},{1,17},{17,1},{2,18},{18,2},{3,19},{19,3},{4,20},{20... | collective-permute-start | bytes 1544 | tf_op jit(solution)/shard_map/ppermute | solution.py:189
  10.2 0.1 sine_negate_fusion
  10.3 1.0 %multiply_sine_fusion = (f32[128,256]{1,0:T(8,128)S(1)}, f32[128,256]{1,0:T(8,128)S(1)}, f32[128,256]{1,0:T(8,128)S(1)}, f32[128,256]{1,0:T(8,128)S(1)}) fusion(f32[256]{0:T(256)S(1)} %get-tuple-element.86, f32[128]{0:T(128)S(1)} %sine_multiply_fusion, f32[256]{0:T(256)S(1)} %get-tuple-element.87), kind=kLoop, calls=%fused_computation.11 | loop fusion | flops 65536 | bytes 526848 | tf_op jit(solution)/shard_map/sin | solution.py:35
  11.3 0.3 fusion.5
  11.7 0.0 collective-permute-done
  11.7 3.0 %collective-permute-start.3 = (s32[2,8,16]{2,1,0:T(8,128)S(1)}, s32[2,8,16]{2,1,0:T(8,128)S(1)}, u32[]{:S(2)}, u32[]{:S(2)}) collective-permute-start(s32[2,8,16]{2,1,0:T(8,128)S(1)} %constant_dynamic-update-slice_fusion.own_ref), channel_id=1, source_target_pairs={{0,64},{32,96},{64,0},{96,32},{1,65},{33,97},{65,1},{97,33},{2,66}... | collective-permute-start | bytes 3080 | tf_op jit(solution)/shard_map/ppermute | solution.py:189
  14.7 0.4 collective-permute-start.2
  15.1 2.3 %collective-permute-start.1 = (s32[2,8,16]{2,1,0:T(8,128)S(1)}, s32[2,8,16]{2,1,0:T(8,128)S(1)}, u32[]{:S(2)}, u32[]{:S(2)}) collective-permute-start(s32[2,8,16]{2,1,0:T(8,128)S(1)} %constant_dynamic-update-slice_fusion.own_ref), channel_id=1, source_target_pairs={{0,96},{32,0},{64,32},{96,64},{1,97},{33,1},{65,33},{97,65},{2,98}... | collective-permute-start | bytes 3080 | tf_op jit(solution)/shard_map/ppermute | solution.py:189
  17.4 1.0 %prepare.1 = (bf16[128,64]{1,0:T(8,128)(2,1)S(1)}, bf16[128,256]{1,0:T(8,128)(2,1)S(1)}) custom-call(bf16[64,128]{1,0:T(8,128)(2,1)} %theta_hbm.1, bf16[128,256]{1,0:T(8,128)(2,1)} %phi_hbm.1), custom_call_target="tpu_custom_call" | custom-call | flops 1048576 | bytes 262144 | tf_op jit(solution)/shard_map/prepare/pallas_call | solution.py:286
  18.3 0.0 collective-permute-done.3.far_ref
  18.3 0.3 collective-permute-done.2.before_ref
  18.7 0.0 collective-permute-done.1.after_ref
  18.7 0.8 %all-to-all-done.x_ref = bf16[16,16,2,4,128]{4,3,2,1,0:T(4,128)(2,1)S(1)} async-done(((bf16[16,16,2,4,128]{4,3,2,1,0:T(4,128)(2,1)}), bf16[16,16,2,4,128]{4,3,2,1,0:T(4,128)(2,1)S(1)}, u32[]{:S(2)}, u32[]{:S(2)}) %all-to-all-start) | async-done | bytes 524320 | tf_op jit(solution)/shard_map/all_to_all | solution.py:283
  19.4 1.9 %aggregate.1 = bf16[16,2,2,8,256]{4,3,2,1,0:T(8,128)(2,1)} custom-call(bf16[16,16,2,4,128]{4,3,2,1,0:T(4,128)(2,1)S(1)} %all-to-all-done.x_ref, bf16[128,64]{1,0:T(8,128)(2,1)S(1)} %get-tuple-element.43.theta_ref, bf16[128,256]{1,0:T(8,128)(2,1)S(1)} %get-tuple-element.44.phi_ref, f32[4,128,256]{2,1,0:T(8,128)S(1)} %get-tuple-element.79.cos_ref, ...), custom_call_target="tpu_custom_call" | custom-call | flops 351272960 | bytes 4194304 | tf_op jit(solution)/shard_map/aggregate/pallas_call | solution.py:306
  21.4 5.9 %all-to-all-start.1 = ((bf16[16,2,2,8,256]{4,3,2,1,0:T(8,128)(2,1)}), bf16[16,2,2,8,256]{4,3,2,1,0:T(8,128)(2,1)S(1)}, u32[]{:S(2)}, u32[]{:S(2)}) async-start(bf16[16,2,2,8,256]{4,3,2,1,0:T(8,128)(2,1)} %aggregate.1), calls=%async_computation.1 | async-start | bytes 524288 | tf_op jit(solution)/shard_map/all_to_all | solution.py:320
  27.3 1.5 %collective-permute-start.4 = (bf16[16,2,2,8,256]{4,3,2,1,0:T(8,128)(2,1)}, bf16[16,2,2,8,256]{4,3,2,1,0:T(8,128)(2,1)S(1)}, u32[]{:S(2)}, u32[]{:S(2)}) collective-permute-start(bf16[16,2,2,8,256]{4,3,2,1,0:T(8,128)(2,1)} %aggregate.1), channel_id=1, source_target_pairs={{0,64},{32,96},{64,0},{96,32},{1,65},{33,97},{65,1},{97,33},{2,66}... | collective-permute-start | bytes 786440 | tf_op jit(solution)/shard_map/ppermute | solution.py:189
  28.8 1.7 %stage.1.x_ref = bf16[316,2,8,256]{3,2,1,0:T(8,128)(2,1)S(1)} custom-call(bf16[316,2,8,256]{3,2,1,0:T(8,128)(2,1)} %x_ref), custom_call_target="tpu_custom_call" | custom-call | flops 1 | bytes 5242880 | tf_op jit(solution)/shard_map/stage/pallas_call | solution.py:322
  30.5 2.0 %plan.1.list_ref = s32[64,128]{1,0:T(8,128)S(4)} custom-call(s32[32,128]{1,0:T(8,128)S(1)} %broadcast_in_dim.2.me_ref, s32[2,8,16]{2,1,0:T(8,128)S(1)} %constant_dynamic-update-slice_fusion.own_ref, s32[2,8,16]{2,1,0:T(8,128)S(1)} %collective-permute-done.1.after_ref, s32[2,8,16]{2,1,0:T(8,128)S(1)} %collective-permute-done.2.before_ref, ...), custom_call_target="tpu_custom_call" | custom-call | flops 1048576 | bytes 1048576 | tf_op jit(solution)/shard_map/plan/pallas_call | solution.py:260
  32.6 2.0 %all-to-all-done.1 = bf16[16,2,2,8,256]{4,3,2,1,0:T(8,128)(2,1)S(1)} async-done(((bf16[16,2,2,8,256]{4,3,2,1,0:T(8,128)(2,1)}), bf16[16,2,2,8,256]{4,3,2,1,0:T(8,128)(2,1)S(1)}, u32[]{:S(2)}, u32[]{:S(2)}) %all-to-all-start.1) | async-done | bytes 262176 | tf_op jit(solution)/shard_map/all_to_all | solution.py:320
  34.6 2.9 %collective-permute-start.5 = (bf16[32,2,8,256]{3,2,1,0:T(8,128)(2,1)S(1)}, bf16[32,2,8,256]{3,2,1,0:T(8,128)(2,1)S(1)}, u32[]{:S(2)}, u32[]{:S(2)}) collective-permute-start(bf16[32,2,8,256]{3,2,1,0:T(8,128)(2,1)S(1)} %bitcast.3), channel_id=1, source_target_pairs={{0,16},{16,0},{1,17},{17,1},{2,18},{18,2},{3,19},{19,3},{4,20},{20... | collective-permute-start | bytes 786440 | tf_op jit(solution)/shard_map/ppermute | solution.py:189
  37.5 0.0 collective-permute-start.7
  37.5 2.9 %collective-permute-start.6 = (bf16[32,2,8,256]{3,2,1,0:T(8,128)(2,1)S(1)}, bf16[32,2,8,256]{3,2,1,0:T(8,128)(2,1)}, u32[]{:S(2)}, u32[]{:S(2)}) collective-permute-start(bf16[32,2,8,256]{3,2,1,0:T(8,128)(2,1)S(1)} %bitcast.5), channel_id=1, source_target_pairs={{0,96},{32,0},{64,32},{96,64},{1,97},{33,1},{65,33},{97,65},{2,98}... | collective-permute-start | bytes 786440 | tf_op jit(solution)/shard_map/ppermute | solution.py:189
  40.5 0.0 collective-permute-done.4
  40.5 0.5 shard_map.86.trans_ref
  41.0 0.2 copy-done.8
  41.2 0.0 collective-permute-done.5.refs_1_
  41.2 1.3 %shard_map.87 = (f32[32,2,8,256]{3,2,1,0:T(8,128)S(1)}, f32[193,2,8,256]{3,2,1,0:T(8,128)S(1)}, bf16[32,2,8,256]{3,2,1,0:T(8,128)(2,1)}) custom-call(s32[64,128]{1,0:T(8,128)S(4)} %plan.1.list_ref, f32[316,2,8,256]{3,2,1,0:T(8,128)S(1)} %shard_map.86.trans_ref, bf16[32,2,8,256]{3,2,1,0:T(8,128)(2,1)S(1)} %bitcast.6, ...), custom_call_target="tpu_custom_call" | custom-call | flops 16777216 | bytes 8388608 | tf_op jit(solution)/shard_map/pallas_call | solution.py:379
  42.4 2.3 %copy-done = f32[316,2,8,256]{3,2,1,0:T(8,128)} copy-done((f32[316,2,8,256]{3,2,1,0:T(8,128)}, f32[316,2,8,256]{3,2,1,0:T(8,128)S(1)}, u32[]{:S(2)}) %copy-start) | copy-done | bytes 5177368
  44.7 1.7 %copy-done.2 = f32[193,2,8,256]{3,2,1,0:T(8,128)} copy-done((f32[193,2,8,256]{3,2,1,0:T(8,128)}, f32[193,2,8,256]{3,2,1,0:T(8,128)S(1)}, u32[]{:S(2)}) %copy-start.2) | copy-done | bytes 3162136
  46.4 0.8 %collective-permute-done.7.refs_1_ = bf16[32,2,8,256]{3,2,1,0:T(8,128)(2,1)} collective-permute-done((bf16[32,2,8,256]{3,2,1,0:T(8,128)(2,1)S(1)}, bf16[32,2,8,256]{3,2,1,0:T(8,128)(2,1)}, u32[]{:S(2)}, u32[]{:S(2)}) %collective-permute-start.7) | collective-permute-done | bytes 262176 | tf_op jit(solution)/shard_map/ppermute | solution.py:189
  47.2 0.0 collective-permute-done.6.refs_2_
  47.2 0.6 collective-permute-start.9
  47.8 0.0 collective-permute-start.8
  47.8 4.7 %all-to-all-start.2 = ((bf16[16,2,2,8,256]{4,3,2,1,0:T(8,128)(2,1)}), bf16[16,2,2,8,256]{4,3,2,1,0:T(8,128)(2,1)S(1)}, u32[]{:S(2)}, u32[]{:S(2)}) async-start(bf16[16,2,2,8,256]{4,3,2,1,0:T(8,128)(2,1)} %copy-done.8), calls=%async_computation.2 | async-start | bytes 524288 | tf_op jit(solution)/shard_map/all_to_all | solution.py:339
  52.5 2.5 %copy-done.1 = f32[316,2,8,256]{3,2,1,0:T(8,128)S(1)} copy-done((f32[316,2,8,256]{3,2,1,0:T(8,128)S(1)}, f32[316,2,8,256]{3,2,1,0:T(8,128)}, u32[]{:S(2)}) %copy-start.1) | copy-done | bytes 5177368
  55.0 1.9 %copy-done.3 = f32[193,2,8,256]{3,2,1,0:T(8,128)S(1)} copy-done((f32[193,2,8,256]{3,2,1,0:T(8,128)S(1)}, f32[193,2,8,256]{3,2,1,0:T(8,128)}, u32[]{:S(2)}) %copy-start.3) | copy-done | bytes 3162136
  56.9 2.4 %shard_map.88 = (f32[32,2,8,256]{3,2,1,0:T(8,128)S(1)}, f32[193,2,8,256]{3,2,1,0:T(8,128)S(1)}) custom-call(s32[64,128]{1,0:T(8,128)S(4)} %plan.1.list_ref, f32[316,2,8,256]{3,2,1,0:T(8,128)S(1)} %copy-done.1, f32[32,2,8,256]{3,2,1,0:T(8,128)S(1)} %get-tuple-element.65.refs_0_, ...), custom_call_target="tpu_custom_call", output_to_operand_aliasing={{1}: (5, {})} | custom-call | flops 16777216 | bytes 8388608 | tf_op jit(solution)/shard_map/pallas_call | solution.py:379
  59.3 1.6 %copy-done.4 = f32[193,2,8,256]{3,2,1,0:T(8,128)} copy-done((f32[193,2,8,256]{3,2,1,0:T(8,128)}, f32[193,2,8,256]{3,2,1,0:T(8,128)S(1)}, u32[]{:S(2)}) %copy-start.4) | copy-done | bytes 3162136
  60.9 0.0 collective-permute-done.9.refs_2_
  60.9 1.9 %copy-done.5 = f32[193,2,8,256]{3,2,1,0:T(8,128)S(1)} copy-done((f32[193,2,8,256]{3,2,1,0:T(8,128)S(1)}, f32[193,2,8,256]{3,2,1,0:T(8,128)}, u32[]{:S(2)}) %copy-start.5) | copy-done | bytes 3162136
  62.8 5.0 %shard_map.89 = (f32[32,2,8,256]{3,2,1,0:T(8,128)S(1)}, f32[193,2,8,256]{3,2,1,0:T(8,128)S(1)}) custom-call(s32[64,128]{1,0:T(8,128)S(4)} %plan.1.list_ref, f32[316,2,8,256]{3,2,1,0:T(8,128)S(1)} %copy-done.1, f32[32,2,8,256]{3,2,1,0:T(8,128)S(1)} %get-tuple-element.69.refs_0_, ...), custom_call_target="tpu_custom_call", output_to_operand_aliasing={{1}: (5, {})} | custom-call | flops 16777216 | bytes 8388608 | tf_op jit(solution)/shard_map/pallas_call | solution.py:379
  67.9 0.0 all-to-all-done.2
  67.9 0.5 collective-permute-start.10
  68.4 0.5 shard_map.90.trans_ref
  68.9 1.4 %shard_map.91 = (f32[32,2,8,256]{3,2,1,0:T(8,128)S(1)}, f32[65,2,8,256]{3,2,1,0:T(8,128)S(1)}) custom-call(s32[64,128]{1,0:T(8,128)S(4)} %plan.1.list_ref, f32[316,2,8,256]{3,2,1,0:T(8,128)S(1)} %shard_map.90.trans_ref, f32[32,2,8,256]{3,2,1,0:T(8,128)S(1)} %get-tuple-element.73.refs_0_, bf16[32,2,8,256]{3,2,1,0:T(8,128)(2,1)S(1)} %bitcast.8), custom_call_target="tpu_custom_call" | custom-call | flops 16777216 | bytes 8388608 | tf_op jit(solution)/shard_map/pallas_call | solution.py:379
  70.3 0.0 collective-permute-done.10.refs_1_
  70.3 2.0 %shard_map.92 = (f32[32,2,8,256]{3,2,1,0:T(8,128)}, f32[65,2,8,256]{3,2,1,0:T(8,128)S(1)}) custom-call(s32[64,128]{1,0:T(8,128)S(4)} %plan.1.list_ref, f32[316,2,8,256]{3,2,1,0:T(8,128)S(1)} %shard_map.90.trans_ref, f32[32,2,8,256]{3,2,1,0:T(8,128)S(1)} %get-tuple-element.75.refs_0_, ...), custom_call_target="tpu_custom_call", output_to_operand_aliasing={{1}: (4, {})} | custom-call | flops 16777216 | bytes 8388608 | tf_op jit(solution)/shard_map/pallas_call | solution.py:379
  (21 shorter events, 0.1 us)
Async XLA Ops:
  0.6 11.0 %copy-start.9 = (s32[1,8,16]{2,1,0:T(8,128)S(1)}, s32[1,8,16]{2,1,0:T(8,128)}, u32[]{:S(2)}) copy-start(s32[1,8,16]{2,1,0:T(8,128)} %param.11) | copy-start | bytes 1540
  0.6 18.8 %all-to-all-start = ((bf16[16,16,2,4,128]{4,3,2,1,0:T(4,128)(2,1)}), bf16[16,16,2,4,128]{4,3,2,1,0:T(4,128)(2,1)S(1)}, u32[]{:S(2)}, u32[]{:S(2)}) async-start(bf16[16,16,2,4,128]{4,3,2,1,0:T(4,128)(2,1)} %bitcast.9), calls=%async_computation | async-start | bytes 1048576 | tf_op jit(solution)/shard_map/all_to_all | solution.py:283
  9.1 2.6 %collective-permute-start = (s32[1,8,16]{2,1,0:T(8,128)}, s32[1,8,16]{2,1,0:T(8,128)S(1)}, u32[]{:S(2)}, u32[]{:S(2)}) collective-permute-start(s32[1,8,16]{2,1,0:T(8,128)} %param.11), channel_id=1, source_target_pairs={{0,16},{16,0},{1,17},{17,1},{2,18},{18,2},{3,19},{19,3},{4,20},{20... | collective-permute-start | bytes 1544 | tf_op jit(solution)/shard_map/ppermute | solution.py:189
  11.7 6.7 %collective-permute-start.3 = (s32[2,8,16]{2,1,0:T(8,128)S(1)}, s32[2,8,16]{2,1,0:T(8,128)S(1)}, u32[]{:S(2)}, u32[]{:S(2)}) collective-permute-start(s32[2,8,16]{2,1,0:T(8,128)S(1)} %constant_dynamic-update-slice_fusion.own_ref), channel_id=1, source_target_pairs={{0,64},{32,96},{64,0},{96,32},{1,65},{33,97},{65,1},{97,33},{2,66}... | collective-permute-start | bytes 3080 | tf_op jit(solution)/shard_map/ppermute | solution.py:189
  14.7 4.0 %collective-permute-start.2 = (s32[2,8,16]{2,1,0:T(8,128)S(1)}, s32[2,8,16]{2,1,0:T(8,128)S(1)}, u32[]{:S(2)}, u32[]{:S(2)}) collective-permute-start(s32[2,8,16]{2,1,0:T(8,128)S(1)} %constant_dynamic-update-slice_fusion.own_ref), channel_id=1, source_target_pairs={{0,32},{32,64},{64,96},{96,0},{1,33},{33,65},{65,97},{97,1},{2,34}... | collective-permute-start | bytes 3080 | tf_op jit(solution)/shard_map/ppermute | solution.py:189
  15.1 3.6 %collective-permute-start.1 = (s32[2,8,16]{2,1,0:T(8,128)S(1)}, s32[2,8,16]{2,1,0:T(8,128)S(1)}, u32[]{:S(2)}, u32[]{:S(2)}) collective-permute-start(s32[2,8,16]{2,1,0:T(8,128)S(1)} %constant_dynamic-update-slice_fusion.own_ref), channel_id=1, source_target_pairs={{0,96},{32,0},{64,32},{96,64},{1,97},{33,1},{65,33},{97,65},{2,98}... | collective-permute-start | bytes 3080 | tf_op jit(solution)/shard_map/ppermute | solution.py:189
  21.3 9.2 %copy-start.6 = (s32[32,64]{1,0:T(8,128)S(1)}, s32[32,64]{1,0:T(8,128)}, u32[]{:S(2)}) copy-start(s32[32,64]{1,0:T(8,128)} %slots_ref.1) | copy-start | bytes 24580
  21.4 9.2 %copy-start.7 = (s32[32,64]{1,0:T(8,128)S(1)}, s32[32,64]{1,0:T(8,128)}, u32[]{:S(2)}) copy-start(s32[32,64]{1,0:T(8,128)} %kinds_ref.1) | copy-start | bytes 24580
  21.4 13.3 %all-to-all-start.1 = ((bf16[16,2,2,8,256]{4,3,2,1,0:T(8,128)(2,1)}), bf16[16,2,2,8,256]{4,3,2,1,0:T(8,128)(2,1)S(1)}, u32[]{:S(2)}, u32[]{:S(2)}) async-start(bf16[16,2,2,8,256]{4,3,2,1,0:T(8,128)(2,1)} %aggregate.1), calls=%async_computation.1 | async-start | bytes 524288 | tf_op jit(solution)/shard_map/all_to_all | solution.py:320
  27.3 13.2 %collective-permute-start.4 = (bf16[16,2,2,8,256]{4,3,2,1,0:T(8,128)(2,1)}, bf16[16,2,2,8,256]{4,3,2,1,0:T(8,128)(2,1)S(1)}, u32[]{:S(2)}, u32[]{:S(2)}) collective-permute-start(bf16[16,2,2,8,256]{4,3,2,1,0:T(8,128)(2,1)} %aggregate.1), channel_id=1, source_target_pairs={{0,64},{32,96},{64,0},{96,32},{1,65},{33,97},{65,1},{97,33},{2,66}... | collective-permute-start | bytes 786440 | tf_op jit(solution)/shard_map/ppermute | solution.py:189
  34.6 6.5 %collective-permute-start.5 = (bf16[32,2,8,256]{3,2,1,0:T(8,128)(2,1)S(1)}, bf16[32,2,8,256]{3,2,1,0:T(8,128)(2,1)S(1)}, u32[]{:S(2)}, u32[]{:S(2)}) collective-permute-start(bf16[32,2,8,256]{3,2,1,0:T(8,128)(2,1)S(1)} %bitcast.3), channel_id=1, source_target_pairs={{0,16},{16,0},{1,17},{17,1},{2,18},{18,2},{3,19},{19,3},{4,20},{20... | collective-permute-start | bytes 786440 | tf_op jit(solution)/shard_map/ppermute | solution.py:189
  37.5 9.7 %collective-permute-start.7 = (bf16[32,2,8,256]{3,2,1,0:T(8,128)(2,1)S(1)}, bf16[32,2,8,256]{3,2,1,0:T(8,128)(2,1)}, u32[]{:S(2)}, u32[]{:S(2)}) collective-permute-start(bf16[32,2,8,256]{3,2,1,0:T(8,128)(2,1)S(1)} %bitcast.4), channel_id=1, source_target_pairs={{0,32},{32,64},{64,96},{96,0},{1,33},{33,65},{65,97},{97,1},{2,34}... | collective-permute-start | bytes 786440 | tf_op jit(solution)/shard_map/ppermute | solution.py:189
  37.5 9.7 %collective-permute-start.6 = (bf16[32,2,8,256]{3,2,1,0:T(8,128)(2,1)S(1)}, bf16[32,2,8,256]{3,2,1,0:T(8,128)(2,1)}, u32[]{:S(2)}, u32[]{:S(2)}) collective-permute-start(bf16[32,2,8,256]{3,2,1,0:T(8,128)(2,1)S(1)} %bitcast.5), channel_id=1, source_target_pairs={{0,96},{32,0},{64,32},{96,64},{1,97},{33,1},{65,33},{97,65},{2,98}... | collective-permute-start | bytes 786440 | tf_op jit(solution)/shard_map/ppermute | solution.py:189
  40.5 0.7 copy-start.8
  42.4 2.3 %copy-start = (f32[316,2,8,256]{3,2,1,0:T(8,128)}, f32[316,2,8,256]{3,2,1,0:T(8,128)S(1)}, u32[]{:S(2)}) copy-start(f32[316,2,8,256]{3,2,1,0:T(8,128)S(1)} %shard_map.86.trans_ref) | copy-start | bytes 15532036
  44.7 1.7 %copy-start.2 = (f32[193,2,8,256]{3,2,1,0:T(8,128)}, f32[193,2,8,256]{3,2,1,0:T(8,128)S(1)}, u32[]{:S(2)}) copy-start(f32[193,2,8,256]{3,2,1,0:T(8,128)S(1)} %get-tuple-element.68.refs_3_) | copy-start | bytes 9486340
  47.2 13.7 %collective-permute-start.9 = (bf16[32,2,8,256]{3,2,1,0:T(8,128)(2,1)}, bf16[32,2,8,256]{3,2,1,0:T(8,128)(2,1)}, u32[]{:S(2)}, u32[]{:S(2)}) collective-permute-start(bf16[32,2,8,256]{3,2,1,0:T(8,128)(2,1)} %collective-permute-done.7.refs_1_), channel_id=1, source_target_pairs={{0,16},{16,0},{1,17},{17,1},{2,18},{18,2},{3,19},{19,3},{4,20},{20... | collective-permute-start | bytes 786440 | tf_op jit(solution)/shard_map/ppermute | solution.py:189
  47.8 13.1 %collective-permute-start.8 = (bf16[32,2,8,256]{3,2,1,0:T(8,128)(2,1)}, bf16[32,2,8,256]{3,2,1,0:T(8,128)(2,1)}, u32[]{:S(2)}, u32[]{:S(2)}) collective-permute-start(bf16[32,2,8,256]{3,2,1,0:T(8,128)(2,1)} %collective-permute-done.6.refs_2_), channel_id=1, source_target_pairs={{0,16},{16,0},{1,17},{17,1},{2,18},{18,2},{3,19},{19,3},{4,20},{20... | collective-permute-start | bytes 786440 | tf_op jit(solution)/shard_map/ppermute | solution.py:189
  47.8 20.0 %all-to-all-start.2 = ((bf16[16,2,2,8,256]{4,3,2,1,0:T(8,128)(2,1)}), bf16[16,2,2,8,256]{4,3,2,1,0:T(8,128)(2,1)S(1)}, u32[]{:S(2)}, u32[]{:S(2)}) async-start(bf16[16,2,2,8,256]{4,3,2,1,0:T(8,128)(2,1)} %copy-done.8), calls=%async_computation.2 | async-start | bytes 524288 | tf_op jit(solution)/shard_map/all_to_all | solution.py:339
  52.5 2.5 %copy-start.1 = (f32[316,2,8,256]{3,2,1,0:T(8,128)S(1)}, f32[316,2,8,256]{3,2,1,0:T(8,128)}, u32[]{:S(2)}) copy-start(f32[316,2,8,256]{3,2,1,0:T(8,128)} %copy-done) | copy-start | bytes 15532036
  55.0 1.9 %copy-start.3 = (f32[193,2,8,256]{3,2,1,0:T(8,128)S(1)}, f32[193,2,8,256]{3,2,1,0:T(8,128)}, u32[]{:S(2)}) copy-start(f32[193,2,8,256]{3,2,1,0:T(8,128)} %copy-done.2) | copy-start | bytes 9486340
  59.3 1.6 %copy-start.4 = (f32[193,2,8,256]{3,2,1,0:T(8,128)}, f32[193,2,8,256]{3,2,1,0:T(8,128)S(1)}, u32[]{:S(2)}) copy-start(f32[193,2,8,256]{3,2,1,0:T(8,128)S(1)} %get-tuple-element.70.refs_3_) | copy-start | bytes 9486340
  60.9 1.9 %copy-start.5 = (f32[193,2,8,256]{3,2,1,0:T(8,128)S(1)}, f32[193,2,8,256]{3,2,1,0:T(8,128)}, u32[]{:S(2)}) copy-start(f32[193,2,8,256]{3,2,1,0:T(8,128)} %copy-done.4) | copy-start | bytes 9486340
  67.9 2.4 %collective-permute-start.10 = (bf16[32,2,8,256]{3,2,1,0:T(8,128)(2,1)S(1)}, bf16[32,2,8,256]{3,2,1,0:T(8,128)(2,1)S(1)}, u32[]{:S(2)}, u32[]{:S(2)}) collective-permute-start(bf16[32,2,8,256]{3,2,1,0:T(8,128)(2,1)S(1)} %bitcast.7), channel_id=1, source_target_pairs={{0,16},{16,0},{1,17},{17,1},{2,18},{18,2},{3,19},{19,3},{4,20},{20... | collective-permute-start | bytes 786440 | tf_op jit(solution)/shard_map/ppermute | solution.py:189

commit v6 on v5

--- a/solution.py
+++ b/solution.py
@@ -252,7 +252,7 @@
 
 def slot_tables(send_index):
     own = jnp.concatenate([send_index, shift(send_index, "c", 1)], axis=0)
-    return own, shift(own, "y", -1), shift(own, "y", 1), shift(own, "y", 2)
+    return own, shift(own, "y", -1), shift(own, "y", 1)
 
 
 def plan_lists(me, tables, list_slots, list_kinds):
@@ -318,6 +318,7 @@
     source, mine = lax.optimization_barrier((translator, mine))
     whole = mine
     mine = lax.all_to_all(whole, SAMP, split_axis=0, concat_axis=0, tiled=True)
+    far_table = shift(tables[0], "y", 2)
     far_whole = shift(whole, "y", 2)
     staged = pl.pallas_call(
         stage_kernel,
@@ -329,7 +330,7 @@
         cost_estimate=pl.CostEstimate(flops=1, bytes_accessed=5 << 20, transcendentals=0),
         name="stage",
     )(source)
-    lists = plan_lists(me, tables, list_slots, list_kinds)
+    lists = plan_lists(me, (*tables, far_table), list_slots, list_kinds)
     mine, lists, staged = lax.optimization_barrier((mine, lists, staged))
     own = mine.reshape((parent_boxes,) + pattern)
     after = shift(own, "y", -1)

time: 73 us -> 75.1 us (1.029)
  waiting for transfers between devices: 3.91 us -> 6.75 us
  starting transfers between devices: 34.2 us -> 32.8 us
    all_to_all x1, waiting for transfers between devices: 0.75 us -> 3.2 us  [local(): x = lax.all_to_all(x, SAMP, split_axis=0, concat_axis=0, tiled=True)]
    ppermute x11, waiting for transfers between devices: 1.14 us -> 3.55 us  [shift(): return lax.ppermute(x, axis, [(i, (i + step) % size) for i in range(size)])]
    all_to_all x1, starting transfers between devices: 5.94 us -> 3.81 us  [local(): mine = lax.all_to_all(whole, SAMP, split_axis=0, concat_axis=0, tiled=True)]
    all_to_all x1, waiting for transfers between devices: 2.02 us -> 0.01 us  [local(): mine = lax.all_to_all(whole, SAMP, split_axis=0, concat_axis=0, tiled=True)]
    all_to_all x1, starting transfers between devices: 4.7 us -> 6.58 us  [local(): lax.all_to_all(far_whole, SAMP, split_axis=0, concat_axis=0, tiled=True)]
    ppermute x11, starting transfers between devices: 15.1 us -> 14 us  [shift(): return lax.ppermute(x, axis, [(i, (i + step) % size) for i in range(size)])]
    unnamed x21 -> x19, local copies, waits for them, and re-layouts: 12.1 us -> 12.8 us
  transfers between devices with their start and end apart: 14 -> 14, of which waited for: 4 -> 3; matrix products, arithmetic and copies ran while one was open for 2% -> 3% of each run, Pallas kernels for 22% -> 21%
where the time goes in v6:
time: 75.1 us; the launch traced here: 74.4 us
  starting transfers between devices  32.8 us (44%)
  Pallas kernels  19.8 us (26%)
  local copies, waits for them, and re-layouts  12.8 us (17%)
  waiting for transfers between devices  6.75 us (9%)
  other arithmetic  1.48 us (2%)
  between operations  0.86 us (1%)
    ppermute x11, starting transfers between devices, shift(): return lax.ppermute(x, axis, [(i, (i + step) % size) for i in range(size)])  14 us
    unnamed x19, local copies, waits for them, and re-layouts  12.8 us
    pallas_call x5, Pallas kernels, translate(): pl.pallas_call(functools.partial(class_kernel, k), out_shape=out, in_spec...  12 us
    all_to_all x1, starting transfers between devices, local(): x = lax.all_to_all(x, SAMP, split_axis=0, concat_axis=0, tiled=True)  8.43 us
    all_to_all x1, starting transfers between devices, local(): lax.all_to_all(far_whole, SAMP, split_axis=0, concat_axis=0, tiled=True)  6.58 us
    all_to_all x1, starting transfers between devices, local(): mine = lax.all_to_all(whole, SAMP, split_axis=0, concat_axis=0, tiled=True)  3.81 us
    ppermute x11, waiting for transfers between devices, shift(): return lax.ppermute(x, axis, [(i, (i + step) % size) for i in range(size)])  3.55 us
    all_to_all x1, waiting for transfers between devices, local(): x = lax.all_to_all(x, SAMP, split_axis=0, concat_axis=0, tiled=True)  3.2 us
  transfers between devices with their start and end apart: 14, of which 3 were waited for; matrix products, arithmetic and copies ran while one was open for 3% of the time, Pallas kernels for 21%

profile of v6, /device:TPU:1, one launch (start us, length us, event | category | flops | bytes accessed | tf_op | source)
XLA Modules:
  0.0 74.4 jit_solution(4794112686450814067)
XLA Ops:
  0.6 8.4 %all-to-all-start = ((bf16[16,16,2,4,128]{4,3,2,1,0:T(4,128)(2,1)}), bf16[16,16,2,4,128]{4,3,2,1,0:T(4,128)(2,1)S(1)}, u32[]{:S(2)}, u32[]{:S(2)}) async-start(bf16[16,16,2,4,128]{4,3,2,1,0:T(4,128)(2,1)} %bitcast.9), calls=%async_computation | async-start | bytes 1048576 | tf_op jit(solution)/shard_map/all_to_all | solution.py:283
  9.1 1.0 %collective-permute-start = (s32[1,8,16]{2,1,0:T(8,128)}, s32[1,8,16]{2,1,0:T(8,128)S(1)}, u32[]{:S(2)}, u32[]{:S(2)}) collective-permute-start(s32[1,8,16]{2,1,0:T(8,128)} %param.11), channel_id=1, source_target_pairs={{0,16},{16,0},{1,17},{17,1},{2,18},{18,2},{3,19},{19,3},{4,20},{20... | collective-permute-start | bytes 1544 | tf_op jit(solution)/shard_map/ppermute | solution.py:189
  10.2 0.7 constant_dynamic-update-slice_fusion.1
  10.9 1.0 %multiply_sine_fusion = (f32[128,256]{1,0:T(8,128)S(1)}, f32[128,256]{1,0:T(8,128)S(1)}, f32[128,256]{1,0:T(8,128)S(1)}, f32[128,256]{1,0:T(8,128)S(1)}) fusion(f32[256]{0:T(256)S(1)} %get-tuple-element.84, f32[128]{0:T(128)S(1)} %sine_multiply_fusion, f32[256]{0:T(256)S(1)} %get-tuple-element.85), kind=kLoop, calls=%fused_computation.11 | loop fusion | flops 65536 | bytes 526848 | tf_op jit(solution)/shard_map/sin | solution.py:35
  11.9 0.1 sine_negate_fusion
  12.0 0.0 collective-permute-done
  12.0 1.4 %collective-permute-start.2 = (s32[2,8,16]{2,1,0:T(8,128)S(1)}, s32[2,8,16]{2,1,0:T(8,128)S(1)}, u32[]{:S(2)}, u32[]{:S(2)}) collective-permute-start(s32[2,8,16]{2,1,0:T(8,128)S(1)} %constant_dynamic-update-slice_fusion.own_ref), channel_id=1, source_target_pairs={{0,32},{32,64},{64,96},{96,0},{1,33},{33,65},{65,97},{97,1},{2,34}... | collective-permute-start | bytes 3080 | tf_op jit(solution)/shard_map/ppermute | solution.py:189
  13.4 1.5 %collective-permute-start.1 = (s32[2,8,16]{2,1,0:T(8,128)S(1)}, s32[2,8,16]{2,1,0:T(8,128)S(1)}, u32[]{:S(2)}, u32[]{:S(2)}) collective-permute-start(s32[2,8,16]{2,1,0:T(8,128)S(1)} %constant_dynamic-update-slice_fusion.own_ref), channel_id=1, source_target_pairs={{0,96},{32,0},{64,32},{96,64},{1,97},{33,1},{65,33},{97,65},{2,98}... | collective-permute-start | bytes 3080 | tf_op jit(solution)/shard_map/ppermute | solution.py:189
  14.9 0.3 fusion.5
  15.2 1.0 %prepare.1 = (bf16[128,64]{1,0:T(8,128)(2,1)S(1)}, bf16[128,256]{1,0:T(8,128)(2,1)S(1)}) custom-call(bf16[64,128]{1,0:T(8,128)(2,1)} %theta_hbm.1, bf16[128,256]{1,0:T(8,128)(2,1)} %phi_hbm.1), custom_call_target="tpu_custom_call" | custom-call | flops 1048576 | bytes 262144 | tf_op jit(solution)/shard_map/prepare/pallas_call | solution.py:286
  16.2 0.0 collective-permute-done.2.before_ref
  16.2 0.0 collective-permute-done.1.after_ref
  16.2 3.2 %all-to-all-done.x_ref = bf16[16,16,2,4,128]{4,3,2,1,0:T(4,128)(2,1)S(1)} async-done(((bf16[16,16,2,4,128]{4,3,2,1,0:T(4,128)(2,1)}), bf16[16,16,2,4,128]{4,3,2,1,0:T(4,128)(2,1)S(1)}, u32[]{:S(2)}, u32[]{:S(2)}) %all-to-all-start) | async-done | bytes 524320 | tf_op jit(solution)/shard_map/all_to_all | solution.py:283
  19.4 1.9 %aggregate.1 = bf16[16,2,2,8,256]{4,3,2,1,0:T(8,128)(2,1)} custom-call(bf16[16,16,2,4,128]{4,3,2,1,0:T(4,128)(2,1)S(1)} %all-to-all-done.x_ref, bf16[128,64]{1,0:T(8,128)(2,1)S(1)} %get-tuple-element.42.theta_ref, bf16[128,256]{1,0:T(8,128)(2,1)S(1)} %get-tuple-element.43.phi_ref, f32[4,128,256]{2,1,0:T(8,128)S(1)} %get-tuple-element.77.cos_ref, ...), custom_call_target="tpu_custom_call" | custom-call | flops 351272960 | bytes 4194304 | tf_op jit(solution)/shard_map/aggregate/pallas_call | solution.py:306
  21.3 3.8 %all-to-all-start.1 = ((bf16[16,2,2,8,256]{4,3,2,1,0:T(8,128)(2,1)}), bf16[16,2,2,8,256]{4,3,2,1,0:T(8,128)(2,1)S(1)}, u32[]{:S(2)}, u32[]{:S(2)}) async-start(bf16[16,2,2,8,256]{4,3,2,1,0:T(8,128)(2,1)} %aggregate.1), calls=%async_computation.1 | async-start | bytes 524288 | tf_op jit(solution)/shard_map/all_to_all | solution.py:320
  25.2 2.8 %collective-permute-start.4 = (bf16[16,2,2,8,256]{4,3,2,1,0:T(8,128)(2,1)}, bf16[16,2,2,8,256]{4,3,2,1,0:T(8,128)(2,1)S(1)}, u32[]{:S(2)}, u32[]{:S(2)}) collective-permute-start(bf16[16,2,2,8,256]{4,3,2,1,0:T(8,128)(2,1)} %aggregate.1), channel_id=1, source_target_pairs={{0,64},{32,96},{64,0},{96,32},{1,65},{33,97},{65,1},{97,33},{2,66}... | collective-permute-start | bytes 786440 | tf_op jit(solution)/shard_map/ppermute | solution.py:189
  28.0 0.2 collective-permute-start.3
  28.2 1.7 %stage.1.x_ref = bf16[316,2,8,256]{3,2,1,0:T(8,128)(2,1)S(1)} custom-call(bf16[316,2,8,256]{3,2,1,0:T(8,128)(2,1)} %x_ref), custom_call_target="tpu_custom_call" | custom-call | flops 1 | bytes 5242880 | tf_op jit(solution)/shard_map/stage/pallas_call | solution.py:323
  30.0 3.1 %collective-permute-done.3.far_ref = s32[2,8,16]{2,1,0:T(8,128)S(1)} collective-permute-done((s32[2,8,16]{2,1,0:T(8,128)S(1)}, s32[2,8,16]{2,1,0:T(8,128)S(1)}, u32[]{:S(2)}, u32[]{:S(2)}) %collective-permute-start.3) | collective-permute-done | bytes 1056 | tf_op jit(solution)/shard_map/ppermute | solution.py:189
  33.1 2.0 %plan.1.list_ref = s32[64,128]{1,0:T(8,128)S(4)} custom-call(s32[32,128]{1,0:T(8,128)S(1)} %broadcast_in_dim.2.me_ref, s32[2,8,16]{2,1,0:T(8,128)S(1)} %constant_dynamic-update-slice_fusion.own_ref, s32[2,8,16]{2,1,0:T(8,128)S(1)} %collective-permute-done.1.after_ref, s32[2,8,16]{2,1,0:T(8,128)S(1)} %collective-permute-done.2.before_ref, ...), custom_call_target="tpu_custom_call" | custom-call | flops 1048576 | bytes 1048576 | tf_op jit(solution)/shard_map/plan/pallas_call | solution.py:260
  35.1 0.0 all-to-all-done.1
  35.1 2.9 %collective-permute-start.5 = (bf16[32,2,8,256]{3,2,1,0:T(8,128)(2,1)S(1)}, bf16[32,2,8,256]{3,2,1,0:T(8,128)(2,1)S(1)}, u32[]{:S(2)}, u32[]{:S(2)}) collective-permute-start(bf16[32,2,8,256]{3,2,1,0:T(8,128)(2,1)S(1)} %bitcast.3), channel_id=1, source_target_pairs={{0,16},{16,0},{1,17},{17,1},{2,18},{18,2},{3,19},{19,3},{4,20},{20... | collective-permute-start | bytes 786440 | tf_op jit(solution)/shard_map/ppermute | solution.py:189
  38.0 1.2 %collective-permute-start.7 = (bf16[32,2,8,256]{3,2,1,0:T(8,128)(2,1)S(1)}, bf16[32,2,8,256]{3,2,1,0:T(8,128)(2,1)}, u32[]{:S(2)}, u32[]{:S(2)}) collective-permute-start(bf16[32,2,8,256]{3,2,1,0:T(8,128)(2,1)S(1)} %bitcast.4), channel_id=1, source_target_pairs={{0,32},{32,64},{64,96},{96,0},{1,33},{33,65},{65,97},{97,1},{2,34}... | collective-permute-start | bytes 786440 | tf_op jit(solution)/shard_map/ppermute | solution.py:189
  39.2 1.4 %collective-permute-start.6 = (bf16[32,2,8,256]{3,2,1,0:T(8,128)(2,1)S(1)}, bf16[32,2,8,256]{3,2,1,0:T(8,128)(2,1)}, u32[]{:S(2)}, u32[]{:S(2)}) collective-permute-start(bf16[32,2,8,256]{3,2,1,0:T(8,128)(2,1)S(1)} %bitcast.5), channel_id=1, source_target_pairs={{0,96},{32,0},{64,32},{96,64},{1,97},{33,1},{65,33},{97,65},{2,98}... | collective-permute-start | bytes 786440 | tf_op jit(solution)/shard_map/ppermute | solution.py:189
  40.7 0.0 collective-permute-done.4
  40.7 0.5 shard_map.86.trans_ref
  41.2 0.2 copy-done.8
  41.4 0.0 collective-permute-done.5.refs_1_
  41.4 1.3 %shard_map.87 = (f32[32,2,8,256]{3,2,1,0:T(8,128)S(1)}, f32[193,2,8,256]{3,2,1,0:T(8,128)S(1)}, bf16[32,2,8,256]{3,2,1,0:T(8,128)(2,1)}) custom-call(s32[64,128]{1,0:T(8,128)S(4)} %plan.1.list_ref, f32[316,2,8,256]{3,2,1,0:T(8,128)S(1)} %shard_map.86.trans_ref, bf16[32,2,8,256]{3,2,1,0:T(8,128)(2,1)S(1)} %bitcast.6, ...), custom_call_target="tpu_custom_call" | custom-call | flops 16777216 | bytes 8388608 | tf_op jit(solution)/shard_map/pallas_call | solution.py:380
  42.7 2.3 %copy-done = f32[316,2,8,256]{3,2,1,0:T(8,128)} copy-done((f32[316,2,8,256]{3,2,1,0:T(8,128)}, f32[316,2,8,256]{3,2,1,0:T(8,128)S(1)}, u32[]{:S(2)}) %copy-start) | copy-done | bytes 5177368
  45.0 1.7 %copy-done.2 = f32[193,2,8,256]{3,2,1,0:T(8,128)} copy-done((f32[193,2,8,256]{3,2,1,0:T(8,128)}, f32[193,2,8,256]{3,2,1,0:T(8,128)S(1)}, u32[]{:S(2)}) %copy-start.2) | copy-done | bytes 3162136
  46.7 0.4 collective-permute-done.7.refs_1_
  47.1 0.0 collective-permute-done.6.refs_2_
  47.1 1.0 %collective-permute-start.9 = (bf16[32,2,8,256]{3,2,1,0:T(8,128)(2,1)}, bf16[32,2,8,256]{3,2,1,0:T(8,128)(2,1)}, u32[]{:S(2)}, u32[]{:S(2)}) collective-permute-start(bf16[32,2,8,256]{3,2,1,0:T(8,128)(2,1)} %collective-permute-done.7.refs_1_), channel_id=1, source_target_pairs={{0,16},{16,0},{1,17},{17,1},{2,18},{18,2},{3,19},{19,3},{4,20},{20... | collective-permute-start | bytes 786440 | tf_op jit(solution)/shard_map/ppermute | solution.py:189
  48.1 0.0 collective-permute-start.8
  48.1 6.6 %all-to-all-start.2 = ((bf16[16,2,2,8,256]{4,3,2,1,0:T(8,128)(2,1)}), bf16[16,2,2,8,256]{4,3,2,1,0:T(8,128)(2,1)S(1)}, u32[]{:S(2)}, u32[]{:S(2)}) async-start(bf16[16,2,2,8,256]{4,3,2,1,0:T(8,128)(2,1)} %copy-done.8), calls=%async_computation.2 | async-start | bytes 524288 | tf_op jit(solution)/shard_map/all_to_all | solution.py:340
  54.7 2.5 %copy-done.1 = f32[316,2,8,256]{3,2,1,0:T(8,128)S(1)} copy-done((f32[316,2,8,256]{3,2,1,0:T(8,128)S(1)}, f32[316,2,8,256]{3,2,1,0:T(8,128)}, u32[]{:S(2)}) %copy-start.1) | copy-done | bytes 5177368
  57.1 1.9 %copy-done.3 = f32[193,2,8,256]{3,2,1,0:T(8,128)S(1)} copy-done((f32[193,2,8,256]{3,2,1,0:T(8,128)S(1)}, f32[193,2,8,256]{3,2,1,0:T(8,128)}, u32[]{:S(2)}) %copy-start.3) | copy-done | bytes 3162136
  59.0 2.4 %shard_map.88 = (f32[32,2,8,256]{3,2,1,0:T(8,128)S(1)}, f32[193,2,8,256]{3,2,1,0:T(8,128)S(1)}) custom-call(s32[64,128]{1,0:T(8,128)S(4)} %plan.1.list_ref, f32[316,2,8,256]{3,2,1,0:T(8,128)S(1)} %copy-done.1, f32[32,2,8,256]{3,2,1,0:T(8,128)S(1)} %get-tuple-element.63.refs_0_, ...), custom_call_target="tpu_custom_call", output_to_operand_aliasing={{1}: (5, {})} | custom-call | flops 16777216 | bytes 8388608 | tf_op jit(solution)/shard_map/pallas_call | solution.py:380
  61.4 1.6 %copy-done.4 = f32[193,2,8,256]{3,2,1,0:T(8,128)} copy-done((f32[193,2,8,256]{3,2,1,0:T(8,128)}, f32[193,2,8,256]{3,2,1,0:T(8,128)S(1)}, u32[]{:S(2)}) %copy-start.4) | copy-done | bytes 3162136
  63.0 0.0 collective-permute-done.9.refs_2_
  63.0 1.9 %copy-done.5 = f32[193,2,8,256]{3,2,1,0:T(8,128)S(1)} copy-done((f32[193,2,8,256]{3,2,1,0:T(8,128)S(1)}, f32[193,2,8,256]{3,2,1,0:T(8,128)}, u32[]{:S(2)}) %copy-start.5) | copy-done | bytes 3162136
  64.9 5.0 %shard_map.89 = (f32[32,2,8,256]{3,2,1,0:T(8,128)S(1)}, f32[193,2,8,256]{3,2,1,0:T(8,128)S(1)}) custom-call(s32[64,128]{1,0:T(8,128)S(4)} %plan.1.list_ref, f32[316,2,8,256]{3,2,1,0:T(8,128)S(1)} %copy-done.1, f32[32,2,8,256]{3,2,1,0:T(8,128)S(1)} %get-tuple-element.67.refs_0_, ...), custom_call_target="tpu_custom_call", output_to_operand_aliasing={{1}: (5, {})} | custom-call | flops 16777216 | bytes 8388608 | tf_op jit(solution)/shard_map/pallas_call | solution.py:380
  70.0 0.5 collective-permute-start.10
  70.5 0.5 shard_map.90.trans_ref
  71.0 1.4 %shard_map.91 = (f32[32,2,8,256]{3,2,1,0:T(8,128)S(1)}, f32[65,2,8,256]{3,2,1,0:T(8,128)S(1)}) custom-call(s32[64,128]{1,0:T(8,128)S(4)} %plan.1.list_ref, f32[316,2,8,256]{3,2,1,0:T(8,128)S(1)} %shard_map.90.trans_ref, f32[32,2,8,256]{3,2,1,0:T(8,128)S(1)} %get-tuple-element.71.refs_0_, bf16[32,2,8,256]{3,2,1,0:T(8,128)(2,1)S(1)} %bitcast.8), custom_call_target="tpu_custom_call" | custom-call | flops 16777216 | bytes 8388608 | tf_op jit(solution)/shard_map/pallas_call | solution.py:380
  72.4 0.0 collective-permute-done.10.refs_1_
  72.4 2.0 %shard_map.92 = (f32[32,2,8,256]{3,2,1,0:T(8,128)}, f32[65,2,8,256]{3,2,1,0:T(8,128)S(1)}) custom-call(s32[64,128]{1,0:T(8,128)S(4)} %plan.1.list_ref, f32[316,2,8,256]{3,2,1,0:T(8,128)S(1)} %shard_map.90.trans_ref, f32[32,2,8,256]{3,2,1,0:T(8,128)S(1)} %get-tuple-element.73.refs_0_, ...), custom_call_target="tpu_custom_call", output_to_operand_aliasing={{1}: (4, {})} | custom-call | flops 16777216 | bytes 8388608 | tf_op jit(solution)/shard_map/pallas_call | solution.py:380
  (19 shorter events, 0.1 us)
Async XLA Ops:
  0.6 18.8 %all-to-all-start = ((bf16[16,16,2,4,128]{4,3,2,1,0:T(4,128)(2,1)}), bf16[16,16,2,4,128]{4,3,2,1,0:T(4,128)(2,1)S(1)}, u32[]{:S(2)}, u32[]{:S(2)}) async-start(bf16[16,16,2,4,128]{4,3,2,1,0:T(4,128)(2,1)} %bitcast.9), calls=%async_computation | async-start | bytes 1048576 | tf_op jit(solution)/shard_map/all_to_all | solution.py:283
  9.1 2.9 %collective-permute-start = (s32[1,8,16]{2,1,0:T(8,128)}, s32[1,8,16]{2,1,0:T(8,128)S(1)}, u32[]{:S(2)}, u32[]{:S(2)}) collective-permute-start(s32[1,8,16]{2,1,0:T(8,128)} %param.11), channel_id=1, source_target_pairs={{0,16},{16,0},{1,17},{17,1},{2,18},{18,2},{3,19},{19,3},{4,20},{20... | collective-permute-start | bytes 1544 | tf_op jit(solution)/shard_map/ppermute | solution.py:189
  12.0 4.2 %collective-permute-start.2 = (s32[2,8,16]{2,1,0:T(8,128)S(1)}, s32[2,8,16]{2,1,0:T(8,128)S(1)}, u32[]{:S(2)}, u32[]{:S(2)}) collective-permute-start(s32[2,8,16]{2,1,0:T(8,128)S(1)} %constant_dynamic-update-slice_fusion.own_ref), channel_id=1, source_target_pairs={{0,32},{32,64},{64,96},{96,0},{1,33},{33,65},{65,97},{97,1},{2,34}... | collective-permute-start | bytes 3080 | tf_op jit(solution)/shard_map/ppermute | solution.py:189
  13.4 2.8 %collective-permute-start.1 = (s32[2,8,16]{2,1,0:T(8,128)S(1)}, s32[2,8,16]{2,1,0:T(8,128)S(1)}, u32[]{:S(2)}, u32[]{:S(2)}) collective-permute-start(s32[2,8,16]{2,1,0:T(8,128)S(1)} %constant_dynamic-update-slice_fusion.own_ref), channel_id=1, source_target_pairs={{0,96},{32,0},{64,32},{96,64},{1,97},{33,1},{65,33},{97,65},{2,98}... | collective-permute-start | bytes 3080 | tf_op jit(solution)/shard_map/ppermute | solution.py:189
  21.3 11.7 %copy-start.6 = (s32[32,64]{1,0:T(8,128)S(1)}, s32[32,64]{1,0:T(8,128)}, u32[]{:S(2)}) copy-start(s32[32,64]{1,0:T(8,128)} %slots_ref.1) | copy-start | bytes 24580
  21.3 11.7 %copy-start.7 = (s32[32,64]{1,0:T(8,128)S(1)}, s32[32,64]{1,0:T(8,128)}, u32[]{:S(2)}) copy-start(s32[32,64]{1,0:T(8,128)} %kinds_ref.1) | copy-start | bytes 24580
  21.3 13.8 %all-to-all-start.1 = ((bf16[16,2,2,8,256]{4,3,2,1,0:T(8,128)(2,1)}), bf16[16,2,2,8,256]{4,3,2,1,0:T(8,128)(2,1)S(1)}, u32[]{:S(2)}, u32[]{:S(2)}) async-start(bf16[16,2,2,8,256]{4,3,2,1,0:T(8,128)(2,1)} %aggregate.1), calls=%async_computation.1 | async-start | bytes 524288 | tf_op jit(solution)/shard_map/all_to_all | solution.py:320
  25.2 15.5 %collective-permute-start.4 = (bf16[16,2,2,8,256]{4,3,2,1,0:T(8,128)(2,1)}, bf16[16,2,2,8,256]{4,3,2,1,0:T(8,128)(2,1)S(1)}, u32[]{:S(2)}, u32[]{:S(2)}) collective-permute-start(bf16[16,2,2,8,256]{4,3,2,1,0:T(8,128)(2,1)} %aggregate.1), channel_id=1, source_target_pairs={{0,64},{32,96},{64,0},{96,32},{1,65},{33,97},{65,1},{97,33},{2,66}... | collective-permute-start | bytes 786440 | tf_op jit(solution)/shard_map/ppermute | solution.py:189
  28.0 5.0 %collective-permute-start.3 = (s32[2,8,16]{2,1,0:T(8,128)S(1)}, s32[2,8,16]{2,1,0:T(8,128)S(1)}, u32[]{:S(2)}, u32[]{:S(2)}) collective-permute-start(s32[2,8,16]{2,1,0:T(8,128)S(1)} %constant_dynamic-update-slice_fusion.own_ref), channel_id=1, source_target_pairs={{0,64},{32,96},{64,0},{96,32},{1,65},{33,97},{65,1},{97,33},{2,66}... | collective-permute-start | bytes 3080 | tf_op jit(solution)/shard_map/ppermute | solution.py:189
  35.1 6.3 %collective-permute-start.5 = (bf16[32,2,8,256]{3,2,1,0:T(8,128)(2,1)S(1)}, bf16[32,2,8,256]{3,2,1,0:T(8,128)(2,1)S(1)}, u32[]{:S(2)}, u32[]{:S(2)}) collective-permute-start(bf16[32,2,8,256]{3,2,1,0:T(8,128)(2,1)S(1)} %bitcast.3), channel_id=1, source_target_pairs={{0,16},{16,0},{1,17},{17,1},{2,18},{18,2},{3,19},{19,3},{4,20},{20... | collective-permute-start | bytes 786440 | tf_op jit(solution)/shard_map/ppermute | solution.py:189
  38.0 9.1 %collective-permute-start.7 = (bf16[32,2,8,256]{3,2,1,0:T(8,128)(2,1)S(1)}, bf16[32,2,8,256]{3,2,1,0:T(8,128)(2,1)}, u32[]{:S(2)}, u32[]{:S(2)}) collective-permute-start(bf16[32,2,8,256]{3,2,1,0:T(8,128)(2,1)S(1)} %bitcast.4), channel_id=1, source_target_pairs={{0,32},{32,64},{64,96},{96,0},{1,33},{33,65},{65,97},{97,1},{2,34}... | collective-permute-start | bytes 786440 | tf_op jit(solution)/shard_map/ppermute | solution.py:189
  39.2 7.9 %collective-permute-start.6 = (bf16[32,2,8,256]{3,2,1,0:T(8,128)(2,1)S(1)}, bf16[32,2,8,256]{3,2,1,0:T(8,128)(2,1)}, u32[]{:S(2)}, u32[]{:S(2)}) collective-permute-start(bf16[32,2,8,256]{3,2,1,0:T(8,128)(2,1)S(1)} %bitcast.5), channel_id=1, source_target_pairs={{0,96},{32,0},{64,32},{96,64},{1,97},{33,1},{65,33},{97,65},{2,98}... | collective-permute-start | bytes 786440 | tf_op jit(solution)/shard_map/ppermute | solution.py:189
  40.7 0.7 copy-start.8
  42.6 2.3 %copy-start = (f32[316,2,8,256]{3,2,1,0:T(8,128)}, f32[316,2,8,256]{3,2,1,0:T(8,128)S(1)}, u32[]{:S(2)}) copy-start(f32[316,2,8,256]{3,2,1,0:T(8,128)S(1)} %shard_map.86.trans_ref) | copy-start | bytes 15532036
  45.0 1.7 %copy-start.2 = (f32[193,2,8,256]{3,2,1,0:T(8,128)}, f32[193,2,8,256]{3,2,1,0:T(8,128)S(1)}, u32[]{:S(2)}) copy-start(f32[193,2,8,256]{3,2,1,0:T(8,128)S(1)} %get-tuple-element.66.refs_3_) | copy-start | bytes 9486340
  47.1 15.9 %collective-permute-start.9 = (bf16[32,2,8,256]{3,2,1,0:T(8,128)(2,1)}, bf16[32,2,8,256]{3,2,1,0:T(8,128)(2,1)}, u32[]{:S(2)}, u32[]{:S(2)}) collective-permute-start(bf16[32,2,8,256]{3,2,1,0:T(8,128)(2,1)} %collective-permute-done.7.refs_1_), channel_id=1, source_target_pairs={{0,16},{16,0},{1,17},{17,1},{2,18},{18,2},{3,19},{19,3},{4,20},{20... | collective-permute-start | bytes 786440 | tf_op jit(solution)/shard_map/ppermute | solution.py:189
  48.1 15.0 %collective-permute-start.8 = (bf16[32,2,8,256]{3,2,1,0:T(8,128)(2,1)}, bf16[32,2,8,256]{3,2,1,0:T(8,128)(2,1)}, u32[]{:S(2)}, u32[]{:S(2)}) collective-permute-start(bf16[32,2,8,256]{3,2,1,0:T(8,128)(2,1)} %collective-permute-done.6.refs_2_), channel_id=1, source_target_pairs={{0,16},{16,0},{1,17},{17,1},{2,18},{18,2},{3,19},{19,3},{4,20},{20... | collective-permute-start | bytes 786440 | tf_op jit(solution)/shard_map/ppermute | solution.py:189
  48.1 21.9 %all-to-all-start.2 = ((bf16[16,2,2,8,256]{4,3,2,1,0:T(8,128)(2,1)}), bf16[16,2,2,8,256]{4,3,2,1,0:T(8,128)(2,1)S(1)}, u32[]{:S(2)}, u32[]{:S(2)}) async-start(bf16[16,2,2,8,256]{4,3,2,1,0:T(8,128)(2,1)} %copy-done.8), calls=%async_computation.2 | async-start | bytes 524288 | tf_op jit(solution)/shard_map/all_to_all | solution.py:340
  54.6 2.5 %copy-start.1 = (f32[316,2,8,256]{3,2,1,0:T(8,128)S(1)}, f32[316,2,8,256]{3,2,1,0:T(8,128)}, u32[]{:S(2)}) copy-start(f32[316,2,8,256]{3,2,1,0:T(8,128)} %copy-done) | copy-start | bytes 15532036
  57.1 1.9 %copy-start.3 = (f32[193,2,8,256]{3,2,1,0:T(8,128)S(1)}, f32[193,2,8,256]{3,2,1,0:T(8,128)}, u32[]{:S(2)}) copy-start(f32[193,2,8,256]{3,2,1,0:T(8,128)} %copy-done.2) | copy-start | bytes 9486340
  61.4 1.6 %copy-start.4 = (f32[193,2,8,256]{3,2,1,0:T(8,128)}, f32[193,2,8,256]{3,2,1,0:T(8,128)S(1)}, u32[]{:S(2)}) copy-start(f32[193,2,8,256]{3,2,1,0:T(8,128)S(1)} %get-tuple-element.68.refs_3_) | copy-start | bytes 9486340
  63.0 1.9 %copy-start.5 = (f32[193,2,8,256]{3,2,1,0:T(8,128)S(1)}, f32[193,2,8,256]{3,2,1,0:T(8,128)}, u32[]{:S(2)}) copy-start(f32[193,2,8,256]{3,2,1,0:T(8,128)} %copy-done.4) | copy-start | bytes 9486340
  70.0 2.4 %collective-permute-start.10 = (bf16[32,2,8,256]{3,2,1,0:T(8,128)(2,1)S(1)}, bf16[32,2,8,256]{3,2,1,0:T(8,128)(2,1)S(1)}, u32[]{:S(2)}, u32[]{:S(2)}) collective-permute-start(bf16[32,2,8,256]{3,2,1,0:T(8,128)(2,1)S(1)} %bitcast.7), channel_id=1, source_target_pairs={{0,16},{16,0},{1,17},{17,1},{2,18},{18,2},{3,19},{19,3},{4,20},{20... | collective-permute-start | bytes 786440 | tf_op jit(solution)/shard_map/ppermute | solution.py:189
